TPU v7x, 32 devices: a whole 2x2x4 slice. The times are simulated.
32 devices in a mesh: row: 8 (over z, x), col: 4 (over y, core).
Axes of the slice: x: 2, y: 2, z: 4, core: 2. Of those that a mesh axis runs over, the one named last changes fastest.
Arguments:
- panel: float32 [128, 131072], P('col', 'row'), may hold values from -6 to 6
- signs: int32 [131072], P('row'), may hold values from -1 to 1, as said below
- offsets: int32 [8192], P('row'), may hold values from 0 to 16383
- owners: int32 [8192, 1], P('row'), may hold values from 0 to 7; in each aligned block of 1024 rows (0 to 1023, 1024 to 2047, ...) at most 256 rows name the same one
Outputs:
- grams: float32 [8, 128, 128], P('row', 'col')
Inputs may be any that keep to these rules, and one draw needn't show every extreme that they name: `signs`: each entry is +1 or -1. `owners`: in each aligned block of 1024 samples (the list of one source), no owner is named more than 256 times, a bound that some block reaches; every owner is named somewhere.
All inputs are finite; a program needn't handle non-finite values.
Results may differ from a plain program's by a relative error of at most 0.0003.
Values sent between devices are 32-bit elements; how exact they have to be, the bound alone decides.
No kernel may reach another device: no remote copies, remote signals or barrier semaphores. Data moves between devices by JAX's collectives and lax.ppermute only.
A program may use at most 128 MiB of HBM per device.

v0:
```python
import functools

import jax
import jax.numpy as jnp
from jax import lax
from jax.experimental import pallas as pl
from jax.experimental.pallas import tpu as pltpu
from jax.sharding import PartitionSpec as P


LANES = 128
f32, bf16 = jnp.float32, jnp.bfloat16


def swapped(x, axis, distance):
    return lax.ppermute(x, axis, [(i, i ^ distance) for i in range(lax.axis_size(axis))])


def parity(v):
    v = v ^ (v >> 8)
    v = v ^ (v >> 4)
    v = v ^ (v >> 2)
    v = v ^ (v >> 1)
    return v & 1


def butterflies(values):
    step = 1
    while step < len(values):
        out = list(values)
        for i in range(len(values)):
            if not i & step:
                out[i] = values[i] + values[i | step]
                out[i | step] = values[i] - values[i | step]
        values = out
        step *= 2
    return values


def halves(x):
    top = x.astype(bf16)
    return top, (x - top.astype(f32)).astype(bf16)


def rows_kernel(width, x_ref, sign_ref, work_ref):
    def some(lo, _):
        signs = [sign_ref[pl.ds(hi * 8 + lo, 1), :].astype(f32) for hi in range(16)]
        for band in range(width // 8):
            rows = pl.ds(band * 8, 8)
            values = []
            for hi in range(16):
                start = pl.multiple_of((hi * 8 + lo) * LANES, LANES)
                values.append(x_ref[rows, pl.ds(start, LANES)] * signs[hi])
            for hi, value in enumerate(butterflies(values)):
                work_ref[hi * 8 + lo, rows, :] = value
        return 0

    lax.fori_loop(0, 8, some, 0)


def table_kernel(width, work_ref, table_ref):
    group = LANES // width
    bands = width // 8
    pair = 2 if width * 8 >= 2 * width else 1
    row = lax.broadcasted_iota(jnp.int32, (LANES, 2 * LANES), 0)
    column = lax.broadcasted_iota(jnp.int32, (LANES, 2 * LANES), 1)
    hadamard = (1 - 2 * parity(row & (column & (LANES - 1)))).astype(f32).astype(bf16)

    def some(hi, _):
        rows = [
            butterflies([work_ref[hi * 8 + lo, pl.ds(band * 8, 8), :] for lo in range(8)]) for band in range(bands)
        ]
        y = jnp.concatenate([rows[band][lo] for lo in range(8) for band in range(bands)], axis=0)
        top, low = halves(y)
        for e in range(0, 8, pair):
            both = [
                jnp.concatenate([v[(e + i) * width : (e + i + 1) * width] for i in range(pair) for _ in range(group)])
                for v in (top, low)
            ]
            mixed = lax.dot_general(
                hadamard,
                jnp.concatenate(both, axis=1),
                (((1,), (1,)), ((), ())),
                preferred_element_type=f32,
            )
            for i in range(pair):
                start = pl.multiple_of((hi * 8 + e + i) * LANES, LANES)
                table_ref[pl.ds(start, LANES), :] = mixed[:, i * LANES : (i + 1) * LANES]
        return 0

    lax.fori_loop(0, 16, some, 0, unroll=4)


def pick_kernel(width, slots, count, straight, *refs):
    offset_refs, table_ref, out_ref = refs[:-2], refs[-2], refs[-1]
    group = LANES // width
    per = count // group
    lane = lax.broadcasted_iota(jnp.int32, (8, LANES), 1) // width
    sub = lax.broadcasted_iota(jnp.int32, (8, LANES), 0)
    in_sub = [sub == s for s in range(8)]
    in_lane = [lane == g for g in range(group)]
    me = lax.axis_index("row")
    for place, slot in enumerate(slots):
        sign = (1 - 2 * parity(me & (me ^ slot))).astype(f32)

        def block(inner):
            total = None
            for g in range(group):
                part = None
                for s in range(8):
                    spot = offset_refs[place][inner + (g * per + s)]
                    value = jnp.broadcast_to(table_ref[pl.ds(spot, 1), :], (8, LANES))
                    part = value if part is None else jnp.where(in_sub[s], value, part)
                total = part if total is None else jnp.where(in_lane[g], part, total)
            return total * sign

        if straight:
            for inner in range(0, per, 8):
                out_ref[pl.ds(place * per + inner, 8), :] = block(inner)
        else:

            def some(it, _):
                inner = pl.multiple_of(it * 8, 8)
                out_ref[pl.ds(place * per + inner, 8), :] = block(inner)
                return 0

            lax.fori_loop(0, per // 8, some, 0)


def gram_kernel(width, count, named, scale, owner_ref, *refs):
    group = LANES // width
    per = count // group
    packed, out_ref = refs[:-1], refs[-1]
    lane = lax.broadcasted_iota(jnp.int32, (per, LANES), 1)
    parts, repeated = [], []
    for g in range(group):
        total = packed[g][...]
        for u in range(group):
            if u != g:
                moved = jnp.take_along_axis(packed[u][...], lane ^ ((u ^ g) * width), axis=1)
                total = jnp.where(lane // width == u, moved, total)
        parts.append(total)
        repeated.append(jnp.take_along_axis(packed[0][...], (lane & (width - 1)) + g * width, axis=1))
    sketch = jnp.concatenate(parts, axis=0)
    mine = jnp.concatenate(repeated, axis=0)
    top, low = halves(sketch)
    mine_top, mine_low = halves(mine)
    whose = jnp.broadcast_to(owner_ref[...], (count, LANES))
    tall = lax.broadcasted_iota(jnp.int32, (count, LANES), 1) // width
    zero = jnp.zeros((count, LANES), bf16)
    me, col = lax.axis_index("row"), lax.axis_index("col")
    turned = lax.broadcasted_iota(jnp.int32, (LANES, LANES), 1) ^ (col * width)
    over = (((0,), (0,)), ((), ()))
    for block in range(named * width // LANES):
        match = whose == tall + block * group
        left = jnp.where(match, mine_top, zero)
        gram = lax.dot_general(left, top, over, preferred_element_type=f32)
        gram = gram + lax.dot_general(left, low, over, preferred_element_type=f32)
        left = jnp.where(match, mine_low, zero)
        gram = gram + lax.dot_general(left, top, over, preferred_element_type=f32)
        gram = jnp.take_along_axis(gram, turned, axis=1) * scale
        for k in range(group):
            slot = (block * group + k) ^ me
            place = (slot & 3) * (named // 4) + (slot >> 2)
            out_ref[pl.ds(pl.multiple_of(place * width, 8), width), :] = gram[k * width : (k + 1) * width]


VMEM = pl.BlockSpec(memory_space=pltpu.VMEM)
SMEM = pl.BlockSpec(memory_space=pltpu.SMEM)
PARAMS = pltpu.CompilerParams(vmem_limit_bytes=24 << 20)


def transform_rows(panel, signs):
    width, _ = panel.shape
    return pl.pallas_call(
        functools.partial(rows_kernel, width),
        out_shape=jax.ShapeDtypeStruct((LANES, width, LANES), f32),
        in_specs=[VMEM] * 2,
        out_specs=VMEM,
        compiler_params=PARAMS,
        name="rows",
    )(panel, signs.reshape(LANES, LANES))


def transform_table(work, width):
    return pl.pallas_call(
        functools.partial(table_kernel, width),
        out_shape=jax.ShapeDtypeStruct((LANES * LANES, LANES), f32),
        in_specs=[VMEM],
        out_specs=VMEM,
        compiler_params=PARAMS,
        name="table",
    )(work)


def reverse(i, bits):
    return int(format(i, f"0{bits}b")[::-1], 2) if bits else 0


def spread(pieces, level):
    distance = 1 << level
    if len(pieces) <= 4:
        arrived = []
        for piece in pieces:
            arrived.append(swapped(piece, "row", distance))
        return pieces + arrived
    arrived = swapped(jnp.stack(pieces), "row", distance)
    return pieces + [arrived[i] for i in range(len(pieces))]


def body(panel, signs, offsets, owners):
    width, row_count = panel.shape
    devices = lax.axis_size("row")
    bits = devices.bit_length() - 1
    count = offsets.shape[0]
    group = LANES // width
    per = count // group
    near = min(bits, 2)
    listed = [offsets]
    for t in range(1, 1 << near):
        listed.append(swapped(offsets, "row", t))
    work = transform_rows(panel, signs)
    for level in range(near, bits):
        listed = spread(listed, level)
    table = transform_table(work, width)

    def pick(slots):
        return pl.pallas_call(
            functools.partial(pick_kernel, width, slots, count, len(slots) <= 4),
            out_shape=jax.ShapeDtypeStruct((len(slots) * per, LANES), f32),
            in_specs=[SMEM] * len(slots) + [VMEM],
            out_specs=VMEM,
            compiler_params=PARAMS,
            name="pick",
        )(*[listed[t] for t in slots], table)

    chunks = []
    for upper in range(2):
        odd = list(range(1 + upper * devices // 2, (1 + upper) * devices // 2, 2))
        odd.sort(key=lambda t: reverse(t, bits))
        chunks.append((odd, swapped(pick(odd), "row", 1)))
    kept = [pick([t - 1 for t in odd]) for odd, _ in chunks]
    totals = []
    for mine, (_, arrived) in zip(kept, chunks):
        total = mine + arrived
        for level in range(1, bits - 1):
            middle = total.shape[0] // 2
            total = total[:middle] + swapped(total[middle:], "row", 1 << level)
        totals.append(total)
    total = totals[0] + swapped(totals[1], "row", devices // 2)
    col_bits = lax.axis_size("col").bit_length() - 1
    stacked = total[None]
    for level in reversed(range(col_bits)):
        stacked = jnp.concatenate([stacked, swapped(stacked, "col", 1 << level)], axis=0)
    packed = [stacked[reverse(u, col_bits)] for u in range(group)]
    scale = 1.0 / (devices * row_count * count)
    gram = pl.pallas_call(
        functools.partial(gram_kernel, width, count, devices, scale),
        out_shape=jax.ShapeDtypeStruct((devices * width, LANES), f32),
        in_specs=[VMEM] * (1 + group),
        out_specs=VMEM,
        compiler_params=PARAMS,
        name="gram",
    )(owners, *packed)
    gram = gram.reshape(1 << near, devices >> near, width, LANES)
    total = gram[0]
    for t in range(1, 1 << near):
        total = total + swapped(gram[t], "row", t)
    for level in reversed(range(near, bits)):
        middle = total.shape[0] // 2
        total = total[:middle] + swapped(total[middle:], "row", 1 << level)
    return total


def solution(mesh):
    placed = (P("col", "row"), P("row"), P("row"), P("row", None))
    return jax.shard_map(
        body, mesh=mesh, in_specs=placed, out_specs=P("row", "col", None), check_vma=False
    )
```

profile of v0, /device:TPU:0, one launch (start us, length us, event | category | flops | bytes accessed | tf_op | source)
XLA Modules:
  0.0 65.1 jit_solution(1478778677595305427)
XLA Ops:
  0.0 3.0 %collective-permute-start.1 = (s32[1024]{0:T(1024)}, s32[1024]{0:T(1024)S(1)}, u32[]{:S(2)}, u32[]{:S(2)}) collective-permute-start(s32[1024]{0:T(1024)} %refs_0_.1), channel_id=1, source_target_pairs={{0,4},{4,0},{8,12},{12,8},{16,20},{20,16},{24,28},{28,24},{1,5},{5... | collective-permute-start | bytes 12296 | tf_op jit(solution)/shard_map/ppermute | solution.py:16
  3.0 1.5 %collective-permute-start.2 = (s32[1024]{0:T(1024)}, s32[1024]{0:T(1024)S(1)}, u32[]{:S(2)}, u32[]{:S(2)}) collective-permute-start(s32[1024]{0:T(1024)} %refs_0_.1), channel_id=1, source_target_pairs={{0,12},{4,8},{8,4},{12,0},{16,28},{20,24},{24,20},{28,16},{1,13},{... | collective-permute-start | bytes 12296 | tf_op jit(solution)/shard_map/ppermute | solution.py:16
  4.8 3.1 %collective-permute-start.7 = (s32[1024]{0:T(1024)S(1)}, s32[1024]{0:T(1024)S(1)}, u32[]{:S(2)}, u32[]{:S(2)}) collective-permute-start(s32[1024]{0:T(1024)S(1)} %collective-permute-done.1.refs_0_), channel_id=1, source_target_pairs={{0,16},{4,20},{8,24},{12,28},{16,0},{20,4},{24,8},{28,12},{1,17},{... | collective-permute-start | bytes 12296 | tf_op jit(solution)/shard_map/ppermute | solution.py:16
  7.9 2.4 %collective-permute-start.8 = (s32[1024]{0:T(1024)S(1)}, s32[1024]{0:T(1024)S(1)}, u32[]{:S(2)}, u32[]{:S(2)}) collective-permute-start(s32[1024]{0:T(1024)S(1)} %collective-permute-done.2.refs_1_), channel_id=1, source_target_pairs={{0,16},{4,20},{8,24},{12,28},{16,0},{20,4},{24,8},{28,12},{1,17},{... | collective-permute-start | bytes 12296 | tf_op jit(solution)/shard_map/ppermute | solution.py:16
  10.3 1.6 %copy-done = f32[32,16384]{1,0:T(8,128)S(1)} copy-done((f32[32,16384]{1,0:T(8,128)S(1)}, f32[32,16384]{1,0:T(8,128)}, u32[]{:S(2)}) %copy-start) | copy-done | bytes 2097176
  13.3 3.4 %table.1.refs_2_ = f32[16384,128]{1,0:T(8,128)S(1)} custom-call(f32[128,32,128]{2,1,0:T(8,128)S(1)} %rows.1.work_ref), custom_call_target="tpu_custom_call" | custom-call | tf_op jit(solution)/shard_map/table/pallas_call | solution.py:186
  16.7 1.8 %pick.7 = f32[512,128]{1,0:T(8,128)S(1)} custom-call(s32[1024]{0:T(1024)S(1)} %collective-permute-done.7.refs_0_, s32[1024]{0:T(1024)S(1)} %collective-permute-done.8.refs_1_, f32[16384,128]{1,0:T(8,128)S(1)} %table.1.refs_2_), custom_call_target="tpu_custom_call" | custom-call | tf_op jit(solution)/shard_map/pick/pallas_call | solution.py:228
  19.1 1.8 %pick.5 = f32[512,128]{1,0:T(8,128)S(1)} custom-call(s32[1024]{0:T(1024)S(1)} %collective-permute-done.1.refs_0_, s32[1024]{0:T(1024)S(1)} %collective-permute-done.2.refs_1_, f32[16384,128]{1,0:T(8,128)S(1)} %table.1.refs_2_), custom_call_target="tpu_custom_call" | custom-call | tf_op jit(solution)/shard_map/pick/pallas_call | solution.py:228
  20.9 1.6 %collective-permute-start.3 = (f32[512,128]{1,0:T(8,128)S(1)}, f32[512,128]{1,0:T(8,128)S(1)}, u32[]{:S(2)}, u32[]{:S(2)}) collective-permute-start(f32[512,128]{1,0:T(8,128)S(1)} %pick.5), channel_id=1, source_target_pairs={{0,4},{4,0},{8,12},{12,8},{16,20},{20,16},{24,28},{28,24},{1,5},{5... | collective-permute-start | bytes 786440 | tf_op jit(solution)/shard_map/ppermute | solution.py:16
  22.5 1.6 %collective-permute-start = (s32[1024]{0:T(1024)S(1)}, s32[1024]{0:T(1024)S(1)}, u32[]{:S(2)}, u32[]{:S(2)}) collective-permute-start(s32[1024]{0:T(1024)S(1)} %copy-done.2), channel_id=1, source_target_pairs={{0,8},{4,12},{8,0},{12,4},{16,24},{20,28},{24,16},{28,20},{1,9},{5... | collective-permute-start | bytes 12296 | tf_op jit(solution)/shard_map/ppermute | solution.py:16
  24.6 1.5 %collective-permute-done.refs_1_ = s32[1024]{0:T(1024)S(1)} collective-permute-done((s32[1024]{0:T(1024)S(1)}, s32[1024]{0:T(1024)S(1)}, u32[]{:S(2)}, u32[]{:S(2)}) %collective-permute-start) | collective-permute-done | bytes 4128 | tf_op jit(solution)/shard_map/ppermute | solution.py:16
  27.0 1.6 %collective-permute-done.5.refs_0_ = s32[1024]{0:T(1024)S(1)} collective-permute-done((s32[1024]{0:T(1024)S(1)}, s32[1024]{0:T(1024)S(1)}, u32[]{:S(2)}, u32[]{:S(2)}) %collective-permute-start.5) | collective-permute-done | bytes 4128 | tf_op jit(solution)/shard_map/ppermute | solution.py:16
  28.6 2.0 %collective-permute-done.6.refs_1_ = s32[1024]{0:T(1024)S(1)} collective-permute-done((s32[1024]{0:T(1024)S(1)}, s32[1024]{0:T(1024)S(1)}, u32[]{:S(2)}, u32[]{:S(2)}) %collective-permute-start.6) | collective-permute-done | bytes 4128 | tf_op jit(solution)/shard_map/ppermute | solution.py:16
  30.6 1.8 %pick.6 = f32[512,128]{1,0:T(8,128)S(1)} custom-call(s32[1024]{0:T(1024)S(1)} %collective-permute-done.5.refs_0_, s32[1024]{0:T(1024)S(1)} %collective-permute-done.6.refs_1_, f32[16384,128]{1,0:T(8,128)S(1)} %table.1.refs_2_), custom_call_target="tpu_custom_call" | custom-call | tf_op jit(solution)/shard_map/pick/pallas_call | solution.py:228
  32.5 1.7 %collective-permute-start.10 = (f32[256,128]{1,0:T(8,128)S(1)}, f32[256,128]{1,0:T(8,128)S(1)}, u32[]{:S(2)}, u32[]{:S(2)}) collective-permute-start(f32[256,128]{1,0:T(8,128)S(1)} %slice.55), channel_id=1, source_target_pairs={{0,8},{4,12},{8,0},{12,4},{16,24},{20,28},{24,16},{28,20},{1,9},{5... | collective-permute-start | bytes 393224 | tf_op jit(solution)/shard_map/ppermute | solution.py:16
  34.2 1.8 %pick.4 = f32[512,128]{1,0:T(8,128)S(1)} custom-call(s32[1024]{0:T(1024)S(1)} %copy-done.2, s32[1024]{0:T(1024)S(1)} %collective-permute-done.refs_1_, f32[16384,128]{1,0:T(8,128)S(1)} %table.1.refs_2_), custom_call_target="tpu_custom_call" | custom-call | tf_op jit(solution)/shard_map/pick/pallas_call | solution.py:228
  36.6 1.8 %collective-permute-done.10 = f32[256,128]{1,0:T(8,128)S(1)} collective-permute-done((f32[256,128]{1,0:T(8,128)S(1)}, f32[256,128]{1,0:T(8,128)S(1)}, u32[]{:S(2)}, u32[]{:S(2)}) %collective-permute-start.10) | collective-permute-done | bytes 131104 | tf_op jit(solution)/shard_map/ppermute | solution.py:16
  38.4 1.5 %collective-permute-start.11 = (f32[256,128]{1,0:T(8,128)S(1)}, f32[256,128]{1,0:T(8,128)S(1)}, u32[]{:S(2)}, u32[]{:S(2)}) collective-permute-start(f32[256,128]{1,0:T(8,128)S(1)} %slice_add_fusion), channel_id=1, source_target_pairs={{0,16},{4,20},{8,24},{12,28},{16,0},{20,4},{24,8},{28,12},{1,17},{... | collective-permute-start | bytes 393224 | tf_op jit(solution)/shard_map/ppermute | solution.py:16
  41.1 4.6 %collective-permute-done.11 = f32[256,128]{1,0:T(8,128)S(1)} collective-permute-done((f32[256,128]{1,0:T(8,128)S(1)}, f32[256,128]{1,0:T(8,128)S(1)}, u32[]{:S(2)}, u32[]{:S(2)}) %collective-permute-start.11) | collective-permute-done | bytes 131104 | tf_op jit(solution)/shard_map/ppermute | solution.py:16
  45.7 1.6 %collective-permute-start.12 = (f32[1,256,128]{2,1,0:T(8,128)S(1)}, f32[1,256,128]{2,1,0:T(8,128)S(1)}, u32[]{:S(2)}, u32[]{:S(2)}) collective-permute-start(f32[1,256,128]{2,1,0:T(8,128)S(1)} %bitcast.11), channel_id=1, source_target_pairs={{0,2},{1,3},{2,0},{3,1},{4,6},{5,7},{6,4},{7,5},{8,10},{9,11},{10,... | collective-permute-start | bytes 393224 | tf_op jit(solution)/shard_map/ppermute | solution.py:16
  47.3 3.4 %collective-permute-done.12 = f32[1,256,128]{2,1,0:T(8,128)S(1)} collective-permute-done((f32[1,256,128]{2,1,0:T(8,128)S(1)}, f32[1,256,128]{2,1,0:T(8,128)S(1)}, u32[]{:S(2)}, u32[]{:S(2)}) %collective-permute-start.12) | collective-permute-done | bytes 131104 | tf_op jit(solution)/shard_map/ppermute | solution.py:16
  54.6 2.9 %collective-permute-start.16 = (f32[2,32,128]{2,1,0:T(8,128)S(1)}, f32[2,32,128]{2,1,0:T(8,128)S(1)}, u32[]{:S(2)}, u32[]{:S(2)}) collective-permute-start(f32[2,32,128]{2,1,0:T(8,128)S(1)} %bitcast.16), channel_id=1, source_target_pairs={{0,12},{4,8},{8,4},{12,0},{16,28},{20,24},{24,20},{28,16},{1,13},{... | collective-permute-start | bytes 98312 | tf_op jit(solution)/shard_map/ppermute | solution.py:16
  59.7 2.8 %collective-permute-start.17 = (f32[1,32,128]{2,1,0:T(8,128)S(1)}, f32[1,32,128]{2,1,0:T(8,128)S(1)}, u32[]{:S(2)}, u32[]{:S(2)}) collective-permute-start(f32[1,32,128]{2,1,0:T(8,128)S(1)} %slice.63), channel_id=1, source_target_pairs={{0,16},{4,20},{8,24},{12,28},{16,0},{20,4},{24,8},{28,12},{1,17},{... | collective-permute-start | bytes 49160 | tf_op jit(solution)/shard_map/ppermute | solution.py:16
  62.5 1.9 %collective-permute-done.17 = f32[1,32,128]{2,1,0:T(8,128)S(1)} collective-permute-done((f32[1,32,128]{2,1,0:T(8,128)S(1)}, f32[1,32,128]{2,1,0:T(8,128)S(1)}, u32[]{:S(2)}, u32[]{:S(2)}) %collective-permute-start.17) | collective-permute-done | bytes 16416 | tf_op jit(solution)/shard_map/ppermute | solution.py:16
  (40 shorter events, 12.2 us)
Async XLA Ops:
  0.0 4.8 %collective-permute-start.1 = (s32[1024]{0:T(1024)}, s32[1024]{0:T(1024)S(1)}, u32[]{:S(2)}, u32[]{:S(2)}) collective-permute-start(s32[1024]{0:T(1024)} %refs_0_.1), channel_id=1, source_target_pairs={{0,4},{4,0},{8,12},{12,8},{16,20},{20,16},{24,28},{28,24},{1,5},{5... | collective-permute-start | bytes 12296 | tf_op jit(solution)/shard_map/ppermute | solution.py:16
  3.0 4.9 %collective-permute-start.2 = (s32[1024]{0:T(1024)}, s32[1024]{0:T(1024)S(1)}, u32[]{:S(2)}, u32[]{:S(2)}) collective-permute-start(s32[1024]{0:T(1024)} %refs_0_.1), channel_id=1, source_target_pairs={{0,12},{4,8},{8,4},{12,0},{16,28},{20,24},{24,20},{28,16},{1,13},{... | collective-permute-start | bytes 12296 | tf_op jit(solution)/shard_map/ppermute | solution.py:16
  4.8 11.9 %collective-permute-start.7 = (s32[1024]{0:T(1024)S(1)}, s32[1024]{0:T(1024)S(1)}, u32[]{:S(2)}, u32[]{:S(2)}) collective-permute-start(s32[1024]{0:T(1024)S(1)} %collective-permute-done.1.refs_0_), channel_id=1, source_target_pairs={{0,16},{4,20},{8,24},{12,28},{16,0},{20,4},{24,8},{28,12},{1,17},{... | collective-permute-start | bytes 12296 | tf_op jit(solution)/shard_map/ppermute | solution.py:16
  7.9 8.8 %collective-permute-start.8 = (s32[1024]{0:T(1024)S(1)}, s32[1024]{0:T(1024)S(1)}, u32[]{:S(2)}, u32[]{:S(2)}) collective-permute-start(s32[1024]{0:T(1024)S(1)} %collective-permute-done.2.refs_1_), channel_id=1, source_target_pairs={{0,16},{4,20},{8,24},{12,28},{16,0},{20,4},{24,8},{28,12},{1,17},{... | collective-permute-start | bytes 12296 | tf_op jit(solution)/shard_map/ppermute | solution.py:16
  10.3 1.6 %copy-start = (f32[32,16384]{1,0:T(8,128)S(1)}, f32[32,16384]{1,0:T(8,128)}, u32[]{:S(2)}) copy-start(f32[32,16384]{1,0:T(8,128)} %x_ref.1) | copy-start | bytes 6291460
  11.9 0.8 %copy-start.1 = (s32[16384]{0:T(1024)S(1)}, s32[16384]{0:T(1024)}, u32[]{:S(2)}) copy-start(s32[16384]{0:T(1024)} %param.5) | copy-start | bytes 196612
  18.5 4.0 %copy-start.2 = (s32[1024]{0:T(1024)S(1)}, s32[1024]{0:T(1024)}, u32[]{:S(2)}) copy-start(s32[1024]{0:T(1024)} %refs_0_.1) | copy-start | bytes 12292
  18.5 13.9 %collective-permute-start.9 = (f32[512,128]{1,0:T(8,128)S(1)}, f32[512,128]{1,0:T(8,128)S(1)}, u32[]{:S(2)}, u32[]{:S(2)}) collective-permute-start(f32[512,128]{1,0:T(8,128)S(1)} %pick.7), channel_id=1, source_target_pairs={{0,4},{4,0},{8,12},{12,8},{16,20},{20,16},{24,28},{28,24},{1,5},{5... | collective-permute-start | bytes 786440 | tf_op jit(solution)/shard_map/ppermute | solution.py:16
  20.9 15.1 %collective-permute-start.3 = (f32[512,128]{1,0:T(8,128)S(1)}, f32[512,128]{1,0:T(8,128)S(1)}, u32[]{:S(2)}, u32[]{:S(2)}) collective-permute-start(f32[512,128]{1,0:T(8,128)S(1)} %pick.5), channel_id=1, source_target_pairs={{0,4},{4,0},{8,12},{12,8},{16,20},{20,16},{24,28},{28,24},{1,5},{5... | collective-permute-start | bytes 786440 | tf_op jit(solution)/shard_map/ppermute | solution.py:16
  22.5 3.6 %collective-permute-start = (s32[1024]{0:T(1024)S(1)}, s32[1024]{0:T(1024)S(1)}, u32[]{:S(2)}, u32[]{:S(2)}) collective-permute-start(s32[1024]{0:T(1024)S(1)} %copy-done.2), channel_id=1, source_target_pairs={{0,8},{4,12},{8,0},{12,4},{16,24},{20,28},{24,16},{28,20},{1,9},{5... | collective-permute-start | bytes 12296 | tf_op jit(solution)/shard_map/ppermute | solution.py:16
  24.1 4.5 %collective-permute-start.5 = (s32[1024]{0:T(1024)S(1)}, s32[1024]{0:T(1024)S(1)}, u32[]{:S(2)}, u32[]{:S(2)}) collective-permute-start(s32[1024]{0:T(1024)S(1)} %copy-done.2), channel_id=1, source_target_pairs={{0,16},{4,20},{8,24},{12,28},{16,0},{20,4},{24,8},{28,12},{1,17},{... | collective-permute-start | bytes 12296 | tf_op jit(solution)/shard_map/ppermute | solution.py:16
  26.1 4.5 %collective-permute-start.6 = (s32[1024]{0:T(1024)S(1)}, s32[1024]{0:T(1024)S(1)}, u32[]{:S(2)}, u32[]{:S(2)}) collective-permute-start(s32[1024]{0:T(1024)S(1)} %collective-permute-done.refs_1_), channel_id=1, source_target_pairs={{0,16},{4,20},{8,24},{12,28},{16,0},{20,4},{24,8},{28,12},{1,17},{... | collective-permute-start | bytes 12296 | tf_op jit(solution)/shard_map/ppermute | solution.py:16
  32.5 5.8 %collective-permute-start.10 = (f32[256,128]{1,0:T(8,128)S(1)}, f32[256,128]{1,0:T(8,128)S(1)}, u32[]{:S(2)}, u32[]{:S(2)}) collective-permute-start(f32[256,128]{1,0:T(8,128)S(1)} %slice.55), channel_id=1, source_target_pairs={{0,8},{4,12},{8,0},{12,4},{16,24},{20,28},{24,16},{28,20},{1,9},{5... | collective-permute-start | bytes 393224 | tf_op jit(solution)/shard_map/ppermute | solution.py:16
  36.0 14.8 %copy-start.3 = (s32[1024,1]{0,1:T(1,128)S(1)}, s32[1024,1]{0,1:T(1,128)}, u32[]{:S(2)}) copy-start(s32[1024,1]{0,1:T(1,128)} %param.7) | copy-start | bytes 12292
  36.1 5.0 %collective-permute-start.4 = (f32[256,128]{1,0:T(8,128)S(1)}, f32[256,128]{1,0:T(8,128)S(1)}, u32[]{:S(2)}, u32[]{:S(2)}) collective-permute-start(f32[256,128]{1,0:T(8,128)S(1)} %slice.53), channel_id=1, source_target_pairs={{0,8},{4,12},{8,0},{12,4},{16,24},{20,28},{24,16},{28,20},{1,9},{5... | collective-permute-start | bytes 393224 | tf_op jit(solution)/shard_map/ppermute | solution.py:16
  38.4 7.3 %collective-permute-start.11 = (f32[256,128]{1,0:T(8,128)S(1)}, f32[256,128]{1,0:T(8,128)S(1)}, u32[]{:S(2)}, u32[]{:S(2)}) collective-permute-start(f32[256,128]{1,0:T(8,128)S(1)} %slice_add_fusion), channel_id=1, source_target_pairs={{0,16},{4,20},{8,24},{12,28},{16,0},{20,4},{24,8},{28,12},{1,17},{... | collective-permute-start | bytes 393224 | tf_op jit(solution)/shard_map/ppermute | solution.py:16
  45.7 5.0 %collective-permute-start.12 = (f32[1,256,128]{2,1,0:T(8,128)S(1)}, f32[1,256,128]{2,1,0:T(8,128)S(1)}, u32[]{:S(2)}, u32[]{:S(2)}) collective-permute-start(f32[1,256,128]{2,1,0:T(8,128)S(1)} %bitcast.11), channel_id=1, source_target_pairs={{0,2},{1,3},{2,0},{3,1},{4,6},{5,7},{6,4},{7,5},{8,10},{9,11},{10,... | collective-permute-start | bytes 393224 | tf_op jit(solution)/shard_map/ppermute | solution.py:16
  50.8 1.6 %collective-permute-start.13 = (f32[2,256,128]{2,1,0:T(8,128)S(1)}, f32[2,256,128]{2,1,0:T(8,128)S(1)}, u32[]{:S(2)}, u32[]{:S(2)}) collective-permute-start(f32[2,256,128]{2,1,0:T(8,128)S(1)} %pad_maximum_fusion), channel_id=1, source_target_pairs={{0,1},{1,0},{2,3},{3,2},{4,5},{5,4},{6,7},{7,6},{8,9},{9,8},{10,11... | collective-permute-start | bytes 786440 | tf_op jit(solution)/shard_map/ppermute | solution.py:16
  53.9 4.0 %collective-permute-start.14 = (f32[2,32,128]{2,1,0:T(8,128)S(1)}, f32[2,32,128]{2,1,0:T(8,128)S(1)}, u32[]{:S(2)}, u32[]{:S(2)}) collective-permute-start(f32[2,32,128]{2,1,0:T(8,128)S(1)} %bitcast.18), channel_id=1, source_target_pairs={{0,4},{4,0},{8,12},{12,8},{16,20},{20,16},{24,28},{28,24},{1,5},{5... | collective-permute-start | bytes 98312 | tf_op jit(solution)/shard_map/ppermute | solution.py:16
  54.6 4.1 %collective-permute-start.15 = (f32[2,32,128]{2,1,0:T(8,128)S(1)}, f32[2,32,128]{2,1,0:T(8,128)S(1)}, u32[]{:S(2)}, u32[]{:S(2)}) collective-permute-start(f32[2,32,128]{2,1,0:T(8,128)S(1)} %bitcast.17), channel_id=1, source_target_pairs={{0,8},{4,12},{8,0},{12,4},{16,24},{20,28},{24,16},{28,20},{1,9},{5... | collective-permute-start | bytes 98312 | tf_op jit(solution)/shard_map/ppermute | solution.py:16
  54.6 5.2 %collective-permute-start.16 = (f32[2,32,128]{2,1,0:T(8,128)S(1)}, f32[2,32,128]{2,1,0:T(8,128)S(1)}, u32[]{:S(2)}, u32[]{:S(2)}) collective-permute-start(f32[2,32,128]{2,1,0:T(8,128)S(1)} %bitcast.16), channel_id=1, source_target_pairs={{0,12},{4,8},{8,4},{12,0},{16,28},{20,24},{24,20},{28,16},{1,13},{... | collective-permute-start | bytes 98312 | tf_op jit(solution)/shard_map/ppermute | solution.py:16
  59.7 4.7 %collective-permute-start.17 = (f32[1,32,128]{2,1,0:T(8,128)S(1)}, f32[1,32,128]{2,1,0:T(8,128)S(1)}, u32[]{:S(2)}, u32[]{:S(2)}) collective-permute-start(f32[1,32,128]{2,1,0:T(8,128)S(1)} %slice.63), channel_id=1, source_target_pairs={{0,16},{4,20},{8,24},{12,28},{16,0},{20,4},{24,8},{28,12},{1,17},{... | collective-permute-start | bytes 49160 | tf_op jit(solution)/shard_map/ppermute | solution.py:16
where the time goes:
time: 65.2 us; the launch traced here: 65.1 us
  starting transfers between devices  26.8 us (41%)
  waiting for transfers between devices  21.9 us (34%)
  Pallas kernels  12.7 us (19%)
  local copies, waits for them, and re-layouts  2.72 us (4%)
  other arithmetic  0.75 us (1%)
    ppermute x18, starting transfers between devices, swapped(): lax.ppermute(x, axis, [(i, i ^ distance) for i in range(lax.axis_size(axi...  26.8 us
    ppermute x18, waiting for transfers between devices, swapped(): lax.ppermute(x, axis, [(i, i ^ distance) for i in range(lax.axis_size(axi...  21.9 us
    pallas_call x4, Pallas kernels, pick(): pl.pallas_call(functools.partial(pick_kernel, width, slots, count, len(sl...  7.3 us
    pallas_call x1, Pallas kernels, transform_table(): pl.pallas_call(functools.partial(table_kernel, width), out_shape=jax.Shap...  3.37 us
    unnamed x9, local copies, waits for them, and re-layouts  2.66 us
    pallas_call x1, Pallas kernels, body(): pl.pallas_call(functools.partial(gram_kernel, width, count, devices, scal...  1.49 us
  transfers between devices with their start and end apart: 18, of which 13 were waited for; matrix products, arithmetic and copies ran while one was open for 1% of the time, Pallas kernels for 14%

commit v1 on v0

--- a/solution.py
+++ b/solution.py
@@ -61,10 +61,16 @@
 def table_kernel(width, work_ref, table_ref):
     group = LANES // width
     bands = width // 8
-    pair = 2 if width * 8 >= 2 * width else 1
     row = lax.broadcasted_iota(jnp.int32, (LANES, 2 * LANES), 0)
     column = lax.broadcasted_iota(jnp.int32, (LANES, 2 * LANES), 1)
     hadamard = (1 - 2 * parity(row & (column & (LANES - 1)))).astype(f32).astype(bf16)
+    lane = lax.broadcasted_iota(jnp.int32, (LANES, LANES), 1) // width
+    in_lane = [lane == g for g in range(group)]
+    repeating = 4 if width * 8 > LANES else 8
+
+    def times(top, low):
+        both = jnp.concatenate([top, low], axis=1)
+        return lax.dot_general(hadamard, both, (((1,), (1,)), ((), ())), preferred_element_type=f32)
 
     def some(hi, _):
         rows = [
@@ -72,20 +78,24 @@
         ]
         y = jnp.concatenate([rows[band][lo] for lo in range(8) for band in range(bands)], axis=0)
         top, low = halves(y)
-        for e in range(0, 8, pair):
-            both = [
-                jnp.concatenate([v[(e + i) * width : (e + i + 1) * width] for i in range(pair) for _ in range(group)])
+        results = []
+        for e in range(0, repeating, 2):
+            parts = [
+                jnp.concatenate([v[(e + i) * width : (e + i + 1) * width] for i in range(2) for _ in range(group)])
                 for v in (top, low)
             ]
-            mixed = lax.dot_general(
-                hadamard,
-                jnp.concatenate(both, axis=1),
-                (((1,), (1,)), ((), ())),
-                preferred_element_type=f32,
-            )
-            for i in range(pair):
-                start = pl.multiple_of((hi * 8 + e + i) * LANES, LANES)
-                table_ref[pl.ds(start, LANES), :] = mixed[:, i * LANES : (i + 1) * LANES]
+            mixed = times(*parts)
+            results += [mixed[:, :LANES], mixed[:, LANES:]]
+        for e in range(repeating, 8, group):
+            mixed = times(top[e * width :][:LANES], low[e * width :][:LANES])
+            turned = [mixed] + [pltpu.roll(mixed, k * width, 1) for k in range(1, group)]
+            for i in range(group):
+                total = turned[-i % group]
+                for g in range(1, group):
+                    total = jnp.where(in_lane[g], turned[(g - i) % group], total)
+                results.append(total)
+        for e, result in enumerate(results):
+            table_ref[pl.ds(pl.multiple_of((hi * 8 + e) * LANES, LANES), LANES), :] = result
         return 0
 
     lax.fori_loop(0, 16, some, 0, unroll=4)

time: 65.2 us -> 64.5 us (0.989)
  Pallas kernels: 12.7 us -> 11.9 us
    pallas_call x1, Pallas kernels: 3.37 us -> 2.59 us  [transform_table(): pl.pallas_call(functools.partial(table_kernel, width), out_shape=jax.Shap...]
  transfers between devices with their start and end apart: 18 -> 18, of which waited for: 13 -> 13; matrix products, arithmetic and copies ran while one was open for 1% -> 1% of each run, Pallas kernels for 14% -> 13%
where the time goes in v1:
time: 64.5 us; the launch traced here: 64.3 us
  starting transfers between devices  26.8 us (42%)
  waiting for transfers between devices  21.9 us (34%)
  Pallas kernels  11.9 us (18%)
  local copies, waits for them, and re-layouts  2.72 us (4%)
  other arithmetic  0.75 us (1%)
    ppermute x18, starting transfers between devices, swapped(): lax.ppermute(x, axis, [(i, i ^ distance) for i in range(lax.axis_size(axi...  26.8 us
    ppermute x18, waiting for transfers between devices, swapped(): lax.ppermute(x, axis, [(i, i ^ distance) for i in range(lax.axis_size(axi...  21.9 us
    pallas_call x4, Pallas kernels, pick(): pl.pallas_call(functools.partial(pick_kernel, width, slots, count, len(sl...  7.3 us
    unnamed x9, local copies, waits for them, and re-layouts  2.66 us
    pallas_call x1, Pallas kernels, transform_table(): pl.pallas_call(functools.partial(table_kernel, width), out_shape=jax.Shap...  2.59 us
    pallas_call x1, Pallas kernels, body(): pl.pallas_call(functools.partial(gram_kernel, width, count, devices, scal...  1.49 us
  transfers between devices with their start and end apart: 18, of which 13 were waited for; matrix products, arithmetic and copies ran while one was open for 1% of the time, Pallas kernels for 13%

profile of v1, /device:TPU:0, one launch (start us, length us, event | category | flops | bytes accessed | tf_op | source)
XLA Modules:
  0.0 64.3 jit_solution(17120523610120939366)
XLA Ops:
  0.0 3.0 %collective-permute-start.1 = (s32[1024]{0:T(1024)}, s32[1024]{0:T(1024)S(1)}, u32[]{:S(2)}, u32[]{:S(2)}) collective-permute-start(s32[1024]{0:T(1024)} %refs_0_.1), channel_id=1, source_target_pairs={{0,4},{4,0},{8,12},{12,8},{16,20},{20,16},{24,28},{28,24},{1,5},{5... | collective-permute-start | bytes 12296 | tf_op jit(solution)/shard_map/ppermute | solution.py:16
  3.0 1.5 %collective-permute-start.2 = (s32[1024]{0:T(1024)}, s32[1024]{0:T(1024)S(1)}, u32[]{:S(2)}, u32[]{:S(2)}) collective-permute-start(s32[1024]{0:T(1024)} %refs_0_.1), channel_id=1, source_target_pairs={{0,12},{4,8},{8,4},{12,0},{16,28},{20,24},{24,20},{28,16},{1,13},{... | collective-permute-start | bytes 12296 | tf_op jit(solution)/shard_map/ppermute | solution.py:16
  4.8 3.1 %collective-permute-start.7 = (s32[1024]{0:T(1024)S(1)}, s32[1024]{0:T(1024)S(1)}, u32[]{:S(2)}, u32[]{:S(2)}) collective-permute-start(s32[1024]{0:T(1024)S(1)} %collective-permute-done.1.refs_0_), channel_id=1, source_target_pairs={{0,16},{4,20},{8,24},{12,28},{16,0},{20,4},{24,8},{28,12},{1,17},{... | collective-permute-start | bytes 12296 | tf_op jit(solution)/shard_map/ppermute | solution.py:16
  7.9 2.4 %collective-permute-start.8 = (s32[1024]{0:T(1024)S(1)}, s32[1024]{0:T(1024)S(1)}, u32[]{:S(2)}, u32[]{:S(2)}) collective-permute-start(s32[1024]{0:T(1024)S(1)} %collective-permute-done.2.refs_1_), channel_id=1, source_target_pairs={{0,16},{4,20},{8,24},{12,28},{16,0},{20,4},{24,8},{28,12},{1,17},{... | collective-permute-start | bytes 12296 | tf_op jit(solution)/shard_map/ppermute | solution.py:16
  10.3 1.6 %copy-done = f32[32,16384]{1,0:T(8,128)S(1)} copy-done((f32[32,16384]{1,0:T(8,128)S(1)}, f32[32,16384]{1,0:T(8,128)}, u32[]{:S(2)}) %copy-start) | copy-done | bytes 2097176
  13.3 2.6 %table.1.refs_2_ = f32[16384,128]{1,0:T(8,128)S(1)} custom-call(f32[128,32,128]{2,1,0:T(8,128)S(1)} %rows.1.work_ref), custom_call_target="tpu_custom_call" | custom-call | tf_op jit(solution)/shard_map/table/pallas_call | solution.py:196
  15.9 1.8 %pick.7 = f32[512,128]{1,0:T(8,128)S(1)} custom-call(s32[1024]{0:T(1024)S(1)} %collective-permute-done.7.refs_0_, s32[1024]{0:T(1024)S(1)} %collective-permute-done.8.refs_1_, f32[16384,128]{1,0:T(8,128)S(1)} %table.1.refs_2_), custom_call_target="tpu_custom_call" | custom-call | tf_op jit(solution)/shard_map/pick/pallas_call | solution.py:238
  18.3 1.8 %pick.5 = f32[512,128]{1,0:T(8,128)S(1)} custom-call(s32[1024]{0:T(1024)S(1)} %collective-permute-done.1.refs_0_, s32[1024]{0:T(1024)S(1)} %collective-permute-done.2.refs_1_, f32[16384,128]{1,0:T(8,128)S(1)} %table.1.refs_2_), custom_call_target="tpu_custom_call" | custom-call | tf_op jit(solution)/shard_map/pick/pallas_call | solution.py:238
  20.2 1.6 %collective-permute-start.3 = (f32[512,128]{1,0:T(8,128)S(1)}, f32[512,128]{1,0:T(8,128)S(1)}, u32[]{:S(2)}, u32[]{:S(2)}) collective-permute-start(f32[512,128]{1,0:T(8,128)S(1)} %pick.5), channel_id=1, source_target_pairs={{0,4},{4,0},{8,12},{12,8},{16,20},{20,16},{24,28},{28,24},{1,5},{5... | collective-permute-start | bytes 786440 | tf_op jit(solution)/shard_map/ppermute | solution.py:16
  21.7 1.6 %collective-permute-start = (s32[1024]{0:T(1024)S(1)}, s32[1024]{0:T(1024)S(1)}, u32[]{:S(2)}, u32[]{:S(2)}) collective-permute-start(s32[1024]{0:T(1024)S(1)} %copy-done.2), channel_id=1, source_target_pairs={{0,8},{4,12},{8,0},{12,4},{16,24},{20,28},{24,16},{28,20},{1,9},{5... | collective-permute-start | bytes 12296 | tf_op jit(solution)/shard_map/ppermute | solution.py:16
  23.8 1.5 %collective-permute-done.refs_1_ = s32[1024]{0:T(1024)S(1)} collective-permute-done((s32[1024]{0:T(1024)S(1)}, s32[1024]{0:T(1024)S(1)}, u32[]{:S(2)}, u32[]{:S(2)}) %collective-permute-start) | collective-permute-done | bytes 4128 | tf_op jit(solution)/shard_map/ppermute | solution.py:16
  26.2 1.6 %collective-permute-done.5.refs_0_ = s32[1024]{0:T(1024)S(1)} collective-permute-done((s32[1024]{0:T(1024)S(1)}, s32[1024]{0:T(1024)S(1)}, u32[]{:S(2)}, u32[]{:S(2)}) %collective-permute-start.5) | collective-permute-done | bytes 4128 | tf_op jit(solution)/shard_map/ppermute | solution.py:16
  27.8 2.0 %collective-permute-done.6.refs_1_ = s32[1024]{0:T(1024)S(1)} collective-permute-done((s32[1024]{0:T(1024)S(1)}, s32[1024]{0:T(1024)S(1)}, u32[]{:S(2)}, u32[]{:S(2)}) %collective-permute-start.6) | collective-permute-done | bytes 4128 | tf_op jit(solution)/shard_map/ppermute | solution.py:16
  29.8 1.8 %pick.6 = f32[512,128]{1,0:T(8,128)S(1)} custom-call(s32[1024]{0:T(1024)S(1)} %collective-permute-done.5.refs_0_, s32[1024]{0:T(1024)S(1)} %collective-permute-done.6.refs_1_, f32[16384,128]{1,0:T(8,128)S(1)} %table.1.refs_2_), custom_call_target="tpu_custom_call" | custom-call | tf_op jit(solution)/shard_map/pick/pallas_call | solution.py:238
  31.7 1.7 %collective-permute-start.10 = (f32[256,128]{1,0:T(8,128)S(1)}, f32[256,128]{1,0:T(8,128)S(1)}, u32[]{:S(2)}, u32[]{:S(2)}) collective-permute-start(f32[256,128]{1,0:T(8,128)S(1)} %slice.55), channel_id=1, source_target_pairs={{0,8},{4,12},{8,0},{12,4},{16,24},{20,28},{24,16},{28,20},{1,9},{5... | collective-permute-start | bytes 393224 | tf_op jit(solution)/shard_map/ppermute | solution.py:16
  33.4 1.8 %pick.4 = f32[512,128]{1,0:T(8,128)S(1)} custom-call(s32[1024]{0:T(1024)S(1)} %copy-done.2, s32[1024]{0:T(1024)S(1)} %collective-permute-done.refs_1_, f32[16384,128]{1,0:T(8,128)S(1)} %table.1.refs_2_), custom_call_target="tpu_custom_call" | custom-call | tf_op jit(solution)/shard_map/pick/pallas_call | solution.py:238
  35.8 1.8 %collective-permute-done.10 = f32[256,128]{1,0:T(8,128)S(1)} collective-permute-done((f32[256,128]{1,0:T(8,128)S(1)}, f32[256,128]{1,0:T(8,128)S(1)}, u32[]{:S(2)}, u32[]{:S(2)}) %collective-permute-start.10) | collective-permute-done | bytes 131104 | tf_op jit(solution)/shard_map/ppermute | solution.py:16
  37.6 1.5 %collective-permute-start.11 = (f32[256,128]{1,0:T(8,128)S(1)}, f32[256,128]{1,0:T(8,128)S(1)}, u32[]{:S(2)}, u32[]{:S(2)}) collective-permute-start(f32[256,128]{1,0:T(8,128)S(1)} %slice_add_fusion), channel_id=1, source_target_pairs={{0,16},{4,20},{8,24},{12,28},{16,0},{20,4},{24,8},{28,12},{1,17},{... | collective-permute-start | bytes 393224 | tf_op jit(solution)/shard_map/ppermute | solution.py:16
  40.4 4.6 %collective-permute-done.11 = f32[256,128]{1,0:T(8,128)S(1)} collective-permute-done((f32[256,128]{1,0:T(8,128)S(1)}, f32[256,128]{1,0:T(8,128)S(1)}, u32[]{:S(2)}, u32[]{:S(2)}) %collective-permute-start.11) | collective-permute-done | bytes 131104 | tf_op jit(solution)/shard_map/ppermute | solution.py:16
  45.0 1.6 %collective-permute-start.12 = (f32[1,256,128]{2,1,0:T(8,128)S(1)}, f32[1,256,128]{2,1,0:T(8,128)S(1)}, u32[]{:S(2)}, u32[]{:S(2)}) collective-permute-start(f32[1,256,128]{2,1,0:T(8,128)S(1)} %bitcast.11), channel_id=1, source_target_pairs={{0,2},{1,3},{2,0},{3,1},{4,6},{5,7},{6,4},{7,5},{8,10},{9,11},{10,... | collective-permute-start | bytes 393224 | tf_op jit(solution)/shard_map/ppermute | solution.py:16
  46.5 3.4 %collective-permute-done.12 = f32[1,256,128]{2,1,0:T(8,128)S(1)} collective-permute-done((f32[1,256,128]{2,1,0:T(8,128)S(1)}, f32[1,256,128]{2,1,0:T(8,128)S(1)}, u32[]{:S(2)}, u32[]{:S(2)}) %collective-permute-start.12) | collective-permute-done | bytes 131104 | tf_op jit(solution)/shard_map/ppermute | solution.py:16
  53.8 2.9 %collective-permute-start.16 = (f32[2,32,128]{2,1,0:T(8,128)S(1)}, f32[2,32,128]{2,1,0:T(8,128)S(1)}, u32[]{:S(2)}, u32[]{:S(2)}) collective-permute-start(f32[2,32,128]{2,1,0:T(8,128)S(1)} %bitcast.16), channel_id=1, source_target_pairs={{0,12},{4,8},{8,4},{12,0},{16,28},{20,24},{24,20},{28,16},{1,13},{... | collective-permute-start | bytes 98312 | tf_op jit(solution)/shard_map/ppermute | solution.py:16
  59.0 2.8 %collective-permute-start.17 = (f32[1,32,128]{2,1,0:T(8,128)S(1)}, f32[1,32,128]{2,1,0:T(8,128)S(1)}, u32[]{:S(2)}, u32[]{:S(2)}) collective-permute-start(f32[1,32,128]{2,1,0:T(8,128)S(1)} %slice.63), channel_id=1, source_target_pairs={{0,16},{4,20},{8,24},{12,28},{16,0},{20,4},{24,8},{28,12},{1,17},{... | collective-permute-start | bytes 49160 | tf_op jit(solution)/shard_map/ppermute | solution.py:16
  61.7 2.0 %collective-permute-done.17 = f32[1,32,128]{2,1,0:T(8,128)S(1)} collective-permute-done((f32[1,32,128]{2,1,0:T(8,128)S(1)}, f32[1,32,128]{2,1,0:T(8,128)S(1)}, u32[]{:S(2)}, u32[]{:S(2)}) %collective-permute-start.17) | collective-permute-done | bytes 16416 | tf_op jit(solution)/shard_map/ppermute | solution.py:16
  (40 shorter events, 12.2 us)
Async XLA Ops:
  0.0 4.8 %collective-permute-start.1 = (s32[1024]{0:T(1024)}, s32[1024]{0:T(1024)S(1)}, u32[]{:S(2)}, u32[]{:S(2)}) collective-permute-start(s32[1024]{0:T(1024)} %refs_0_.1), channel_id=1, source_target_pairs={{0,4},{4,0},{8,12},{12,8},{16,20},{20,16},{24,28},{28,24},{1,5},{5... | collective-permute-start | bytes 12296 | tf_op jit(solution)/shard_map/ppermute | solution.py:16
  3.0 4.9 %collective-permute-start.2 = (s32[1024]{0:T(1024)}, s32[1024]{0:T(1024)S(1)}, u32[]{:S(2)}, u32[]{:S(2)}) collective-permute-start(s32[1024]{0:T(1024)} %refs_0_.1), channel_id=1, source_target_pairs={{0,12},{4,8},{8,4},{12,0},{16,28},{20,24},{24,20},{28,16},{1,13},{... | collective-permute-start | bytes 12296 | tf_op jit(solution)/shard_map/ppermute | solution.py:16
  4.8 11.1 %collective-permute-start.7 = (s32[1024]{0:T(1024)S(1)}, s32[1024]{0:T(1024)S(1)}, u32[]{:S(2)}, u32[]{:S(2)}) collective-permute-start(s32[1024]{0:T(1024)S(1)} %collective-permute-done.1.refs_0_), channel_id=1, source_target_pairs={{0,16},{4,20},{8,24},{12,28},{16,0},{20,4},{24,8},{28,12},{1,17},{... | collective-permute-start | bytes 12296 | tf_op jit(solution)/shard_map/ppermute | solution.py:16
  7.9 8.0 %collective-permute-start.8 = (s32[1024]{0:T(1024)S(1)}, s32[1024]{0:T(1024)S(1)}, u32[]{:S(2)}, u32[]{:S(2)}) collective-permute-start(s32[1024]{0:T(1024)S(1)} %collective-permute-done.2.refs_1_), channel_id=1, source_target_pairs={{0,16},{4,20},{8,24},{12,28},{16,0},{20,4},{24,8},{28,12},{1,17},{... | collective-permute-start | bytes 12296 | tf_op jit(solution)/shard_map/ppermute | solution.py:16
  10.3 1.6 %copy-start = (f32[32,16384]{1,0:T(8,128)S(1)}, f32[32,16384]{1,0:T(8,128)}, u32[]{:S(2)}) copy-start(f32[32,16384]{1,0:T(8,128)} %x_ref.1) | copy-start | bytes 6291460
  11.9 0.8 %copy-start.1 = (s32[16384]{0:T(1024)S(1)}, s32[16384]{0:T(1024)}, u32[]{:S(2)}) copy-start(s32[16384]{0:T(1024)} %param.5) | copy-start | bytes 196612
  17.7 4.0 %copy-start.2 = (s32[1024]{0:T(1024)S(1)}, s32[1024]{0:T(1024)}, u32[]{:S(2)}) copy-start(s32[1024]{0:T(1024)} %refs_0_.1) | copy-start | bytes 12292
  17.7 13.9 %collective-permute-start.9 = (f32[512,128]{1,0:T(8,128)S(1)}, f32[512,128]{1,0:T(8,128)S(1)}, u32[]{:S(2)}, u32[]{:S(2)}) collective-permute-start(f32[512,128]{1,0:T(8,128)S(1)} %pick.7), channel_id=1, source_target_pairs={{0,4},{4,0},{8,12},{12,8},{16,20},{20,16},{24,28},{28,24},{1,5},{5... | collective-permute-start | bytes 786440 | tf_op jit(solution)/shard_map/ppermute | solution.py:16
  20.2 15.1 %collective-permute-start.3 = (f32[512,128]{1,0:T(8,128)S(1)}, f32[512,128]{1,0:T(8,128)S(1)}, u32[]{:S(2)}, u32[]{:S(2)}) collective-permute-start(f32[512,128]{1,0:T(8,128)S(1)} %pick.5), channel_id=1, source_target_pairs={{0,4},{4,0},{8,12},{12,8},{16,20},{20,16},{24,28},{28,24},{1,5},{5... | collective-permute-start | bytes 786440 | tf_op jit(solution)/shard_map/ppermute | solution.py:16
  21.7 3.6 %collective-permute-start = (s32[1024]{0:T(1024)S(1)}, s32[1024]{0:T(1024)S(1)}, u32[]{:S(2)}, u32[]{:S(2)}) collective-permute-start(s32[1024]{0:T(1024)S(1)} %copy-done.2), channel_id=1, source_target_pairs={{0,8},{4,12},{8,0},{12,4},{16,24},{20,28},{24,16},{28,20},{1,9},{5... | collective-permute-start | bytes 12296 | tf_op jit(solution)/shard_map/ppermute | solution.py:16
  23.3 4.5 %collective-permute-start.5 = (s32[1024]{0:T(1024)S(1)}, s32[1024]{0:T(1024)S(1)}, u32[]{:S(2)}, u32[]{:S(2)}) collective-permute-start(s32[1024]{0:T(1024)S(1)} %copy-done.2), channel_id=1, source_target_pairs={{0,16},{4,20},{8,24},{12,28},{16,0},{20,4},{24,8},{28,12},{1,17},{... | collective-permute-start | bytes 12296 | tf_op jit(solution)/shard_map/ppermute | solution.py:16
  25.3 4.5 %collective-permute-start.6 = (s32[1024]{0:T(1024)S(1)}, s32[1024]{0:T(1024)S(1)}, u32[]{:S(2)}, u32[]{:S(2)}) collective-permute-start(s32[1024]{0:T(1024)S(1)} %collective-permute-done.refs_1_), channel_id=1, source_target_pairs={{0,16},{4,20},{8,24},{12,28},{16,0},{20,4},{24,8},{28,12},{1,17},{... | collective-permute-start | bytes 12296 | tf_op jit(solution)/shard_map/ppermute | solution.py:16
  31.7 5.8 %collective-permute-start.10 = (f32[256,128]{1,0:T(8,128)S(1)}, f32[256,128]{1,0:T(8,128)S(1)}, u32[]{:S(2)}, u32[]{:S(2)}) collective-permute-start(f32[256,128]{1,0:T(8,128)S(1)} %slice.55), channel_id=1, source_target_pairs={{0,8},{4,12},{8,0},{12,4},{16,24},{20,28},{24,16},{28,20},{1,9},{5... | collective-permute-start | bytes 393224 | tf_op jit(solution)/shard_map/ppermute | solution.py:16
  35.3 14.8 %copy-start.3 = (s32[1024,1]{0,1:T(1,128)S(1)}, s32[1024,1]{0,1:T(1,128)}, u32[]{:S(2)}) copy-start(s32[1024,1]{0,1:T(1,128)} %param.7) | copy-start | bytes 12292
  35.3 5.0 %collective-permute-start.4 = (f32[256,128]{1,0:T(8,128)S(1)}, f32[256,128]{1,0:T(8,128)S(1)}, u32[]{:S(2)}, u32[]{:S(2)}) collective-permute-start(f32[256,128]{1,0:T(8,128)S(1)} %slice.53), channel_id=1, source_target_pairs={{0,8},{4,12},{8,0},{12,4},{16,24},{20,28},{24,16},{28,20},{1,9},{5... | collective-permute-start | bytes 393224 | tf_op jit(solution)/shard_map/ppermute | solution.py:16
  37.6 7.3 %collective-permute-start.11 = (f32[256,128]{1,0:T(8,128)S(1)}, f32[256,128]{1,0:T(8,128)S(1)}, u32[]{:S(2)}, u32[]{:S(2)}) collective-permute-start(f32[256,128]{1,0:T(8,128)S(1)} %slice_add_fusion), channel_id=1, source_target_pairs={{0,16},{4,20},{8,24},{12,28},{16,0},{20,4},{24,8},{28,12},{1,17},{... | collective-permute-start | bytes 393224 | tf_op jit(solution)/shard_map/ppermute | solution.py:16
  45.0 5.0 %collective-permute-start.12 = (f32[1,256,128]{2,1,0:T(8,128)S(1)}, f32[1,256,128]{2,1,0:T(8,128)S(1)}, u32[]{:S(2)}, u32[]{:S(2)}) collective-permute-start(f32[1,256,128]{2,1,0:T(8,128)S(1)} %bitcast.11), channel_id=1, source_target_pairs={{0,2},{1,3},{2,0},{3,1},{4,6},{5,7},{6,4},{7,5},{8,10},{9,11},{10,... | collective-permute-start | bytes 393224 | tf_op jit(solution)/shard_map/ppermute | solution.py:16
  50.0 1.6 %collective-permute-start.13 = (f32[2,256,128]{2,1,0:T(8,128)S(1)}, f32[2,256,128]{2,1,0:T(8,128)S(1)}, u32[]{:S(2)}, u32[]{:S(2)}) collective-permute-start(f32[2,256,128]{2,1,0:T(8,128)S(1)} %pad_maximum_fusion), channel_id=1, source_target_pairs={{0,1},{1,0},{2,3},{3,2},{4,5},{5,4},{6,7},{7,6},{8,9},{9,8},{10,11... | collective-permute-start | bytes 786440 | tf_op jit(solution)/shard_map/ppermute | solution.py:16
  53.1 4.0 %collective-permute-start.14 = (f32[2,32,128]{2,1,0:T(8,128)S(1)}, f32[2,32,128]{2,1,0:T(8,128)S(1)}, u32[]{:S(2)}, u32[]{:S(2)}) collective-permute-start(f32[2,32,128]{2,1,0:T(8,128)S(1)} %bitcast.18), channel_id=1, source_target_pairs={{0,4},{4,0},{8,12},{12,8},{16,20},{20,16},{24,28},{28,24},{1,5},{5... | collective-permute-start | bytes 98312 | tf_op jit(solution)/shard_map/ppermute | solution.py:16
  53.8 4.1 %collective-permute-start.15 = (f32[2,32,128]{2,1,0:T(8,128)S(1)}, f32[2,32,128]{2,1,0:T(8,128)S(1)}, u32[]{:S(2)}, u32[]{:S(2)}) collective-permute-start(f32[2,32,128]{2,1,0:T(8,128)S(1)} %bitcast.17), channel_id=1, source_target_pairs={{0,8},{4,12},{8,0},{12,4},{16,24},{20,28},{24,16},{28,20},{1,9},{5... | collective-permute-start | bytes 98312 | tf_op jit(solution)/shard_map/ppermute | solution.py:16
  53.8 5.2 %collective-permute-start.16 = (f32[2,32,128]{2,1,0:T(8,128)S(1)}, f32[2,32,128]{2,1,0:T(8,128)S(1)}, u32[]{:S(2)}, u32[]{:S(2)}) collective-permute-start(f32[2,32,128]{2,1,0:T(8,128)S(1)} %bitcast.16), channel_id=1, source_target_pairs={{0,12},{4,8},{8,4},{12,0},{16,28},{20,24},{24,20},{28,16},{1,13},{... | collective-permute-start | bytes 98312 | tf_op jit(solution)/shard_map/ppermute | solution.py:16
  59.0 4.7 %collective-permute-start.17 = (f32[1,32,128]{2,1,0:T(8,128)S(1)}, f32[1,32,128]{2,1,0:T(8,128)S(1)}, u32[]{:S(2)}, u32[]{:S(2)}) collective-permute-start(f32[1,32,128]{2,1,0:T(8,128)S(1)} %slice.63), channel_id=1, source_target_pairs={{0,16},{4,20},{8,24},{12,28},{16,0},{20,4},{24,8},{28,12},{1,17},{... | collective-permute-start | bytes 49160 | tf_op jit(solution)/shard_map/ppermute | solution.py:16

commit v2 on v1

--- a/solution.py
+++ b/solution.py
@@ -101,7 +101,7 @@
     lax.fori_loop(0, 16, some, 0, unroll=4)
 
 
-def pick_kernel(width, slots, count, straight, *refs):
+def pick_kernel(width, slots, spots, count, first, rows, straight, *refs):
     offset_refs, table_ref, out_ref = refs[:-2], refs[-2], refs[-1]
     group = LANES // width
     per = count // group
@@ -112,29 +112,30 @@
     me = lax.axis_index("row")
     for place, slot in enumerate(slots):
         sign = (1 - 2 * parity(me & (me ^ slot))).astype(f32)
+        which, base = spots[place]
 
         def block(inner):
             total = None
             for g in range(group):
                 part = None
                 for s in range(8):
-                    spot = offset_refs[place][inner + (g * per + s)]
+                    spot = offset_refs[which][inner + (base + first + g * per + s)]
                     value = jnp.broadcast_to(table_ref[pl.ds(spot, 1), :], (8, LANES))
                     part = value if part is None else jnp.where(in_sub[s], value, part)
                 total = part if total is None else jnp.where(in_lane[g], part, total)
             return total * sign
 
         if straight:
-            for inner in range(0, per, 8):
-                out_ref[pl.ds(place * per + inner, 8), :] = block(inner)
+            for inner in range(0, rows, 8):
+                out_ref[pl.ds(place * rows + inner, 8), :] = block(inner)
         else:
 
             def some(it, _):
                 inner = pl.multiple_of(it * 8, 8)
-                out_ref[pl.ds(place * per + inner, 8), :] = block(inner)
+                out_ref[pl.ds(place * rows + inner, 8), :] = block(inner)
                 return 0
 
-            lax.fori_loop(0, per // 8, some, 0)
+            lax.fori_loop(0, rows // 8, some, 0)
 
 
 def gram_kernel(width, count, named, scale, owner_ref, *refs):
@@ -207,17 +208,6 @@
     return int(format(i, f"0{bits}b")[::-1], 2) if bits else 0
 
 
-def spread(pieces, level):
-    distance = 1 << level
-    if len(pieces) <= 4:
-        arrived = []
-        for piece in pieces:
-            arrived.append(swapped(piece, "row", distance))
-        return pieces + arrived
-    arrived = swapped(jnp.stack(pieces), "row", distance)
-    return pieces + [arrived[i] for i in range(len(pieces))]
-
-
 def body(panel, signs, offsets, owners):
     width, row_count = panel.shape
     devices = lax.axis_size("row")
@@ -230,37 +220,58 @@
     for t in range(1, 1 << near):
         listed.append(swapped(offsets, "row", t))
     work = transform_rows(panel, signs)
-    for level in range(near, bits):
-        listed = spread(listed, level)
+    arrays, entries = list(listed), [(t, 0) for t in range(1 << near)]
+    if bits > near:
+        far = jnp.concatenate(listed)
+        far = swapped(far, "row", 1 << near)
+        arrays.append(far)
+        entries += [(len(arrays) - 1, t * count) for t in range(1 << near)]
+        for level in range(near + 1, bits):
+            held = jnp.concatenate([arrays[k][at : at + count] for k, at in entries])
+            arrays.append(swapped(held, "row", 1 << level))
+            entries += [(len(arrays) - 1, t * count) for t in range(1 << level)]
     table = transform_table(work, width)
 
-    def pick(slots):
+    def pick(slots, first, rows):
+        used = sorted({entries[t][0] for t in slots})
+        spots = [(used.index(entries[t][0]), entries[t][1]) for t in slots]
+        straight = len(slots) * rows * group <= 4096
         return pl.pallas_call(
-            functools.partial(pick_kernel, width, slots, count, len(slots) <= 4),
-            out_shape=jax.ShapeDtypeStruct((len(slots) * per, LANES), f32),
-            in_specs=[SMEM] * len(slots) + [VMEM],
+            functools.partial(pick_kernel, width, slots, spots, count, first, rows, straight),
+            out_shape=jax.ShapeDtypeStruct((len(slots) * rows, LANES), f32),
+            in_specs=[SMEM] * len(used) + [VMEM],
             out_specs=VMEM,
             compiler_params=PARAMS,
             name="pick",
-        )(*[listed[t] for t in slots], table)
-
-    chunks = []
-    for upper in range(2):
-        odd = list(range(1 + upper * devices // 2, (1 + upper) * devices // 2, 2))
-        odd.sort(key=lambda t: reverse(t, bits))
-        chunks.append((odd, swapped(pick(odd), "row", 1)))
-    kept = [pick([t - 1 for t in odd]) for odd, _ in chunks]
+        )(*[arrays[k] for k in used], table)
+
+    order = sorted(range(1, devices, 2), key=lambda t: reverse(t, bits))
+    upper = [t for t in order if t >= devices // 2]
+    lower = [t for t in order if t < devices // 2]
+    chunks = [(upper, 0, per // 2), (upper, per // 2, per // 2), (lower, 0, per)]
+    arrived = []
+    for chunk in chunks:
+        sent = pick(*chunk)
+        arrived.append(swapped(sent, "row", 1))
     totals = []
-    for mine, (_, arrived) in zip(kept, chunks):
-        total = mine + arrived
+    for (odd, first, rows), other in zip(chunks, arrived):
+        total = pick([t - 1 for t in odd], first, rows) + other
         for level in range(1, bits - 1):
             middle = total.shape[0] // 2
-            total = total[:middle] + swapped(total[middle:], "row", 1 << level)
+            other = swapped(total[middle:], "row", 1 << level)
+            total = total[:middle] + other
         totals.append(total)
-    total = totals[0] + swapped(totals[1], "row", devices // 2)
-    col_bits = lax.axis_size("col").bit_length() - 1
-    stacked = total[None]
-    for level in reversed(range(col_bits)):
+    col_size = lax.axis_size("col")
+    col_bits = col_size.bit_length() - 1
+    own, other = [], []
+    for part in range(2):
+        mine = totals[2][part * per // 2 : (part + 1) * per // 2]
+        if part:
+            mine, own[0] = lax.optimization_barrier((mine, own[0]))
+        own.append(mine + swapped(totals[part], "row", devices // 2))
+        other.append(swapped(own[part], "col", col_size // 2))
+    stacked = jnp.stack([jnp.concatenate(own), jnp.concatenate(other)])
+    for level in reversed(range(col_bits - 1)):
         stacked = jnp.concatenate([stacked, swapped(stacked, "col", 1 << level)], axis=0)
     packed = [stacked[reverse(u, col_bits)] for u in range(group)]
     scale = 1.0 / (devices * row_count * count)

time: 64.5 us -> 61.5 us (0.953)
  starting transfers between devices: 26.8 us -> 23.9 us
  waiting for transfers between devices: 21.9 us -> 19.2 us
  Pallas kernels: 11.9 us -> 13.8 us
  other arithmetic: 0.75 us -> 1.46 us
    ppermute x18 -> x19, starting transfers between devices: 26.8 us -> 23.9 us  [swapped(): lax.ppermute(x, axis, [(i, i ^ distance) for i in range(lax.axis_size(axi...]
    ppermute x18 -> x19, waiting for transfers between devices: 21.9 us -> 19.2 us  [swapped(): lax.ppermute(x, axis, [(i, i ^ distance) for i in range(lax.axis_size(axi...]
    pallas_call x4 -> x6, Pallas kernels: 7.3 us -> 9.14 us  [pick(): pl.pallas_call(functools.partial(pick_kernel, width, slots, spots, count,...]
    concatenate x1, other arithmetic: 0.02 us -> 0.69 us  [body(): far = jnp.concatenate(listed)]
    unnamed x9 -> x10, local copies, waits for them, and re-layouts: 2.66 us -> 2.67 us
  transfers between devices with their start and end apart: 18 -> 19, of which waited for: 13 -> 14; matrix products, arithmetic and copies ran while one was open for 1% -> 1% of each run, Pallas kernels for 13% -> 18%
where the time goes in v2:
time: 61.5 us; the launch traced here: 61.3 us
  starting transfers between devices  23.9 us (39%)
  waiting for transfers between devices  19.2 us (31%)
  Pallas kernels  13.8 us (22%)
  local copies, waits for them, and re-layouts  2.73 us (4%)
  other arithmetic  1.46 us (2%)
    ppermute x19, starting transfers between devices, swapped(): lax.ppermute(x, axis, [(i, i ^ distance) for i in range(lax.axis_size(axi...  23.9 us
    ppermute x19, waiting for transfers between devices, swapped(): lax.ppermute(x, axis, [(i, i ^ distance) for i in range(lax.axis_size(axi...  19.2 us
    pallas_call x6, Pallas kernels, pick(): pl.pallas_call(functools.partial(pick_kernel, width, slots, spots, count,...  9.14 us
    unnamed x10, local copies, waits for them, and re-layouts  2.67 us
    pallas_call x1, Pallas kernels, transform_table(): pl.pallas_call(functools.partial(table_kernel, width), out_shape=jax.Shap...  2.59 us
    pallas_call x1, Pallas kernels, body(): pl.pallas_call(functools.partial(gram_kernel, width, count, devices, scal...  1.49 us
  transfers between devices with their start and end apart: 19, of which 14 were waited for; matrix products, arithmetic and copies ran while one was open for 1% of the time, Pallas kernels for 18%

profile of v2, /device:TPU:0, one launch (start us, length us, event | category | flops | bytes accessed | tf_op | source)
XLA Modules:
  0.0 61.3 jit_solution(18434595776874573651)
XLA Ops:
  0.0 3.1 %collective-permute-start = (s32[1024]{0:T(1024)}, s32[1024]{0:T(1024)S(1)}, u32[]{:S(2)}, u32[]{:S(2)}) collective-permute-start(s32[1024]{0:T(1024)} %refs_0_.1), channel_id=1, source_target_pairs={{0,8},{4,12},{8,0},{12,4},{16,24},{20,28},{24,16},{28,20},{1,9},{5... | collective-permute-start | bytes 12296 | tf_op jit(solution)/shard_map/ppermute | solution.py:16
  3.1 1.5 %collective-permute-start.1 = (s32[1024]{0:T(1024)}, s32[1024]{0:T(1024)S(1)}, u32[]{:S(2)}, u32[]{:S(2)}) collective-permute-start(s32[1024]{0:T(1024)} %refs_0_.1), channel_id=1, source_target_pairs={{0,4},{4,0},{8,12},{12,8},{16,20},{20,16},{24,28},{28,24},{1,5},{5... | collective-permute-start | bytes 12296 | tf_op jit(solution)/shard_map/ppermute | solution.py:16
  4.8 2.0 %collective-permute-done.1.refs_0_ = s32[1024]{0:T(1024)S(1)} collective-permute-done((s32[1024]{0:T(1024)}, s32[1024]{0:T(1024)S(1)}, u32[]{:S(2)}, u32[]{:S(2)}) %collective-permute-start.1) | collective-permute-done | bytes 4128 | tf_op jit(solution)/shard_map/ppermute | solution.py:16
  6.9 2.4 %collective-permute-done.2.refs_1_ = s32[1024]{0:T(1024)S(1)} collective-permute-done((s32[1024]{0:T(1024)}, s32[1024]{0:T(1024)S(1)}, u32[]{:S(2)}, u32[]{:S(2)}) %collective-permute-start.2) | collective-permute-done | bytes 4128 | tf_op jit(solution)/shard_map/ppermute | solution.py:16
  10.0 2.6 %collective-permute-start.5 = (s32[4096]{0:T(1024)S(1)}, s32[4096]{0:T(1024)S(1)}, u32[]{:S(2)}, u32[]{:S(2)}) collective-permute-start(s32[4096]{0:T(1024)S(1)} %pad_add_fusion), channel_id=1, source_target_pairs={{0,16},{4,20},{8,24},{12,28},{16,0},{20,4},{24,8},{28,12},{1,17},{... | collective-permute-start | bytes 49160 | tf_op jit(solution)/shard_map/ppermute | solution.py:16
  12.5 1.6 %copy-done = f32[32,16384]{1,0:T(8,128)S(1)} copy-done((f32[32,16384]{1,0:T(8,128)S(1)}, f32[32,16384]{1,0:T(8,128)}, u32[]{:S(2)}) %copy-start) | copy-done | bytes 2097176
  15.5 2.6 %table.1.refs_2_.refs_1_ = f32[16384,128]{1,0:T(8,128)S(1)} custom-call(f32[128,32,128]{2,1,0:T(8,128)S(1)} %rows.1.work_ref), custom_call_target="tpu_custom_call" | custom-call | tf_op jit(solution)/shard_map/table/pallas_call | solution.py:197
  18.1 1.4 %pick.9 = f32[256,128]{1,0:T(8,128)S(1)} custom-call(s32[4096]{0:T(1024)S(1)} %collective-permute-done.5.refs_0_, f32[16384,128]{1,0:T(8,128)S(1)} %table.1.refs_2_.refs_1_), custom_call_target="tpu_custom_call" | custom-call | tf_op jit(solution)/shard_map/pick/pallas_call | solution.py:239
  21.5 1.6 %collective-permute-start.9 = (f32[256,128]{1,0:T(8,128)S(1)}, f32[256,128]{1,0:T(8,128)S(1)}, u32[]{:S(2)}, u32[]{:S(2)}) collective-permute-start(f32[256,128]{1,0:T(8,128)S(1)} %pick.11), channel_id=1, source_target_pairs={{0,4},{4,0},{8,12},{12,8},{16,20},{20,16},{24,28},{28,24},{1,5},{5... | collective-permute-start | bytes 393224 | tf_op jit(solution)/shard_map/ppermute | solution.py:16
  23.1 1.4 %pick.8 = f32[256,128]{1,0:T(8,128)S(1)} custom-call(s32[4096]{0:T(1024)S(1)} %collective-permute-done.5.refs_0_, f32[16384,128]{1,0:T(8,128)S(1)} %table.1.refs_2_.refs_1_), custom_call_target="tpu_custom_call" | custom-call | tf_op jit(solution)/shard_map/pick/pallas_call | solution.py:239
  25.1 1.8 %pick.7 = f32[512,128]{1,0:T(8,128)S(1)} custom-call(s32[1024]{0:T(1024)S(1)} %collective-permute-done.1.refs_0_, s32[1024]{0:T(1024)S(1)} %collective-permute-done.2.refs_1_, f32[16384,128]{1,0:T(8,128)S(1)} %table.1.refs_2_.refs_1_), custom_call_target="tpu_custom_call" | custom-call | tf_op jit(solution)/shard_map/pick/pallas_call | solution.py:239
  27.0 1.5 %collective-permute-start.3 = (f32[512,128]{1,0:T(8,128)S(1)}, f32[512,128]{1,0:T(8,128)S(1)}, u32[]{:S(2)}, u32[]{:S(2)}) collective-permute-start(f32[512,128]{1,0:T(8,128)S(1)} %pick.7), channel_id=1, source_target_pairs={{0,4},{4,0},{8,12},{12,8},{16,20},{20,16},{24,28},{28,24},{1,5},{5... | collective-permute-start | bytes 786440 | tf_op jit(solution)/shard_map/ppermute | solution.py:16
  28.5 1.8 %pick.6 = f32[512,128]{1,0:T(8,128)S(1)} custom-call(s32[1024]{0:T(1024)S(1)} %copy-done.2, s32[1024]{0:T(1024)S(1)} %collective-permute-done.refs_1_, f32[16384,128]{1,0:T(8,128)S(1)} %table.1.refs_2_.refs_1_), custom_call_target="tpu_custom_call" | custom-call | tf_op jit(solution)/shard_map/pick/pallas_call | solution.py:239
  30.3 1.4 %pick.10 = f32[256,128]{1,0:T(8,128)S(1)} custom-call(s32[4096]{0:T(1024)S(1)} %collective-permute-done.5.refs_0_, f32[16384,128]{1,0:T(8,128)S(1)} %table.1.refs_2_.refs_1_), custom_call_target="tpu_custom_call" | custom-call | tf_op jit(solution)/shard_map/pick/pallas_call | solution.py:239
  31.8 1.6 %collective-permute-start.10 = (f32[128,128]{1,0:T(8,128)S(1)}, f32[128,128]{1,0:T(8,128)S(1)}, u32[]{:S(2)}, u32[]{:S(2)}) collective-permute-start(f32[128,128]{1,0:T(8,128)S(1)} %slice.75), channel_id=1, source_target_pairs={{0,8},{4,12},{8,0},{12,4},{16,24},{20,28},{24,16},{28,20},{1,9},{5... | collective-permute-start | bytes 196616 | tf_op jit(solution)/shard_map/ppermute | solution.py:16
  37.1 2.5 %collective-permute-done.4 = f32[256,128]{1,0:T(8,128)S(1)} collective-permute-done((f32[256,128]{1,0:T(8,128)S(1)}, f32[256,128]{1,0:T(8,128)S(1)}, u32[]{:S(2)}, u32[]{:S(2)}) %collective-permute-start.4) | collective-permute-done | bytes 131104 | tf_op jit(solution)/shard_map/ppermute | solution.py:16
  39.7 1.6 %collective-permute-start.12 = (f32[128,128]{1,0:T(8,128)S(1)}, f32[128,128]{1,0:T(8,128)S(1)}, u32[]{:S(2)}, u32[]{:S(2)}) collective-permute-start(f32[128,128]{1,0:T(8,128)S(1)} %get-tuple-element.7), channel_id=1, source_target_pairs={{0,2},{1,3},{2,0},{3,1},{4,6},{5,7},{6,4},{7,5},{8,10},{9,11},{10,... | collective-permute-start | bytes 196616 | tf_op jit(solution)/shard_map/ppermute | solution.py:16
  41.4 1.6 %collective-permute-start.13 = (f32[128,128]{1,0:T(8,128)S(1)}, f32[128,128]{1,0:T(8,128)S(1)}, u32[]{:S(2)}, u32[]{:S(2)}) collective-permute-start(f32[128,128]{1,0:T(8,128)S(1)} %add.43), channel_id=1, source_target_pairs={{0,2},{1,3},{2,0},{3,1},{4,6},{5,7},{6,4},{7,5},{8,10},{9,11},{10,... | collective-permute-start | bytes 196616 | tf_op jit(solution)/shard_map/ppermute | solution.py:16
  44.0 1.7 %collective-permute-done.13 = f32[128,128]{1,0:T(8,128)S(1)} collective-permute-done((f32[128,128]{1,0:T(8,128)S(1)}, f32[128,128]{1,0:T(8,128)S(1)}, u32[]{:S(2)}, u32[]{:S(2)}) %collective-permute-start.13) | collective-permute-done | bytes 65568 | tf_op jit(solution)/shard_map/ppermute | solution.py:16
  47.3 1.5 %gram.1 = f32[256,128]{1,0:T(8,128)S(1)} custom-call(s32[1024,1]{1,0:T(8,128)S(1)} %copy.5.owner_ref, f32[256,128]{1,0:T(8,128)S(1)} %get-tuple-element.16.refs_0_, f32[256,128]{1,0:T(8,128)S(1)} %get-tuple-element.10.refs_1_, f32[256,128]{1,0:T(8,128)S(1)} %constant_dynamic-update-slice_fusion.refs_2_, f32[256,128]{1,0:T(8,128)S(1)} %get-tuple-element.9.refs_3_), custom_call_target="tpu_custom_call" | custom-call | tf_op jit(solution)/shard_map/gram/pallas_call | solution.py:278
  48.8 2.0 %collective-permute-start.15 = (f32[2,32,128]{2,1,0:T(8,128)S(1)}, f32[2,32,128]{2,1,0:T(8,128)S(1)}, u32[]{:S(2)}, u32[]{:S(2)}) collective-permute-start(f32[2,32,128]{2,1,0:T(8,128)S(1)} %bitcast.17), channel_id=1, source_target_pairs={{0,4},{4,0},{8,12},{12,8},{16,20},{20,16},{24,28},{28,24},{1,5},{5... | collective-permute-start | bytes 98312 | tf_op jit(solution)/shard_map/ppermute | solution.py:16
  52.8 2.0 %collective-permute-done.16 = f32[2,32,128]{2,1,0:T(8,128)S(1)} collective-permute-done((f32[2,32,128]{2,1,0:T(8,128)S(1)}, f32[2,32,128]{2,1,0:T(8,128)S(1)}, u32[]{:S(2)}, u32[]{:S(2)}) %collective-permute-start.16) | collective-permute-done | bytes 32800 | tf_op jit(solution)/shard_map/ppermute | solution.py:16
  56.0 1.6 %collective-permute-start.18 = (f32[1,32,128]{2,1,0:T(8,128)S(1)}, f32[1,32,128]{2,1,0:T(8,128)S(1)}, u32[]{:S(2)}, u32[]{:S(2)}) collective-permute-start(f32[1,32,128]{2,1,0:T(8,128)S(1)} %slice.83), channel_id=1, source_target_pairs={{0,16},{4,20},{8,24},{12,28},{16,0},{20,4},{24,8},{28,12},{1,17},{... | collective-permute-start | bytes 49160 | tf_op jit(solution)/shard_map/ppermute | solution.py:16
  57.5 3.1 %collective-permute-done.18 = f32[1,32,128]{2,1,0:T(8,128)S(1)} collective-permute-done((f32[1,32,128]{2,1,0:T(8,128)S(1)}, f32[1,32,128]{2,1,0:T(8,128)S(1)}, u32[]{:S(2)}, u32[]{:S(2)}) %collective-permute-start.18) | collective-permute-done | bytes 16416 | tf_op jit(solution)/shard_map/ppermute | solution.py:16
  (53 shorter events, 15.2 us)
Async XLA Ops:
  0.0 4.8 %collective-permute-start = (s32[1024]{0:T(1024)}, s32[1024]{0:T(1024)S(1)}, u32[]{:S(2)}, u32[]{:S(2)}) collective-permute-start(s32[1024]{0:T(1024)} %refs_0_.1), channel_id=1, source_target_pairs={{0,8},{4,12},{8,0},{12,4},{16,24},{20,28},{24,16},{28,20},{1,9},{5... | collective-permute-start | bytes 12296 | tf_op jit(solution)/shard_map/ppermute | solution.py:16
  3.1 3.8 %collective-permute-start.1 = (s32[1024]{0:T(1024)}, s32[1024]{0:T(1024)S(1)}, u32[]{:S(2)}, u32[]{:S(2)}) collective-permute-start(s32[1024]{0:T(1024)} %refs_0_.1), channel_id=1, source_target_pairs={{0,4},{4,0},{8,12},{12,8},{16,20},{20,16},{24,28},{28,24},{1,5},{5... | collective-permute-start | bytes 12296 | tf_op jit(solution)/shard_map/ppermute | solution.py:16
  4.5 4.7 %collective-permute-start.2 = (s32[1024]{0:T(1024)}, s32[1024]{0:T(1024)S(1)}, u32[]{:S(2)}, u32[]{:S(2)}) collective-permute-start(s32[1024]{0:T(1024)} %refs_0_.1), channel_id=1, source_target_pairs={{0,12},{4,8},{8,4},{12,0},{16,28},{20,24},{24,20},{28,16},{1,13},{... | collective-permute-start | bytes 12296 | tf_op jit(solution)/shard_map/ppermute | solution.py:16
  10.0 8.2 %collective-permute-start.5 = (s32[4096]{0:T(1024)S(1)}, s32[4096]{0:T(1024)S(1)}, u32[]{:S(2)}, u32[]{:S(2)}) collective-permute-start(s32[4096]{0:T(1024)S(1)} %pad_add_fusion), channel_id=1, source_target_pairs={{0,16},{4,20},{8,24},{12,28},{16,0},{20,4},{24,8},{28,12},{1,17},{... | collective-permute-start | bytes 49160 | tf_op jit(solution)/shard_map/ppermute | solution.py:16
  12.5 1.6 %copy-start = (f32[32,16384]{1,0:T(8,128)S(1)}, f32[32,16384]{1,0:T(8,128)}, u32[]{:S(2)}) copy-start(f32[32,16384]{1,0:T(8,128)} %x_ref.1) | copy-start | bytes 6291460
  14.1 0.8 %copy-start.1 = (s32[16384]{0:T(1024)S(1)}, s32[16384]{0:T(1024)}, u32[]{:S(2)}) copy-start(s32[16384]{0:T(1024)} %param.5) | copy-start | bytes 196612
  19.5 5.0 %collective-permute-start.6 = (f32[256,128]{1,0:T(8,128)S(1)}, f32[256,128]{1,0:T(8,128)S(1)}, u32[]{:S(2)}, u32[]{:S(2)}) collective-permute-start(f32[256,128]{1,0:T(8,128)S(1)} %pick.9), channel_id=1, source_target_pairs={{0,4},{4,0},{8,12},{12,8},{16,20},{20,16},{24,28},{28,24},{1,5},{5... | collective-permute-start | bytes 393224 | tf_op jit(solution)/shard_map/ppermute | solution.py:16
  21.5 10.2 %collective-permute-start.9 = (f32[256,128]{1,0:T(8,128)S(1)}, f32[256,128]{1,0:T(8,128)S(1)}, u32[]{:S(2)}, u32[]{:S(2)}) collective-permute-start(f32[256,128]{1,0:T(8,128)S(1)} %pick.11), channel_id=1, source_target_pairs={{0,4},{4,0},{8,12},{12,8},{16,20},{20,16},{24,28},{28,24},{1,5},{5... | collective-permute-start | bytes 393224 | tf_op jit(solution)/shard_map/ppermute | solution.py:16
  24.6 3.9 %copy-start.2 = (s32[1024]{0:T(1024)S(1)}, s32[1024]{0:T(1024)}, u32[]{:S(2)}) copy-start(s32[1024]{0:T(1024)} %refs_0_.1) | copy-start | bytes 12292
  24.6 8.8 %collective-permute-start.7 = (f32[128,128]{1,0:T(8,128)S(1)}, f32[128,128]{1,0:T(8,128)S(1)}, u32[]{:S(2)}, u32[]{:S(2)}) collective-permute-start(f32[128,128]{1,0:T(8,128)S(1)} %slice.73), channel_id=1, source_target_pairs={{0,8},{4,12},{8,0},{12,4},{16,24},{20,28},{24,16},{28,20},{1,9},{5... | collective-permute-start | bytes 196616 | tf_op jit(solution)/shard_map/ppermute | solution.py:16
  27.0 6.9 %collective-permute-start.3 = (f32[512,128]{1,0:T(8,128)S(1)}, f32[512,128]{1,0:T(8,128)S(1)}, u32[]{:S(2)}, u32[]{:S(2)}) collective-permute-start(f32[512,128]{1,0:T(8,128)S(1)} %pick.7), channel_id=1, source_target_pairs={{0,4},{4,0},{8,12},{12,8},{16,20},{20,16},{24,28},{28,24},{1,5},{5... | collective-permute-start | bytes 786440 | tf_op jit(solution)/shard_map/ppermute | solution.py:16
  31.7 14.1 %copy-start.3 = (s32[1024,1]{0,1:T(1,128)S(1)}, s32[1024,1]{0,1:T(1,128)}, u32[]{:S(2)}) copy-start(s32[1024,1]{0,1:T(1,128)} %param.7) | copy-start | bytes 12292
  31.8 4.3 %collective-permute-start.10 = (f32[128,128]{1,0:T(8,128)S(1)}, f32[128,128]{1,0:T(8,128)S(1)}, u32[]{:S(2)}, u32[]{:S(2)}) collective-permute-start(f32[128,128]{1,0:T(8,128)S(1)} %slice.75), channel_id=1, source_target_pairs={{0,8},{4,12},{8,0},{12,4},{16,24},{20,28},{24,16},{28,20},{1,9},{5... | collective-permute-start | bytes 196616 | tf_op jit(solution)/shard_map/ppermute | solution.py:16
  33.4 6.2 %collective-permute-start.8 = (f32[128,128]{1,0:T(8,128)S(1)}, f32[128,128]{1,0:T(8,128)S(1)}, u32[]{:S(2)}, u32[]{:S(2)}) collective-permute-start(f32[128,128]{1,0:T(8,128)S(1)} %slice_add_fusion.2), channel_id=1, source_target_pairs={{0,16},{4,20},{8,24},{12,28},{16,0},{20,4},{24,8},{28,12},{1,17},{... | collective-permute-start | bytes 196616 | tf_op jit(solution)/shard_map/ppermute | solution.py:16
  33.9 5.7 %collective-permute-start.4 = (f32[256,128]{1,0:T(8,128)S(1)}, f32[256,128]{1,0:T(8,128)S(1)}, u32[]{:S(2)}, u32[]{:S(2)}) collective-permute-start(f32[256,128]{1,0:T(8,128)S(1)} %slice.69), channel_id=1, source_target_pairs={{0,8},{4,12},{8,0},{12,4},{16,24},{20,28},{24,16},{28,20},{1,9},{5... | collective-permute-start | bytes 393224 | tf_op jit(solution)/shard_map/ppermute | solution.py:16
  36.1 5.2 %collective-permute-start.11 = (f32[128,128]{1,0:T(8,128)S(1)}, f32[128,128]{1,0:T(8,128)S(1)}, u32[]{:S(2)}, u32[]{:S(2)}) collective-permute-start(f32[128,128]{1,0:T(8,128)S(1)} %slice_add_fusion.1), channel_id=1, source_target_pairs={{0,16},{4,20},{8,24},{12,28},{16,0},{20,4},{24,8},{28,12},{1,17},{... | collective-permute-start | bytes 196616 | tf_op jit(solution)/shard_map/ppermute | solution.py:16
  39.7 4.3 %collective-permute-start.12 = (f32[128,128]{1,0:T(8,128)S(1)}, f32[128,128]{1,0:T(8,128)S(1)}, u32[]{:S(2)}, u32[]{:S(2)}) collective-permute-start(f32[128,128]{1,0:T(8,128)S(1)} %get-tuple-element.7), channel_id=1, source_target_pairs={{0,2},{1,3},{2,0},{3,1},{4,6},{5,7},{6,4},{7,5},{8,10},{9,11},{10,... | collective-permute-start | bytes 196616 | tf_op jit(solution)/shard_map/ppermute | solution.py:16
  41.4 4.3 %collective-permute-start.13 = (f32[128,128]{1,0:T(8,128)S(1)}, f32[128,128]{1,0:T(8,128)S(1)}, u32[]{:S(2)}, u32[]{:S(2)}) collective-permute-start(f32[128,128]{1,0:T(8,128)S(1)} %add.43), channel_id=1, source_target_pairs={{0,2},{1,3},{2,0},{3,1},{4,6},{5,7},{6,4},{7,5},{8,10},{9,11},{10,... | collective-permute-start | bytes 196616 | tf_op jit(solution)/shard_map/ppermute | solution.py:16
  45.7 1.6 %collective-permute-start.14 = (f32[2,256,128]{2,1,0:T(8,128)S(1)}, f32[2,256,128]{2,1,0:T(8,128)S(1)}, u32[]{:S(2)}, u32[]{:S(2)}) collective-permute-start(f32[2,256,128]{2,1,0:T(8,128)S(1)} %pad_maximum_fusion), channel_id=1, source_target_pairs={{0,1},{1,0},{2,3},{3,2},{4,5},{5,4},{6,7},{7,6},{8,9},{9,8},{10,11... | collective-permute-start | bytes 786440 | tf_op jit(solution)/shard_map/ppermute | solution.py:16
  48.8 4.0 %collective-permute-start.15 = (f32[2,32,128]{2,1,0:T(8,128)S(1)}, f32[2,32,128]{2,1,0:T(8,128)S(1)}, u32[]{:S(2)}, u32[]{:S(2)}) collective-permute-start(f32[2,32,128]{2,1,0:T(8,128)S(1)} %bitcast.17), channel_id=1, source_target_pairs={{0,4},{4,0},{8,12},{12,8},{16,20},{20,16},{24,28},{28,24},{1,5},{5... | collective-permute-start | bytes 98312 | tf_op jit(solution)/shard_map/ppermute | solution.py:16
  50.9 4.0 %collective-permute-start.16 = (f32[2,32,128]{2,1,0:T(8,128)S(1)}, f32[2,32,128]{2,1,0:T(8,128)S(1)}, u32[]{:S(2)}, u32[]{:S(2)}) collective-permute-start(f32[2,32,128]{2,1,0:T(8,128)S(1)} %bitcast.16), channel_id=1, source_target_pairs={{0,8},{4,12},{8,0},{12,4},{16,24},{20,28},{24,16},{28,20},{1,9},{5... | collective-permute-start | bytes 98312 | tf_op jit(solution)/shard_map/ppermute | solution.py:16
  51.1 4.8 %collective-permute-start.17 = (f32[2,32,128]{2,1,0:T(8,128)S(1)}, f32[2,32,128]{2,1,0:T(8,128)S(1)}, u32[]{:S(2)}, u32[]{:S(2)}) collective-permute-start(f32[2,32,128]{2,1,0:T(8,128)S(1)} %bitcast.15), channel_id=1, source_target_pairs={{0,12},{4,8},{8,4},{12,0},{16,28},{20,24},{24,20},{28,16},{1,13},{... | collective-permute-start | bytes 98312 | tf_op jit(solution)/shard_map/ppermute | solution.py:16
  56.0 4.7 %collective-permute-start.18 = (f32[1,32,128]{2,1,0:T(8,128)S(1)}, f32[1,32,128]{2,1,0:T(8,128)S(1)}, u32[]{:S(2)}, u32[]{:S(2)}) collective-permute-start(f32[1,32,128]{2,1,0:T(8,128)S(1)} %slice.83), channel_id=1, source_target_pairs={{0,16},{4,20},{8,24},{12,28},{16,0},{20,4},{24,8},{28,12},{1,17},{... | collective-permute-start | bytes 49160 | tf_op jit(solution)/shard_map/ppermute | solution.py:16

commit v3 on v2

--- a/solution.py
+++ b/solution.py
@@ -101,8 +101,8 @@
     lax.fori_loop(0, 16, some, 0, unroll=4)
 
 
-def pick_kernel(width, slots, spots, count, first, rows, straight, *refs):
-    offset_refs, table_ref, out_ref = refs[:-2], refs[-2], refs[-1]
+def pick_kernel(width, pieces, count, straight, *refs):
+    offset_refs, table_ref, out_refs = refs[: -1 - len(pieces)], refs[-1 - len(pieces)], refs[-len(pieces) :]
     group = LANES // width
     per = count // group
     lane = lax.broadcasted_iota(jnp.int32, (8, LANES), 1) // width
@@ -110,32 +110,32 @@
     in_sub = [sub == s for s in range(8)]
     in_lane = [lane == g for g in range(group)]
     me = lax.axis_index("row")
-    for place, slot in enumerate(slots):
-        sign = (1 - 2 * parity(me & (me ^ slot))).astype(f32)
-        which, base = spots[place]
-
-        def block(inner):
-            total = None
-            for g in range(group):
-                part = None
-                for s in range(8):
-                    spot = offset_refs[which][inner + (base + first + g * per + s)]
-                    value = jnp.broadcast_to(table_ref[pl.ds(spot, 1), :], (8, LANES))
-                    part = value if part is None else jnp.where(in_sub[s], value, part)
-                total = part if total is None else jnp.where(in_lane[g], part, total)
-            return total * sign
-
-        if straight:
-            for inner in range(0, rows, 8):
-                out_ref[pl.ds(place * rows + inner, 8), :] = block(inner)
-        else:
-
-            def some(it, _):
-                inner = pl.multiple_of(it * 8, 8)
-                out_ref[pl.ds(place * rows + inner, 8), :] = block(inner)
-                return 0
-
-            lax.fori_loop(0, rows // 8, some, 0)
+    for out_ref, (slots, first, rows) in zip(out_refs, pieces):
+        for place, (slot, which, base) in enumerate(slots):
+            sign = (1 - 2 * parity(me & (me ^ slot))).astype(f32)
+
+            def block(inner):
+                total = None
+                for g in range(group):
+                    part = None
+                    for s in range(8):
+                        spot = offset_refs[which][inner + (base + first + g * per + s)]
+                        value = jnp.broadcast_to(table_ref[pl.ds(spot, 1), :], (8, LANES))
+                        part = value if part is None else jnp.where(in_sub[s], value, part)
+                    total = part if total is None else jnp.where(in_lane[g], part, total)
+                return total * sign
+
+            if straight:
+                for inner in range(0, rows, 8):
+                    out_ref[pl.ds(place * rows + inner, 8), :] = block(inner)
+            else:
+
+                def some(it, _):
+                    inner = pl.multiple_of(it * 8, 8)
+                    out_ref[pl.ds(place * rows + inner, 8), :] = block(inner)
+                    return 0
+
+                lax.fori_loop(0, rows // 8, some, 0)
 
 
 def gram_kernel(width, count, named, scale, owner_ref, *refs):
@@ -232,34 +232,44 @@
             entries += [(len(arrays) - 1, t * count) for t in range(1 << level)]
     table = transform_table(work, width)
 
-    def pick(slots, first, rows):
-        used = sorted({entries[t][0] for t in slots})
-        spots = [(used.index(entries[t][0]), entries[t][1]) for t in slots]
-        straight = len(slots) * rows * group <= 4096
+    def pick(*pieces):
+        used = sorted({entries[t][0] for slots, _, _ in pieces for t in slots})
+        full = [
+            ([(t, used.index(entries[t][0]), entries[t][1]) for t in slots], first, rows)
+            for slots, first, rows in pieces
+        ]
+        straight = sum(len(slots) * rows for slots, _, rows in pieces) * group <= 4096
         return pl.pallas_call(
-            functools.partial(pick_kernel, width, slots, spots, count, first, rows, straight),
-            out_shape=jax.ShapeDtypeStruct((len(slots) * rows, LANES), f32),
+            functools.partial(pick_kernel, width, full, count, straight),
+            out_shape=[jax.ShapeDtypeStruct((len(slots) * rows, LANES), f32) for slots, _, rows in pieces],
             in_specs=[SMEM] * len(used) + [VMEM],
-            out_specs=VMEM,
+            out_specs=[VMEM] * len(pieces),
             compiler_params=PARAMS,
             name="pick",
         )(*[arrays[k] for k in used], table)
 
-    order = sorted(range(1, devices, 2), key=lambda t: reverse(t, bits))
-    upper = [t for t in order if t >= devices // 2]
-    lower = [t for t in order if t < devices // 2]
-    chunks = [(upper, 0, per // 2), (upper, per // 2, per // 2), (lower, 0, per)]
-    arrived = []
-    for chunk in chunks:
-        sent = pick(*chunk)
-        arrived.append(swapped(sent, "row", 1))
+    def split(slots, levels):
+        slots = sorted(slots, key=lambda t: [t >> level & 1 for level in levels])
+        return slots[: len(slots) // 2], slots[len(slots) // 2 :]
+
+    levels = list(range(bits - 1))
+    turned = [1, 0] + levels[2:] if bits > 2 else levels
+    half = per // 2
+    keep_up, send_up = split(range(devices // 2, devices), levels)
+    keep_low, send_low = split(range(devices // 2), turned)
+    sent, kept = [None] * 3, [None] * 3
+    sent[0], kept[0] = pick((send_up, 0, half), (keep_up, 0, half))
+    sent[1], sent[2], kept[1] = pick((send_up, half, half), (send_low, 0, per), (keep_up, half, half))
+    (kept[2],) = pick((keep_low, 0, per))
     totals = []
-    for (odd, first, rows), other in zip(chunks, arrived):
-        total = pick([t - 1 for t in odd], first, rows) + other
-        for level in range(1, bits - 1):
-            middle = total.shape[0] // 2
-            other = swapped(total[middle:], "row", 1 << level)
-            total = total[:middle] + other
+    for k, order in enumerate((levels, levels, turned)):
+        total, out = kept[k], sent[k]
+        for step, level in enumerate(order):
+            if step:
+                middle = total.shape[0] // 2
+                total, out = total[:middle], total[middle:]
+            other = swapped(out, "row", 1 << level)
+            total = total + other
         totals.append(total)
     col_size = lax.axis_size("col")
     col_bits = col_size.bit_length() - 1
@@ -295,6 +305,4 @@
 
 def solution(mesh):
     placed = (P("col", "row"), P("row"), P("row"), P("row", None))
-    return jax.shard_map(
-        body, mesh=mesh, in_specs=placed, out_specs=P("row", "col", None), check_vma=False
-    )
+    return jax.shard_map(body, mesh=mesh, in_specs=placed, out_specs=P("row", "col", None), check_vma=False)

time: 61.5 us -> 61.1 us (level)
  waiting for transfers between devices: 19.2 us -> 25.3 us
  starting transfers between devices: 23.9 us -> 19.6 us
  Pallas kernels: 13.8 us -> 11.7 us
    ppermute x19, waiting for transfers between devices: 19.2 us -> 25.3 us  [swapped(): lax.ppermute(x, axis, [(i, i ^ distance) for i in range(lax.axis_size(axi...]
    ppermute x19, starting transfers between devices: 23.9 us -> 19.6 us  [swapped(): lax.ppermute(x, axis, [(i, i ^ distance) for i in range(lax.axis_size(axi...]
    pallas_call x6 -> x3, Pallas kernels: 9.14 us -> 7.03 us  [pick(): pl.pallas_call(functools.partial(pick_kernel, width, full, count, straigh...]
  transfers between devices with their start and end apart: 19 -> 19, of which waited for: 14 -> 15; matrix products, arithmetic and copies ran while one was open for 1% -> 1% of each run, Pallas kernels for 18% -> 14%
where the time goes in v3:
time: 61.1 us; the launch traced here: 60.9 us
  waiting for transfers between devices  25.3 us (41%)
  starting transfers between devices  19.6 us (32%)
  Pallas kernels  11.7 us (19%)
  local copies, waits for them, and re-layouts  2.73 us (4%)
  other arithmetic  1.47 us (2%)
    ppermute x19, waiting for transfers between devices, swapped(): lax.ppermute(x, axis, [(i, i ^ distance) for i in range(lax.axis_size(axi...  25.3 us
    ppermute x19, starting transfers between devices, swapped(): lax.ppermute(x, axis, [(i, i ^ distance) for i in range(lax.axis_size(axi...  19.6 us
    pallas_call x3, Pallas kernels, pick(): pl.pallas_call(functools.partial(pick_kernel, width, full, count, straigh...  7.03 us
    unnamed x10, local copies, waits for them, and re-layouts  2.67 us
    pallas_call x1, Pallas kernels, transform_table(): pl.pallas_call(functools.partial(table_kernel, width), out_shape=jax.Shap...  2.59 us
    pallas_call x1, Pallas kernels, body(): pl.pallas_call(functools.partial(gram_kernel, width, count, devices, scal...  1.49 us
  transfers between devices with their start and end apart: 19, of which 15 were waited for; matrix products, arithmetic and copies ran while one was open for 1% of the time, Pallas kernels for 14%

profile of v3, /device:TPU:0, one launch (start us, length us, event | category | flops | bytes accessed | tf_op | source)
XLA Modules:
  0.0 60.9 jit_solution(8633734972652889594)
XLA Ops:
  0.0 3.0 %collective-permute-start = (s32[1024]{0:T(1024)}, s32[1024]{0:T(1024)S(1)}, u32[]{:S(2)}, u32[]{:S(2)}) collective-permute-start(s32[1024]{0:T(1024)} %refs_0_.1), channel_id=1, source_target_pairs={{0,4},{4,0},{8,12},{12,8},{16,20},{20,16},{24,28},{28,24},{1,5},{5... | collective-permute-start | bytes 12296 | tf_op jit(solution)/shard_map/ppermute | solution.py:16
  3.0 1.6 %collective-permute-start.1 = (s32[1024]{0:T(1024)}, s32[1024]{0:T(1024)S(1)}, u32[]{:S(2)}, u32[]{:S(2)}) collective-permute-start(s32[1024]{0:T(1024)} %refs_0_.1), channel_id=1, source_target_pairs={{0,8},{4,12},{8,0},{12,4},{16,24},{20,28},{24,16},{28,20},{1,9},{5... | collective-permute-start | bytes 12296 | tf_op jit(solution)/shard_map/ppermute | solution.py:16
  4.8 2.0 %collective-permute-done.1.refs_0_ = s32[1024]{0:T(1024)S(1)} collective-permute-done((s32[1024]{0:T(1024)}, s32[1024]{0:T(1024)S(1)}, u32[]{:S(2)}, u32[]{:S(2)}) %collective-permute-start.1) | collective-permute-done | bytes 4128 | tf_op jit(solution)/shard_map/ppermute | solution.py:16
  6.8 2.5 %collective-permute-done.2.refs_1_ = s32[1024]{0:T(1024)S(1)} collective-permute-done((s32[1024]{0:T(1024)}, s32[1024]{0:T(1024)S(1)}, u32[]{:S(2)}, u32[]{:S(2)}) %collective-permute-start.2) | collective-permute-done | bytes 4128 | tf_op jit(solution)/shard_map/ppermute | solution.py:16
  10.0 2.6 %collective-permute-start.3 = (s32[4096]{0:T(1024)S(1)}, s32[4096]{0:T(1024)S(1)}, u32[]{:S(2)}, u32[]{:S(2)}) collective-permute-start(s32[4096]{0:T(1024)S(1)} %pad_add_fusion), channel_id=1, source_target_pairs={{0,16},{4,20},{8,24},{12,28},{16,0},{20,4},{24,8},{28,12},{1,17},{... | collective-permute-start | bytes 49160 | tf_op jit(solution)/shard_map/ppermute | solution.py:16
  12.5 1.6 %copy-done = f32[32,16384]{1,0:T(8,128)S(1)} copy-done((f32[32,16384]{1,0:T(8,128)S(1)}, f32[32,16384]{1,0:T(8,128)}, u32[]{:S(2)}) %copy-start) | copy-done | bytes 2097176
  15.5 2.6 %table.1.refs_2_.refs_3_.refs_1_ = f32[16384,128]{1,0:T(8,128)S(1)} custom-call(f32[128,32,128]{2,1,0:T(8,128)S(1)} %rows.1.work_ref), custom_call_target="tpu_custom_call" | custom-call | tf_op jit(solution)/shard_map/table/pallas_call | solution.py:197
  18.1 1.9 %pick.5 = (f32[256,128]{1,0:T(8,128)S(1)}, f32[256,128]{1,0:T(8,128)S(1)}) custom-call(s32[4096]{0:T(1024)S(1)} %collective-permute-done.3.refs_2_.refs_0_, f32[16384,128]{1,0:T(8,128)S(1)} %table.1.refs_2_.refs_3_.refs_1_), custom_call_target="tpu_custom_call" | custom-call | tf_op jit(solution)/shard_map/pick/pallas_call | solution.py:242
  20.7 3.3 %pick.4 = (f32[256,128]{1,0:T(8,128)S(1)}, f32[512,128]{1,0:T(8,128)S(1)}, f32[256,128]{1,0:T(8,128)S(1)}) custom-call(s32[1024]{0:T(1024)S(1)} %collective-permute-done.1.refs_0_, s32[1024]{0:T(1024)S(1)} %collective-permute-done.2.refs_1_, s32[4096]{0:T(1024)S(1)} %collective-permute-done.3.refs_2_.refs_0_, f32[16384,128]{1,0:T(8,128)S(1)} %table.1.refs_2_.refs_3_.refs_1_), custom_call_target="tpu_custom_call" | custom-call | tf_op jit(solution)/shard_map/pick/pallas_call | solution.py:242
  24.0 1.6 %collective-permute-start.9 = (f32[256,128]{1,0:T(8,128)S(1)}, f32[256,128]{1,0:T(8,128)S(1)}, u32[]{:S(2)}, u32[]{:S(2)}) collective-permute-start(f32[256,128]{1,0:T(8,128)S(1)} %get-tuple-element.18), channel_id=1, source_target_pairs={{0,4},{4,0},{8,12},{12,8},{16,20},{20,16},{24,28},{28,24},{1,5},{5... | collective-permute-start | bytes 393224 | tf_op jit(solution)/shard_map/ppermute | solution.py:16
  26.6 1.6 %collective-permute-start.4 = (f32[512,128]{1,0:T(8,128)S(1)}, f32[512,128]{1,0:T(8,128)S(1)}, u32[]{:S(2)}, u32[]{:S(2)}) collective-permute-start(f32[512,128]{1,0:T(8,128)S(1)} %get-tuple-element.12), channel_id=1, source_target_pairs={{0,8},{4,12},{8,0},{12,4},{16,24},{20,28},{24,16},{28,20},{1,9},{5... | collective-permute-start | bytes 786440 | tf_op jit(solution)/shard_map/ppermute | solution.py:16
  28.2 1.8 %pick.3 = f32[512,128]{1,0:T(8,128)S(1)} custom-call(s32[1024]{0:T(1024)S(1)} %copy-done.2, s32[1024]{0:T(1024)S(1)} %collective-permute-done.refs_1_, f32[16384,128]{1,0:T(8,128)S(1)} %table.1.refs_2_.refs_3_.refs_1_), custom_call_target="tpu_custom_call" | custom-call | tf_op jit(solution)/shard_map/pick/pallas_call | solution.py:242
  31.2 3.4 %collective-permute-done.4 = f32[512,128]{1,0:T(8,128)S(1)} collective-permute-done((f32[512,128]{1,0:T(8,128)S(1)}, f32[512,128]{1,0:T(8,128)S(1)}, u32[]{:S(2)}, u32[]{:S(2)}) %collective-permute-start.4) | collective-permute-done | bytes 262176 | tf_op jit(solution)/shard_map/ppermute | solution.py:16
  35.4 4.3 %collective-permute-done.5 = f32[256,128]{1,0:T(8,128)S(1)} collective-permute-done((f32[256,128]{1,0:T(8,128)S(1)}, f32[256,128]{1,0:T(8,128)S(1)}, u32[]{:S(2)}, u32[]{:S(2)}) %collective-permute-start.5) | collective-permute-done | bytes 131104 | tf_op jit(solution)/shard_map/ppermute | solution.py:16
  39.8 1.6 %collective-permute-start.12 = (f32[128,128]{1,0:T(8,128)S(1)}, f32[128,128]{1,0:T(8,128)S(1)}, u32[]{:S(2)}, u32[]{:S(2)}) collective-permute-start(f32[128,128]{1,0:T(8,128)S(1)} %get-tuple-element.15), channel_id=1, source_target_pairs={{0,2},{1,3},{2,0},{3,1},{4,6},{5,7},{6,4},{7,5},{8,10},{9,11},{10,... | collective-permute-start | bytes 196616 | tf_op jit(solution)/shard_map/ppermute | solution.py:16
  41.4 1.5 %collective-permute-start.13 = (f32[128,128]{1,0:T(8,128)S(1)}, f32[128,128]{1,0:T(8,128)S(1)}, u32[]{:S(2)}, u32[]{:S(2)}) collective-permute-start(f32[128,128]{1,0:T(8,128)S(1)} %add.43), channel_id=1, source_target_pairs={{0,2},{1,3},{2,0},{3,1},{4,6},{5,7},{6,4},{7,5},{8,10},{9,11},{10,... | collective-permute-start | bytes 196616 | tf_op jit(solution)/shard_map/ppermute | solution.py:16
  44.1 1.6 %collective-permute-done.13 = f32[128,128]{1,0:T(8,128)S(1)} collective-permute-done((f32[128,128]{1,0:T(8,128)S(1)}, f32[128,128]{1,0:T(8,128)S(1)}, u32[]{:S(2)}, u32[]{:S(2)}) %collective-permute-start.13) | collective-permute-done | bytes 65568 | tf_op jit(solution)/shard_map/ppermute | solution.py:16
  46.1 1.3 %collective-permute-done.14 = f32[2,256,128]{2,1,0:T(8,128)S(1)} collective-permute-done((f32[2,256,128]{2,1,0:T(8,128)S(1)}, f32[2,256,128]{2,1,0:T(8,128)S(1)}, u32[]{:S(2)}, u32[]{:S(2)}) %collective-permute-start.14) | collective-permute-done | bytes 262176 | tf_op jit(solution)/shard_map/ppermute | solution.py:16
  47.4 1.5 %gram.1 = f32[256,128]{1,0:T(8,128)S(1)} custom-call(s32[1024,1]{1,0:T(8,128)S(1)} %copy.5.owner_ref, f32[256,128]{1,0:T(8,128)S(1)} %get-tuple-element.26.refs_0_, f32[256,128]{1,0:T(8,128)S(1)} %get-tuple-element.20.refs_1_, f32[256,128]{1,0:T(8,128)S(1)} %constant_dynamic-update-slice_fusion.refs_2_, f32[256,128]{1,0:T(8,128)S(1)} %get-tuple-element.19.refs_3_), custom_call_target="tpu_custom_call" | custom-call | tf_op jit(solution)/shard_map/gram/pallas_call | solution.py:288
  48.9 1.4 %collective-permute-start.15 = (f32[2,32,128]{2,1,0:T(8,128)S(1)}, f32[2,32,128]{2,1,0:T(8,128)S(1)}, u32[]{:S(2)}, u32[]{:S(2)}) collective-permute-start(f32[2,32,128]{2,1,0:T(8,128)S(1)} %bitcast.17), channel_id=1, source_target_pairs={{0,4},{4,0},{8,12},{12,8},{16,20},{20,16},{24,28},{28,24},{1,5},{5... | collective-permute-start | bytes 98312 | tf_op jit(solution)/shard_map/ppermute | solution.py:16
  50.8 1.7 %collective-permute-start.17 = (f32[2,32,128]{2,1,0:T(8,128)S(1)}, f32[2,32,128]{2,1,0:T(8,128)S(1)}, u32[]{:S(2)}, u32[]{:S(2)}) collective-permute-start(f32[2,32,128]{2,1,0:T(8,128)S(1)} %bitcast.15), channel_id=1, source_target_pairs={{0,12},{4,8},{8,4},{12,0},{16,28},{20,24},{24,20},{28,16},{1,13},{... | collective-permute-start | bytes 98312 | tf_op jit(solution)/shard_map/ppermute | solution.py:16
  52.9 1.5 %collective-permute-done.16 = f32[2,32,128]{2,1,0:T(8,128)S(1)} collective-permute-done((f32[2,32,128]{2,1,0:T(8,128)S(1)}, f32[2,32,128]{2,1,0:T(8,128)S(1)}, u32[]{:S(2)}, u32[]{:S(2)}) %collective-permute-start.16) | collective-permute-done | bytes 32800 | tf_op jit(solution)/shard_map/ppermute | solution.py:16
  54.3 1.2 %collective-permute-done.17 = f32[2,32,128]{2,1,0:T(8,128)S(1)} collective-permute-done((f32[2,32,128]{2,1,0:T(8,128)S(1)}, f32[2,32,128]{2,1,0:T(8,128)S(1)}, u32[]{:S(2)}, u32[]{:S(2)}) %collective-permute-start.17) | collective-permute-done | bytes 32800 | tf_op jit(solution)/shard_map/ppermute | solution.py:16
  56.3 4.0 %collective-permute-done.18 = f32[1,32,128]{2,1,0:T(8,128)S(1)} collective-permute-done((f32[1,32,128]{2,1,0:T(8,128)S(1)}, f32[1,32,128]{2,1,0:T(8,128)S(1)}, u32[]{:S(2)}, u32[]{:S(2)}) %collective-permute-start.18) | collective-permute-done | bytes 16416 | tf_op jit(solution)/shard_map/ppermute | solution.py:16
  (50 shorter events, 9.7 us)
Async XLA Ops:
  0.0 4.8 %collective-permute-start = (s32[1024]{0:T(1024)}, s32[1024]{0:T(1024)S(1)}, u32[]{:S(2)}, u32[]{:S(2)}) collective-permute-start(s32[1024]{0:T(1024)} %refs_0_.1), channel_id=1, source_target_pairs={{0,4},{4,0},{8,12},{12,8},{16,20},{20,16},{24,28},{28,24},{1,5},{5... | collective-permute-start | bytes 12296 | tf_op jit(solution)/shard_map/ppermute | solution.py:16
  3.0 3.8 %collective-permute-start.1 = (s32[1024]{0:T(1024)}, s32[1024]{0:T(1024)S(1)}, u32[]{:S(2)}, u32[]{:S(2)}) collective-permute-start(s32[1024]{0:T(1024)} %refs_0_.1), channel_id=1, source_target_pairs={{0,8},{4,12},{8,0},{12,4},{16,24},{20,28},{24,16},{28,20},{1,9},{5... | collective-permute-start | bytes 12296 | tf_op jit(solution)/shard_map/ppermute | solution.py:16
  4.5 4.7 %collective-permute-start.2 = (s32[1024]{0:T(1024)}, s32[1024]{0:T(1024)S(1)}, u32[]{:S(2)}, u32[]{:S(2)}) collective-permute-start(s32[1024]{0:T(1024)} %refs_0_.1), channel_id=1, source_target_pairs={{0,12},{4,8},{8,4},{12,0},{16,28},{20,24},{24,20},{28,16},{1,13},{... | collective-permute-start | bytes 12296 | tf_op jit(solution)/shard_map/ppermute | solution.py:16
  10.0 8.2 %collective-permute-start.3 = (s32[4096]{0:T(1024)S(1)}, s32[4096]{0:T(1024)S(1)}, u32[]{:S(2)}, u32[]{:S(2)}) collective-permute-start(s32[4096]{0:T(1024)S(1)} %pad_add_fusion), channel_id=1, source_target_pairs={{0,16},{4,20},{8,24},{12,28},{16,0},{20,4},{24,8},{28,12},{1,17},{... | collective-permute-start | bytes 49160 | tf_op jit(solution)/shard_map/ppermute | solution.py:16
  12.5 1.6 %copy-start = (f32[32,16384]{1,0:T(8,128)S(1)}, f32[32,16384]{1,0:T(8,128)}, u32[]{:S(2)}) copy-start(f32[32,16384]{1,0:T(8,128)} %x_ref.1) | copy-start | bytes 6291460
  14.1 0.8 %copy-start.1 = (s32[16384]{0:T(1024)S(1)}, s32[16384]{0:T(1024)}, u32[]{:S(2)}) copy-start(s32[16384]{0:T(1024)} %param.5) | copy-start | bytes 196612
  20.1 8.1 %copy-start.2 = (s32[1024]{0:T(1024)S(1)}, s32[1024]{0:T(1024)}, u32[]{:S(2)}) copy-start(s32[1024]{0:T(1024)} %refs_0_.1) | copy-start | bytes 12292
  20.1 5.9 %collective-permute-start.6 = (f32[256,128]{1,0:T(8,128)S(1)}, f32[256,128]{1,0:T(8,128)S(1)}, u32[]{:S(2)}, u32[]{:S(2)}) collective-permute-start(f32[256,128]{1,0:T(8,128)S(1)} %get-tuple-element.14), channel_id=1, source_target_pairs={{0,4},{4,0},{8,12},{12,8},{16,20},{20,16},{24,28},{28,24},{1,5},{5... | collective-permute-start | bytes 393224 | tf_op jit(solution)/shard_map/ppermute | solution.py:16
  24.0 6.0 %collective-permute-start.9 = (f32[256,128]{1,0:T(8,128)S(1)}, f32[256,128]{1,0:T(8,128)S(1)}, u32[]{:S(2)}, u32[]{:S(2)}) collective-permute-start(f32[256,128]{1,0:T(8,128)S(1)} %get-tuple-element.18), channel_id=1, source_target_pairs={{0,4},{4,0},{8,12},{12,8},{16,20},{20,16},{24,28},{28,24},{1,5},{5... | collective-permute-start | bytes 393224 | tf_op jit(solution)/shard_map/ppermute | solution.py:16
  26.1 5.1 %collective-permute-start.7 = (f32[128,128]{1,0:T(8,128)S(1)}, f32[128,128]{1,0:T(8,128)S(1)}, u32[]{:S(2)}, u32[]{:S(2)}) collective-permute-start(f32[128,128]{1,0:T(8,128)S(1)} %slice.73), channel_id=1, source_target_pairs={{0,8},{4,12},{8,0},{12,4},{16,24},{20,28},{24,16},{28,20},{1,9},{5... | collective-permute-start | bytes 196616 | tf_op jit(solution)/shard_map/ppermute | solution.py:16
  26.6 8.1 %collective-permute-start.4 = (f32[512,128]{1,0:T(8,128)S(1)}, f32[512,128]{1,0:T(8,128)S(1)}, u32[]{:S(2)}, u32[]{:S(2)}) collective-permute-start(f32[512,128]{1,0:T(8,128)S(1)} %get-tuple-element.12), channel_id=1, source_target_pairs={{0,8},{4,12},{8,0},{12,4},{16,24},{20,28},{24,16},{28,20},{1,9},{5... | collective-permute-start | bytes 786440 | tf_op jit(solution)/shard_map/ppermute | solution.py:16
  30.0 15.8 %copy-start.3 = (s32[1024,1]{0,1:T(1,128)S(1)}, s32[1024,1]{0,1:T(1,128)}, u32[]{:S(2)}) copy-start(s32[1024,1]{0,1:T(1,128)} %param.7) | copy-start | bytes 12292
  30.1 5.3 %collective-permute-start.10 = (f32[128,128]{1,0:T(8,128)S(1)}, f32[128,128]{1,0:T(8,128)S(1)}, u32[]{:S(2)}, u32[]{:S(2)}) collective-permute-start(f32[128,128]{1,0:T(8,128)S(1)} %slice.75), channel_id=1, source_target_pairs={{0,8},{4,12},{8,0},{12,4},{16,24},{20,28},{24,16},{28,20},{1,9},{5... | collective-permute-start | bytes 196616 | tf_op jit(solution)/shard_map/ppermute | solution.py:16
  31.2 8.6 %collective-permute-start.8 = (f32[128,128]{1,0:T(8,128)S(1)}, f32[128,128]{1,0:T(8,128)S(1)}, u32[]{:S(2)}, u32[]{:S(2)}) collective-permute-start(f32[128,128]{1,0:T(8,128)S(1)} %slice_add_fusion.2), channel_id=1, source_target_pairs={{0,16},{4,20},{8,24},{12,28},{16,0},{20,4},{24,8},{28,12},{1,17},{... | collective-permute-start | bytes 196616 | tf_op jit(solution)/shard_map/ppermute | solution.py:16
  34.7 5.0 %collective-permute-start.5 = (f32[256,128]{1,0:T(8,128)S(1)}, f32[256,128]{1,0:T(8,128)S(1)}, u32[]{:S(2)}, u32[]{:S(2)}) collective-permute-start(f32[256,128]{1,0:T(8,128)S(1)} %slice.69), channel_id=1, source_target_pairs={{0,4},{4,0},{8,12},{12,8},{16,20},{20,16},{24,28},{28,24},{1,5},{5... | collective-permute-start | bytes 393224 | tf_op jit(solution)/shard_map/ppermute | solution.py:16
  35.4 6.0 %collective-permute-start.11 = (f32[128,128]{1,0:T(8,128)S(1)}, f32[128,128]{1,0:T(8,128)S(1)}, u32[]{:S(2)}, u32[]{:S(2)}) collective-permute-start(f32[128,128]{1,0:T(8,128)S(1)} %slice_add_fusion.1), channel_id=1, source_target_pairs={{0,16},{4,20},{8,24},{12,28},{16,0},{20,4},{24,8},{28,12},{1,17},{... | collective-permute-start | bytes 196616 | tf_op jit(solution)/shard_map/ppermute | solution.py:16
  39.8 4.3 %collective-permute-start.12 = (f32[128,128]{1,0:T(8,128)S(1)}, f32[128,128]{1,0:T(8,128)S(1)}, u32[]{:S(2)}, u32[]{:S(2)}) collective-permute-start(f32[128,128]{1,0:T(8,128)S(1)} %get-tuple-element.15), channel_id=1, source_target_pairs={{0,2},{1,3},{2,0},{3,1},{4,6},{5,7},{6,4},{7,5},{8,10},{9,11},{10,... | collective-permute-start | bytes 196616 | tf_op jit(solution)/shard_map/ppermute | solution.py:16
  41.4 4.3 %collective-permute-start.13 = (f32[128,128]{1,0:T(8,128)S(1)}, f32[128,128]{1,0:T(8,128)S(1)}, u32[]{:S(2)}, u32[]{:S(2)}) collective-permute-start(f32[128,128]{1,0:T(8,128)S(1)} %add.43), channel_id=1, source_target_pairs={{0,2},{1,3},{2,0},{3,1},{4,6},{5,7},{6,4},{7,5},{8,10},{9,11},{10,... | collective-permute-start | bytes 196616 | tf_op jit(solution)/shard_map/ppermute | solution.py:16
  45.8 1.6 %collective-permute-start.14 = (f32[2,256,128]{2,1,0:T(8,128)S(1)}, f32[2,256,128]{2,1,0:T(8,128)S(1)}, u32[]{:S(2)}, u32[]{:S(2)}) collective-permute-start(f32[2,256,128]{2,1,0:T(8,128)S(1)} %pad_maximum_fusion), channel_id=1, source_target_pairs={{0,1},{1,0},{2,3},{3,2},{4,5},{5,4},{6,7},{7,6},{8,9},{9,8},{10,11... | collective-permute-start | bytes 786440 | tf_op jit(solution)/shard_map/ppermute | solution.py:16
  48.9 4.0 %collective-permute-start.15 = (f32[2,32,128]{2,1,0:T(8,128)S(1)}, f32[2,32,128]{2,1,0:T(8,128)S(1)}, u32[]{:S(2)}, u32[]{:S(2)}) collective-permute-start(f32[2,32,128]{2,1,0:T(8,128)S(1)} %bitcast.17), channel_id=1, source_target_pairs={{0,4},{4,0},{8,12},{12,8},{16,20},{20,16},{24,28},{28,24},{1,5},{5... | collective-permute-start | bytes 98312 | tf_op jit(solution)/shard_map/ppermute | solution.py:16
  50.3 4.0 %collective-permute-start.16 = (f32[2,32,128]{2,1,0:T(8,128)S(1)}, f32[2,32,128]{2,1,0:T(8,128)S(1)}, u32[]{:S(2)}, u32[]{:S(2)}) collective-permute-start(f32[2,32,128]{2,1,0:T(8,128)S(1)} %bitcast.16), channel_id=1, source_target_pairs={{0,8},{4,12},{8,0},{12,4},{16,24},{20,28},{24,16},{28,20},{1,9},{5... | collective-permute-start | bytes 98312 | tf_op jit(solution)/shard_map/ppermute | solution.py:16
  50.8 4.8 %collective-permute-start.17 = (f32[2,32,128]{2,1,0:T(8,128)S(1)}, f32[2,32,128]{2,1,0:T(8,128)S(1)}, u32[]{:S(2)}, u32[]{:S(2)}) collective-permute-start(f32[2,32,128]{2,1,0:T(8,128)S(1)} %bitcast.15), channel_id=1, source_target_pairs={{0,12},{4,8},{8,4},{12,0},{16,28},{20,24},{24,20},{28,16},{1,13},{... | collective-permute-start | bytes 98312 | tf_op jit(solution)/shard_map/ppermute | solution.py:16
  55.6 4.7 %collective-permute-start.18 = (f32[1,32,128]{2,1,0:T(8,128)S(1)}, f32[1,32,128]{2,1,0:T(8,128)S(1)}, u32[]{:S(2)}, u32[]{:S(2)}) collective-permute-start(f32[1,32,128]{2,1,0:T(8,128)S(1)} %slice.83), channel_id=1, source_target_pairs={{0,16},{4,20},{8,24},{12,28},{16,0},{20,4},{24,8},{28,12},{1,17},{... | collective-permute-start | bytes 49160 | tf_op jit(solution)/shard_map/ppermute | solution.py:16

commit v4 on v3

--- a/solution.py
+++ b/solution.py
@@ -42,10 +42,12 @@
     return top, (x - top.astype(f32)).astype(bf16)
 
 
-def rows_kernel(width, x_ref, sign_ref, work_ref):
-    def some(lo, _):
+def transform_kernel(width, x_ref, sign_ref, mixed_ref, work_ref):
+    bands = width // 8
+
+    def first(lo, _):
         signs = [sign_ref[pl.ds(hi * 8 + lo, 1), :].astype(f32) for hi in range(16)]
-        for band in range(width // 8):
+        for band in range(bands):
             rows = pl.ds(band * 8, 8)
             values = []
             for hi in range(16):
@@ -55,50 +57,43 @@
                 work_ref[hi * 8 + lo, rows, :] = value
         return 0
 
-    lax.fori_loop(0, 8, some, 0)
-
-
-def table_kernel(width, work_ref, table_ref):
-    group = LANES // width
-    bands = width // 8
+    lax.fori_loop(0, 8, first, 0)
     row = lax.broadcasted_iota(jnp.int32, (LANES, 2 * LANES), 0)
     column = lax.broadcasted_iota(jnp.int32, (LANES, 2 * LANES), 1)
     hadamard = (1 - 2 * parity(row & (column & (LANES - 1)))).astype(f32).astype(bf16)
-    lane = lax.broadcasted_iota(jnp.int32, (LANES, LANES), 1) // width
-    in_lane = [lane == g for g in range(group)]
-    repeating = 4 if width * 8 > LANES else 8
-
-    def times(top, low):
-        both = jnp.concatenate([top, low], axis=1)
-        return lax.dot_general(hadamard, both, (((1,), (1,)), ((), ())), preferred_element_type=f32)
-
-    def some(hi, _):
+    blocks = 8 * width // LANES
+
+    def second(hi, _):
         rows = [
             butterflies([work_ref[hi * 8 + lo, pl.ds(band * 8, 8), :] for lo in range(8)]) for band in range(bands)
         ]
         y = jnp.concatenate([rows[band][lo] for lo in range(8) for band in range(bands)], axis=0)
-        top, low = halves(y)
-        results = []
-        for e in range(0, repeating, 2):
-            parts = [
-                jnp.concatenate([v[(e + i) * width : (e + i + 1) * width] for i in range(2) for _ in range(group)])
-                for v in (top, low)
-            ]
-            mixed = times(*parts)
-            results += [mixed[:, :LANES], mixed[:, LANES:]]
-        for e in range(repeating, 8, group):
-            mixed = times(top[e * width :][:LANES], low[e * width :][:LANES])
-            turned = [mixed] + [pltpu.roll(mixed, k * width, 1) for k in range(1, group)]
-            for i in range(group):
-                total = turned[-i % group]
-                for g in range(1, group):
-                    total = jnp.where(in_lane[g], turned[(g - i) % group], total)
-                results.append(total)
-        for e, result in enumerate(results):
-            table_ref[pl.ds(pl.multiple_of((hi * 8 + e) * LANES, LANES), LANES), :] = result
+        both = jnp.concatenate(halves(y), axis=1)
+        mixed = lax.dot_general(hadamard, both, (((1,), (1,)), ((), ())), preferred_element_type=f32)
+        for block in range(blocks):
+            start = pl.multiple_of((hi * blocks + block) * LANES, LANES)
+            mixed_ref[pl.ds(start, LANES), :] = mixed[:, block * LANES : (block + 1) * LANES]
         return 0
 
-    lax.fori_loop(0, 16, some, 0, unroll=4)
+    lax.fori_loop(0, 16, second, 0, unroll=4)
+
+
+def table_kernel(width, mixed_ref, table_ref):
+    group = LANES // width
+    lane = lax.broadcasted_iota(jnp.int32, (LANES, LANES), 1) // width
+    in_lane = [lane == g for g in range(group)]
+
+    def some(block, _):
+        mixed = mixed_ref[pl.ds(pl.multiple_of(block * LANES, LANES), LANES), :]
+        turned = [mixed] + [pltpu.roll(mixed, k * width, 1) for k in range(1, group)]
+        for e in range(group):
+            total = turned[-e % group]
+            for g in range(1, group):
+                total = jnp.where(in_lane[g], turned[(g - e) % group], total)
+            table_ref[pl.ds(pl.multiple_of((block * group + e) * LANES, LANES), LANES), :] = total
+        return 0
+
+    lax.fori_loop(0, LANES // group, some, 0, unroll=2)
 
 
 def pick_kernel(width, pieces, count, straight, *refs):
@@ -181,19 +176,20 @@
 PARAMS = pltpu.CompilerParams(vmem_limit_bytes=24 << 20)
 
 
-def transform_rows(panel, signs):
-    width, _ = panel.shape
+def transform(panel, signs):
+    width, row_count = panel.shape
     return pl.pallas_call(
-        functools.partial(rows_kernel, width),
-        out_shape=jax.ShapeDtypeStruct((LANES, width, LANES), f32),
+        functools.partial(transform_kernel, width),
+        out_shape=jax.ShapeDtypeStruct((row_count * width // LANES, LANES), f32),
         in_specs=[VMEM] * 2,
         out_specs=VMEM,
+        scratch_shapes=[pltpu.VMEM((LANES, width, LANES), f32)],
         compiler_params=PARAMS,
-        name="rows",
+        name="transform",
     )(panel, signs.reshape(LANES, LANES))
 
 
-def transform_table(work, width):
+def spread_lanes(mixed, width):
     return pl.pallas_call(
         functools.partial(table_kernel, width),
         out_shape=jax.ShapeDtypeStruct((LANES * LANES, LANES), f32),
@@ -201,7 +197,7 @@
         out_specs=VMEM,
         compiler_params=PARAMS,
         name="table",
-    )(work)
+    )(mixed)
 
 
 def reverse(i, bits):
@@ -219,7 +215,7 @@
     listed = [offsets]
     for t in range(1, 1 << near):
         listed.append(swapped(offsets, "row", t))
-    work = transform_rows(panel, signs)
+    mixed = transform(panel, signs)
     arrays, entries = list(listed), [(t, 0) for t in range(1 << near)]
     if bits > near:
         far = jnp.concatenate(listed)
@@ -230,7 +226,7 @@
             held = jnp.concatenate([arrays[k][at : at + count] for k, at in entries])
             arrays.append(swapped(held, "row", 1 << level))
             entries += [(len(arrays) - 1, t * count) for t in range(1 << level)]
-    table = transform_table(work, width)
+    table = spread_lanes(mixed, width)
 
     def pick(*pieces):
         used = sorted({entries[t][0] for slots, _, _ in pieces for t in slots})
@@ -253,18 +249,17 @@
         return slots[: len(slots) // 2], slots[len(slots) // 2 :]
 
     levels = list(range(bits - 1))
-    turned = [1, 0] + levels[2:] if bits > 2 else levels
     half = per // 2
     keep_up, send_up = split(range(devices // 2, devices), levels)
-    keep_low, send_low = split(range(devices // 2), turned)
+    keep_low, send_low = split(range(devices // 2), levels)
     sent, kept = [None] * 3, [None] * 3
-    sent[0], kept[0] = pick((send_up, 0, half), (keep_up, 0, half))
-    sent[1], sent[2], kept[1] = pick((send_up, half, half), (send_low, 0, per), (keep_up, half, half))
+    sent[0], sent[1] = pick((send_up, 0, half), (send_up, half, half))
+    sent[2], kept[0], kept[1] = pick((send_low, 0, per), (keep_up, 0, half), (keep_up, half, half))
     (kept[2],) = pick((keep_low, 0, per))
     totals = []
-    for k, order in enumerate((levels, levels, turned)):
+    for k in range(3):
         total, out = kept[k], sent[k]
-        for step, level in enumerate(order):
+        for step, level in enumerate(levels):
             if step:
                 middle = total.shape[0] // 2
                 total, out = total[:middle], total[middle:]

time: 61.1 us -> 61.1 us (level)
  waiting for transfers between devices: 25.3 us -> 21.5 us
  starting transfers between devices: 19.6 us -> 21.7 us
  Pallas kernels: 11.7 us -> 13.3 us
    ppermute x19, waiting for transfers between devices: 25.3 us -> 21.5 us  [swapped(): lax.ppermute(x, axis, [(i, i ^ distance) for i in range(lax.axis_size(axi...]
    ppermute x19, starting transfers between devices: 19.6 us -> 21.7 us  [swapped(): lax.ppermute(x, axis, [(i, i ^ distance) for i in range(lax.axis_size(axi...]
    pallas_call x2, Pallas kernels: 3.15 us -> 4.83 us  [the longest x1 2.85 us: spread_lanes(): pl.pallas_call(functools.partial(table_kernel, width), out_shape=jax.Shap...]
  transfers between devices with their start and end apart: 19 -> 19, of which waited for: 15 -> 13; matrix products, arithmetic and copies ran while one was open for 1% -> 1% of each run, Pallas kernels for 14% -> 16%
where the time goes in v4:
time: 61.1 us; the launch traced here: 60.9 us
  starting transfers between devices  21.7 us (36%)
  waiting for transfers between devices  21.5 us (35%)
  Pallas kernels  13.3 us (22%)
  local copies, waits for them, and re-layouts  2.73 us (4%)
  other arithmetic  1.47 us (2%)
    ppermute x19, starting transfers between devices, swapped(): lax.ppermute(x, axis, [(i, i ^ distance) for i in range(lax.axis_size(axi...  21.7 us
    ppermute x19, waiting for transfers between devices, swapped(): lax.ppermute(x, axis, [(i, i ^ distance) for i in range(lax.axis_size(axi...  21.5 us
    pallas_call x3, Pallas kernels, pick(): pl.pallas_call(functools.partial(pick_kernel, width, full, count, straigh...  7 us
    pallas_call x1, Pallas kernels, spread_lanes(): pl.pallas_call(functools.partial(table_kernel, width), out_shape=jax.Shap...  2.85 us
    unnamed x10, local copies, waits for them, and re-layouts  2.67 us
    pallas_call x1, Pallas kernels, transform(): pl.pallas_call(functools.partial(transform_kernel, width), out_shape=jax....  1.98 us
    pallas_call x1, Pallas kernels, body(): pl.pallas_call(functools.partial(gram_kernel, width, count, devices, scal...  1.49 us
  transfers between devices with their start and end apart: 19, of which 13 were waited for; matrix products, arithmetic and copies ran while one was open for 1% of the time, Pallas kernels for 16%

profile of v4, /device:TPU:0, one launch (start us, length us, event | category | flops | bytes accessed | tf_op | source)
XLA Modules:
  0.0 60.9 jit_solution(1438294380434085496)
XLA Ops:
  0.0 3.1 %collective-permute-start = (s32[1024]{0:T(1024)}, s32[1024]{0:T(1024)S(1)}, u32[]{:S(2)}, u32[]{:S(2)}) collective-permute-start(s32[1024]{0:T(1024)} %refs_0_.1), channel_id=1, source_target_pairs={{0,8},{4,12},{8,0},{12,4},{16,24},{20,28},{24,16},{28,20},{1,9},{5... | collective-permute-start | bytes 12296 | tf_op jit(solution)/shard_map/ppermute | solution.py:16
  3.1 1.5 %collective-permute-start.1 = (s32[1024]{0:T(1024)}, s32[1024]{0:T(1024)S(1)}, u32[]{:S(2)}, u32[]{:S(2)}) collective-permute-start(s32[1024]{0:T(1024)} %refs_0_.1), channel_id=1, source_target_pairs={{0,4},{4,0},{8,12},{12,8},{16,20},{20,16},{24,28},{28,24},{1,5},{5... | collective-permute-start | bytes 12296 | tf_op jit(solution)/shard_map/ppermute | solution.py:16
  4.8 2.0 %collective-permute-done.1.refs_0_ = s32[1024]{0:T(1024)S(1)} collective-permute-done((s32[1024]{0:T(1024)}, s32[1024]{0:T(1024)S(1)}, u32[]{:S(2)}, u32[]{:S(2)}) %collective-permute-start.1) | collective-permute-done | bytes 4128 | tf_op jit(solution)/shard_map/ppermute | solution.py:16
  6.9 2.4 %collective-permute-done.2.refs_1_ = s32[1024]{0:T(1024)S(1)} collective-permute-done((s32[1024]{0:T(1024)}, s32[1024]{0:T(1024)S(1)}, u32[]{:S(2)}, u32[]{:S(2)}) %collective-permute-start.2) | collective-permute-done | bytes 4128 | tf_op jit(solution)/shard_map/ppermute | solution.py:16
  10.0 2.6 %collective-permute-start.3 = (s32[4096]{0:T(1024)S(1)}, s32[4096]{0:T(1024)S(1)}, u32[]{:S(2)}, u32[]{:S(2)}) collective-permute-start(s32[4096]{0:T(1024)S(1)} %pad_add_fusion), channel_id=1, source_target_pairs={{0,16},{4,20},{8,24},{12,28},{16,0},{20,4},{24,8},{28,12},{1,17},{... | collective-permute-start | bytes 49160 | tf_op jit(solution)/shard_map/ppermute | solution.py:16
  12.5 1.6 %copy-done = f32[32,16384]{1,0:T(8,128)S(1)} copy-done((f32[32,16384]{1,0:T(8,128)S(1)}, f32[32,16384]{1,0:T(8,128)}, u32[]{:S(2)}) %copy-start) | copy-done | bytes 2097176
  15.0 2.0 %transform.1.mixed_ref = f32[4096,128]{1,0:T(8,128)S(1)} custom-call(f32[32,16384]{1,0:T(8,128)S(1)} %copy-done, s32[128,128]{1,0:T(8,128)S(1)} %bitcast.13), custom_call_target="tpu_custom_call" | custom-call | tf_op jit(solution)/shard_map/transform/pallas_call | solution.py:181
  17.0 2.8 %table.1.refs_2_.refs_3_.refs_1_ = f32[16384,128]{1,0:T(8,128)S(1)} custom-call(f32[4096,128]{1,0:T(8,128)S(1)} %transform.1.mixed_ref), custom_call_target="tpu_custom_call" | custom-call | tf_op jit(solution)/shard_map/table/pallas_call | solution.py:193
  19.8 1.9 %pick.5 = (f32[256,128]{1,0:T(8,128)S(1)}, f32[256,128]{1,0:T(8,128)S(1)}) custom-call(s32[4096]{0:T(1024)S(1)} %collective-permute-done.3.refs_2_.refs_0_, f32[16384,128]{1,0:T(8,128)S(1)} %table.1.refs_2_.refs_3_.refs_1_), custom_call_target="tpu_custom_call" | custom-call | tf_op jit(solution)/shard_map/pick/pallas_call | solution.py:238
  22.4 1.5 %collective-permute-start.9 = (f32[256,128]{1,0:T(8,128)S(1)}, f32[256,128]{1,0:T(8,128)S(1)}, u32[]{:S(2)}, u32[]{:S(2)}) collective-permute-start(f32[256,128]{1,0:T(8,128)S(1)} %get-tuple-element.18), channel_id=1, source_target_pairs={{0,4},{4,0},{8,12},{12,8},{16,20},{20,16},{24,28},{28,24},{1,5},{5... | collective-permute-start | bytes 393224 | tf_op jit(solution)/shard_map/ppermute | solution.py:16
  23.8 3.3 %pick.4 = (f32[512,128]{1,0:T(8,128)S(1)}, f32[256,128]{1,0:T(8,128)S(1)}, f32[256,128]{1,0:T(8,128)S(1)}) custom-call(s32[1024]{0:T(1024)S(1)} %collective-permute-done.1.refs_0_, s32[1024]{0:T(1024)S(1)} %collective-permute-done.2.refs_1_, s32[4096]{0:T(1024)S(1)} %collective-permute-done.3.refs_2_.refs_0_, f32[16384,128]{1,0:T(8,128)S(1)} %table.1.refs_2_.refs_3_.refs_1_), custom_call_target="tpu_custom_call" | custom-call | tf_op jit(solution)/shard_map/pick/pallas_call | solution.py:238
  28.2 1.8 %pick.3 = f32[512,128]{1,0:T(8,128)S(1)} custom-call(s32[1024]{0:T(1024)S(1)} %copy-done.2, s32[1024]{0:T(1024)S(1)} %collective-permute-done.refs_1_, f32[16384,128]{1,0:T(8,128)S(1)} %table.1.refs_2_.refs_3_.refs_1_), custom_call_target="tpu_custom_call" | custom-call | tf_op jit(solution)/shard_map/pick/pallas_call | solution.py:238
  30.1 1.6 %collective-permute-start.10 = (f32[128,128]{1,0:T(8,128)S(1)}, f32[128,128]{1,0:T(8,128)S(1)}, u32[]{:S(2)}, u32[]{:S(2)}) collective-permute-start(f32[128,128]{1,0:T(8,128)S(1)} %slice.75), channel_id=1, source_target_pairs={{0,8},{4,12},{8,0},{12,4},{16,24},{20,28},{24,16},{28,20},{1,9},{5... | collective-permute-start | bytes 196616 | tf_op jit(solution)/shard_map/ppermute | solution.py:16
  32.2 1.9 %collective-permute-done.4 = f32[512,128]{1,0:T(8,128)S(1)} collective-permute-done((f32[512,128]{1,0:T(8,128)S(1)}, f32[512,128]{1,0:T(8,128)S(1)}, u32[]{:S(2)}, u32[]{:S(2)}) %collective-permute-start.4) | collective-permute-done | bytes 262176 | tf_op jit(solution)/shard_map/ppermute | solution.py:16
  34.1 1.6 %collective-permute-start.5 = (f32[256,128]{1,0:T(8,128)S(1)}, f32[256,128]{1,0:T(8,128)S(1)}, u32[]{:S(2)}, u32[]{:S(2)}) collective-permute-start(f32[256,128]{1,0:T(8,128)S(1)} %slice.69), channel_id=1, source_target_pairs={{0,8},{4,12},{8,0},{12,4},{16,24},{20,28},{24,16},{28,20},{1,9},{5... | collective-permute-start | bytes 393224 | tf_op jit(solution)/shard_map/ppermute | solution.py:16
  36.2 3.3 %collective-permute-done.5 = f32[256,128]{1,0:T(8,128)S(1)} collective-permute-done((f32[256,128]{1,0:T(8,128)S(1)}, f32[256,128]{1,0:T(8,128)S(1)}, u32[]{:S(2)}, u32[]{:S(2)}) %collective-permute-start.5) | collective-permute-done | bytes 131104 | tf_op jit(solution)/shard_map/ppermute | solution.py:16
  39.5 1.6 %collective-permute-start.12 = (f32[128,128]{1,0:T(8,128)S(1)}, f32[128,128]{1,0:T(8,128)S(1)}, u32[]{:S(2)}, u32[]{:S(2)}) collective-permute-start(f32[128,128]{1,0:T(8,128)S(1)} %get-tuple-element.15), channel_id=1, source_target_pairs={{0,2},{1,3},{2,0},{3,1},{4,6},{5,7},{6,4},{7,5},{8,10},{9,11},{10,... | collective-permute-start | bytes 196616 | tf_op jit(solution)/shard_map/ppermute | solution.py:16
  41.7 1.6 %collective-permute-start.13 = (f32[128,128]{1,0:T(8,128)S(1)}, f32[128,128]{1,0:T(8,128)S(1)}, u32[]{:S(2)}, u32[]{:S(2)}) collective-permute-start(f32[128,128]{1,0:T(8,128)S(1)} %add.43), channel_id=1, source_target_pairs={{0,2},{1,3},{2,0},{3,1},{4,6},{5,7},{6,4},{7,5},{8,10},{9,11},{10,... | collective-permute-start | bytes 196616 | tf_op jit(solution)/shard_map/ppermute | solution.py:16
  43.9 2.1 %collective-permute-done.13 = f32[128,128]{1,0:T(8,128)S(1)} collective-permute-done((f32[128,128]{1,0:T(8,128)S(1)}, f32[128,128]{1,0:T(8,128)S(1)}, u32[]{:S(2)}, u32[]{:S(2)}) %collective-permute-start.13) | collective-permute-done | bytes 65568 | tf_op jit(solution)/shard_map/ppermute | solution.py:16
  47.7 1.5 %gram.1 = f32[256,128]{1,0:T(8,128)S(1)} custom-call(s32[1024,1]{1,0:T(8,128)S(1)} %copy.5.owner_ref, f32[256,128]{1,0:T(8,128)S(1)} %get-tuple-element.26.refs_0_, f32[256,128]{1,0:T(8,128)S(1)} %get-tuple-element.20.refs_1_, f32[256,128]{1,0:T(8,128)S(1)} %constant_dynamic-update-slice_fusion.refs_2_, f32[256,128]{1,0:T(8,128)S(1)} %get-tuple-element.19.refs_3_), custom_call_target="tpu_custom_call" | custom-call | tf_op jit(solution)/shard_map/gram/pallas_call | solution.py:283
  49.2 1.6 %collective-permute-start.15 = (f32[2,32,128]{2,1,0:T(8,128)S(1)}, f32[2,32,128]{2,1,0:T(8,128)S(1)}, u32[]{:S(2)}, u32[]{:S(2)}) collective-permute-start(f32[2,32,128]{2,1,0:T(8,128)S(1)} %bitcast.17), channel_id=1, source_target_pairs={{0,4},{4,0},{8,12},{12,8},{16,20},{20,16},{24,28},{28,24},{1,5},{5... | collective-permute-start | bytes 98312 | tf_op jit(solution)/shard_map/ppermute | solution.py:16
  50.8 2.0 %collective-permute-start.17 = (f32[2,32,128]{2,1,0:T(8,128)S(1)}, f32[2,32,128]{2,1,0:T(8,128)S(1)}, u32[]{:S(2)}, u32[]{:S(2)}) collective-permute-start(f32[2,32,128]{2,1,0:T(8,128)S(1)} %bitcast.15), channel_id=1, source_target_pairs={{0,12},{4,8},{8,4},{12,0},{16,28},{20,24},{24,20},{28,16},{1,13},{... | collective-permute-start | bytes 98312 | tf_op jit(solution)/shard_map/ppermute | solution.py:16
  53.2 1.5 %collective-permute-done.16 = f32[2,32,128]{2,1,0:T(8,128)S(1)} collective-permute-done((f32[2,32,128]{2,1,0:T(8,128)S(1)}, f32[2,32,128]{2,1,0:T(8,128)S(1)}, u32[]{:S(2)}, u32[]{:S(2)}) %collective-permute-start.16) | collective-permute-done | bytes 32800 | tf_op jit(solution)/shard_map/ppermute | solution.py:16
  56.1 4.2 %collective-permute-done.18 = f32[1,32,128]{2,1,0:T(8,128)S(1)} collective-permute-done((f32[1,32,128]{2,1,0:T(8,128)S(1)}, f32[1,32,128]{2,1,0:T(8,128)S(1)}, u32[]{:S(2)}, u32[]{:S(2)}) %collective-permute-start.18) | collective-permute-done | bytes 16416 | tf_op jit(solution)/shard_map/ppermute | solution.py:16
  (50 shorter events, 9.7 us)
Async XLA Ops:
  0.0 4.8 %collective-permute-start = (s32[1024]{0:T(1024)}, s32[1024]{0:T(1024)S(1)}, u32[]{:S(2)}, u32[]{:S(2)}) collective-permute-start(s32[1024]{0:T(1024)} %refs_0_.1), channel_id=1, source_target_pairs={{0,8},{4,12},{8,0},{12,4},{16,24},{20,28},{24,16},{28,20},{1,9},{5... | collective-permute-start | bytes 12296 | tf_op jit(solution)/shard_map/ppermute | solution.py:16
  3.1 3.8 %collective-permute-start.1 = (s32[1024]{0:T(1024)}, s32[1024]{0:T(1024)S(1)}, u32[]{:S(2)}, u32[]{:S(2)}) collective-permute-start(s32[1024]{0:T(1024)} %refs_0_.1), channel_id=1, source_target_pairs={{0,4},{4,0},{8,12},{12,8},{16,20},{20,16},{24,28},{28,24},{1,5},{5... | collective-permute-start | bytes 12296 | tf_op jit(solution)/shard_map/ppermute | solution.py:16
  4.5 4.7 %collective-permute-start.2 = (s32[1024]{0:T(1024)}, s32[1024]{0:T(1024)S(1)}, u32[]{:S(2)}, u32[]{:S(2)}) collective-permute-start(s32[1024]{0:T(1024)} %refs_0_.1), channel_id=1, source_target_pairs={{0,12},{4,8},{8,4},{12,0},{16,28},{20,24},{24,20},{28,16},{1,13},{... | collective-permute-start | bytes 12296 | tf_op jit(solution)/shard_map/ppermute | solution.py:16
  10.0 9.9 %collective-permute-start.3 = (s32[4096]{0:T(1024)S(1)}, s32[4096]{0:T(1024)S(1)}, u32[]{:S(2)}, u32[]{:S(2)}) collective-permute-start(s32[4096]{0:T(1024)S(1)} %pad_add_fusion), channel_id=1, source_target_pairs={{0,16},{4,20},{8,24},{12,28},{16,0},{20,4},{24,8},{28,12},{1,17},{... | collective-permute-start | bytes 49160 | tf_op jit(solution)/shard_map/ppermute | solution.py:16
  12.5 1.6 %copy-start = (f32[32,16384]{1,0:T(8,128)S(1)}, f32[32,16384]{1,0:T(8,128)}, u32[]{:S(2)}) copy-start(f32[32,16384]{1,0:T(8,128)} %x_ref.1) | copy-start | bytes 6291460
  14.1 0.8 %copy-start.1 = (s32[16384]{0:T(1024)S(1)}, s32[16384]{0:T(1024)}, u32[]{:S(2)}) copy-start(s32[16384]{0:T(1024)} %param.5) | copy-start | bytes 196612
  21.8 5.4 %collective-permute-start.6 = (f32[256,128]{1,0:T(8,128)S(1)}, f32[256,128]{1,0:T(8,128)S(1)}, u32[]{:S(2)}, u32[]{:S(2)}) collective-permute-start(f32[256,128]{1,0:T(8,128)S(1)} %get-tuple-element.14), channel_id=1, source_target_pairs={{0,4},{4,0},{8,12},{12,8},{16,20},{20,16},{24,28},{28,24},{1,5},{5... | collective-permute-start | bytes 393224 | tf_op jit(solution)/shard_map/ppermute | solution.py:16
  22.4 5.9 %copy-start.2 = (s32[1024]{0:T(1024)S(1)}, s32[1024]{0:T(1024)}, u32[]{:S(2)}) copy-start(s32[1024]{0:T(1024)} %refs_0_.1) | copy-start | bytes 12292
  22.4 7.7 %collective-permute-start.9 = (f32[256,128]{1,0:T(8,128)S(1)}, f32[256,128]{1,0:T(8,128)S(1)}, u32[]{:S(2)}, u32[]{:S(2)}) collective-permute-start(f32[256,128]{1,0:T(8,128)S(1)} %get-tuple-element.18), channel_id=1, source_target_pairs={{0,4},{4,0},{8,12},{12,8},{16,20},{20,16},{24,28},{28,24},{1,5},{5... | collective-permute-start | bytes 393224 | tf_op jit(solution)/shard_map/ppermute | solution.py:16
  27.2 4.6 %collective-permute-start.7 = (f32[128,128]{1,0:T(8,128)S(1)}, f32[128,128]{1,0:T(8,128)S(1)}, u32[]{:S(2)}, u32[]{:S(2)}) collective-permute-start(f32[128,128]{1,0:T(8,128)S(1)} %slice.73), channel_id=1, source_target_pairs={{0,8},{4,12},{8,0},{12,4},{16,24},{20,28},{24,16},{28,20},{1,9},{5... | collective-permute-start | bytes 196616 | tf_op jit(solution)/shard_map/ppermute | solution.py:16
  27.7 6.4 %collective-permute-start.4 = (f32[512,128]{1,0:T(8,128)S(1)}, f32[512,128]{1,0:T(8,128)S(1)}, u32[]{:S(2)}, u32[]{:S(2)}) collective-permute-start(f32[512,128]{1,0:T(8,128)S(1)} %get-tuple-element.12), channel_id=1, source_target_pairs={{0,4},{4,0},{8,12},{12,8},{16,20},{20,16},{24,28},{28,24},{1,5},{5... | collective-permute-start | bytes 786440 | tf_op jit(solution)/shard_map/ppermute | solution.py:16
  30.0 16.1 %copy-start.3 = (s32[1024,1]{0,1:T(1,128)S(1)}, s32[1024,1]{0,1:T(1,128)}, u32[]{:S(2)}) copy-start(s32[1024,1]{0,1:T(1,128)} %param.7) | copy-start | bytes 12292
  30.1 5.6 %collective-permute-start.10 = (f32[128,128]{1,0:T(8,128)S(1)}, f32[128,128]{1,0:T(8,128)S(1)}, u32[]{:S(2)}, u32[]{:S(2)}) collective-permute-start(f32[128,128]{1,0:T(8,128)S(1)} %slice.75), channel_id=1, source_target_pairs={{0,8},{4,12},{8,0},{12,4},{16,24},{20,28},{24,16},{28,20},{1,9},{5... | collective-permute-start | bytes 196616 | tf_op jit(solution)/shard_map/ppermute | solution.py:16
  31.8 7.8 %collective-permute-start.8 = (f32[128,128]{1,0:T(8,128)S(1)}, f32[128,128]{1,0:T(8,128)S(1)}, u32[]{:S(2)}, u32[]{:S(2)}) collective-permute-start(f32[128,128]{1,0:T(8,128)S(1)} %slice_add_fusion.2), channel_id=1, source_target_pairs={{0,16},{4,20},{8,24},{12,28},{16,0},{20,4},{24,8},{28,12},{1,17},{... | collective-permute-start | bytes 196616 | tf_op jit(solution)/shard_map/ppermute | solution.py:16
  34.1 5.4 %collective-permute-start.5 = (f32[256,128]{1,0:T(8,128)S(1)}, f32[256,128]{1,0:T(8,128)S(1)}, u32[]{:S(2)}, u32[]{:S(2)}) collective-permute-start(f32[256,128]{1,0:T(8,128)S(1)} %slice.69), channel_id=1, source_target_pairs={{0,8},{4,12},{8,0},{12,4},{16,24},{20,28},{24,16},{28,20},{1,9},{5... | collective-permute-start | bytes 393224 | tf_op jit(solution)/shard_map/ppermute | solution.py:16
  35.8 5.9 %collective-permute-start.11 = (f32[128,128]{1,0:T(8,128)S(1)}, f32[128,128]{1,0:T(8,128)S(1)}, u32[]{:S(2)}, u32[]{:S(2)}) collective-permute-start(f32[128,128]{1,0:T(8,128)S(1)} %slice_add_fusion.1), channel_id=1, source_target_pairs={{0,16},{4,20},{8,24},{12,28},{16,0},{20,4},{24,8},{28,12},{1,17},{... | collective-permute-start | bytes 196616 | tf_op jit(solution)/shard_map/ppermute | solution.py:16
  39.5 4.3 %collective-permute-start.12 = (f32[128,128]{1,0:T(8,128)S(1)}, f32[128,128]{1,0:T(8,128)S(1)}, u32[]{:S(2)}, u32[]{:S(2)}) collective-permute-start(f32[128,128]{1,0:T(8,128)S(1)} %get-tuple-element.15), channel_id=1, source_target_pairs={{0,2},{1,3},{2,0},{3,1},{4,6},{5,7},{6,4},{7,5},{8,10},{9,11},{10,... | collective-permute-start | bytes 196616 | tf_op jit(solution)/shard_map/ppermute | solution.py:16
  41.7 4.3 %collective-permute-start.13 = (f32[128,128]{1,0:T(8,128)S(1)}, f32[128,128]{1,0:T(8,128)S(1)}, u32[]{:S(2)}, u32[]{:S(2)}) collective-permute-start(f32[128,128]{1,0:T(8,128)S(1)} %add.43), channel_id=1, source_target_pairs={{0,2},{1,3},{2,0},{3,1},{4,6},{5,7},{6,4},{7,5},{8,10},{9,11},{10,... | collective-permute-start | bytes 196616 | tf_op jit(solution)/shard_map/ppermute | solution.py:16
  46.1 1.6 %collective-permute-start.14 = (f32[2,256,128]{2,1,0:T(8,128)S(1)}, f32[2,256,128]{2,1,0:T(8,128)S(1)}, u32[]{:S(2)}, u32[]{:S(2)}) collective-permute-start(f32[2,256,128]{2,1,0:T(8,128)S(1)} %pad_maximum_fusion), channel_id=1, source_target_pairs={{0,1},{1,0},{2,3},{3,2},{4,5},{5,4},{6,7},{7,6},{8,9},{9,8},{10,11... | collective-permute-start | bytes 786440 | tf_op jit(solution)/shard_map/ppermute | solution.py:16
  49.2 4.0 %collective-permute-start.15 = (f32[2,32,128]{2,1,0:T(8,128)S(1)}, f32[2,32,128]{2,1,0:T(8,128)S(1)}, u32[]{:S(2)}, u32[]{:S(2)}) collective-permute-start(f32[2,32,128]{2,1,0:T(8,128)S(1)} %bitcast.17), channel_id=1, source_target_pairs={{0,4},{4,0},{8,12},{12,8},{16,20},{20,16},{24,28},{28,24},{1,5},{5... | collective-permute-start | bytes 98312 | tf_op jit(solution)/shard_map/ppermute | solution.py:16
  50.8 3.9 %collective-permute-start.16 = (f32[2,32,128]{2,1,0:T(8,128)S(1)}, f32[2,32,128]{2,1,0:T(8,128)S(1)}, u32[]{:S(2)}, u32[]{:S(2)}) collective-permute-start(f32[2,32,128]{2,1,0:T(8,128)S(1)} %bitcast.16), channel_id=1, source_target_pairs={{0,8},{4,12},{8,0},{12,4},{16,24},{20,28},{24,16},{28,20},{1,9},{5... | collective-permute-start | bytes 98312 | tf_op jit(solution)/shard_map/ppermute | solution.py:16
  50.8 4.8 %collective-permute-start.17 = (f32[2,32,128]{2,1,0:T(8,128)S(1)}, f32[2,32,128]{2,1,0:T(8,128)S(1)}, u32[]{:S(2)}, u32[]{:S(2)}) collective-permute-start(f32[2,32,128]{2,1,0:T(8,128)S(1)} %bitcast.15), channel_id=1, source_target_pairs={{0,12},{4,8},{8,4},{12,0},{16,28},{20,24},{24,20},{28,16},{1,13},{... | collective-permute-start | bytes 98312 | tf_op jit(solution)/shard_map/ppermute | solution.py:16
  55.6 4.7 %collective-permute-start.18 = (f32[1,32,128]{2,1,0:T(8,128)S(1)}, f32[1,32,128]{2,1,0:T(8,128)S(1)}, u32[]{:S(2)}, u32[]{:S(2)}) collective-permute-start(f32[1,32,128]{2,1,0:T(8,128)S(1)} %slice.83), channel_id=1, source_target_pairs={{0,16},{4,20},{8,24},{12,28},{16,0},{20,4},{24,8},{28,12},{1,17},{... | collective-permute-start | bytes 49160 | tf_op jit(solution)/shard_map/ppermute | solution.py:16

commit v5 on v4

--- a/solution.py
+++ b/solution.py
@@ -42,7 +42,17 @@
     return top, (x - top.astype(f32)).astype(bf16)
 
 
-def transform_kernel(width, x_ref, sign_ref, mixed_ref, work_ref):
+def signs_of(rows, columns):
+    row = lax.broadcasted_iota(jnp.int32, (rows, columns), 0)
+    column = lax.broadcasted_iota(jnp.int32, (rows, columns), 1)
+    return (1 - 2 * parity(row & (column & (LANES - 1)))).astype(f32).astype(bf16)
+
+
+def times(hadamard, both):
+    return lax.dot_general(hadamard, both, (((1,), (1,)), ((), ())), preferred_element_type=f32)
+
+
+def transform_kernel(width, rolled, x_ref, sign_ref, both_ref, mixed_ref, work_ref):
     bands = width // 8
 
     def first(lo, _):
@@ -58,10 +68,8 @@
         return 0
 
     lax.fori_loop(0, 8, first, 0)
-    row = lax.broadcasted_iota(jnp.int32, (LANES, 2 * LANES), 0)
-    column = lax.broadcasted_iota(jnp.int32, (LANES, 2 * LANES), 1)
-    hadamard = (1 - 2 * parity(row & (column & (LANES - 1)))).astype(f32).astype(bf16)
-    blocks = 8 * width // LANES
+    hadamard = signs_of(LANES, 2 * LANES)
+    straight = (8 - rolled) * width
 
     def second(hi, _):
         rows = [
@@ -69,31 +77,40 @@
         ]
         y = jnp.concatenate([rows[band][lo] for lo in range(8) for band in range(bands)], axis=0)
         both = jnp.concatenate(halves(y), axis=1)
-        mixed = lax.dot_general(hadamard, both, (((1,), (1,)), ((), ())), preferred_element_type=f32)
-        for block in range(blocks):
-            start = pl.multiple_of((hi * blocks + block) * LANES, LANES)
-            mixed_ref[pl.ds(start, LANES), :] = mixed[:, block * LANES : (block + 1) * LANES]
+        both_ref[pl.ds(pl.multiple_of(hi * straight, 8), straight), :] = both[:straight]
+        if rolled:
+            mixed_ref[pl.ds(pl.multiple_of(hi * LANES, LANES), LANES), :] = times(hadamard, both[straight:])
         return 0
 
     lax.fori_loop(0, 16, second, 0, unroll=4)
 
 
-def table_kernel(width, mixed_ref, table_ref):
+def table_kernel(width, rolled, both_ref, mixed_ref, table_ref):
     group = LANES // width
     lane = lax.broadcasted_iota(jnp.int32, (LANES, LANES), 1) // width
     in_lane = [lane == g for g in range(group)]
-
-    def some(block, _):
-        mixed = mixed_ref[pl.ds(pl.multiple_of(block * LANES, LANES), LANES), :]
-        turned = [mixed] + [pltpu.roll(mixed, k * width, 1) for k in range(1, group)]
-        for e in range(group):
-            total = turned[-e % group]
-            for g in range(1, group):
-                total = jnp.where(in_lane[g], turned[(g - e) % group], total)
-            table_ref[pl.ds(pl.multiple_of((block * group + e) * LANES, LANES), LANES), :] = total
+    hadamard = signs_of(LANES, 2 * LANES)
+    straight = (8 - rolled) * width
+
+    def some(hi, _):
+        results = []
+        for e in range(0, 8 - rolled, 2):
+            rows = [both_ref[pl.ds(hi * straight + (e + i) * width, width), :] for i in range(2)]
+            mixed = times(hadamard, jnp.concatenate([row for row in rows for _ in range(group)], axis=0))
+            results += [mixed[:, :LANES], mixed[:, LANES:]]
+        if rolled:
+            mixed = mixed_ref[pl.ds(pl.multiple_of(hi * LANES, LANES), LANES), :]
+            turned = [mixed] + [pltpu.roll(mixed, k * width, 1) for k in range(1, group)]
+            for e in range(group):
+                total = turned[-e % group]
+                for g in range(1, group):
+                    total = jnp.where(in_lane[g], turned[(g - e) % group], total)
+                results.append(total)
+        for e, result in enumerate(results):
+            table_ref[pl.ds(pl.multiple_of((hi * 8 + e) * LANES, LANES), LANES), :] = result
         return 0
 
-    lax.fori_loop(0, LANES // group, some, 0, unroll=2)
+    lax.fori_loop(0, 16, some, 0, unroll=4)
 
 
 def pick_kernel(width, pieces, count, straight, *refs):
@@ -138,15 +155,16 @@
     per = count // group
     packed, out_ref = refs[:-1], refs[-1]
     lane = lax.broadcasted_iota(jnp.int32, (per, LANES), 1)
+    in_lane = [lane // width == u for u in range(group)]
+    turned = [[ref[...]] + [pltpu.roll(ref[...], k * width, 1) for k in range(1, group)] for ref in packed]
     parts, repeated = [], []
     for g in range(group):
-        total = packed[g][...]
-        for u in range(group):
-            if u != g:
-                moved = jnp.take_along_axis(packed[u][...], lane ^ ((u ^ g) * width), axis=1)
-                total = jnp.where(lane // width == u, moved, total)
+        total, mine = turned[0][-g % group], turned[0][-g % group]
+        for u in range(1, group):
+            total = jnp.where(in_lane[u], turned[u][(u - g) % group], total)
+            mine = jnp.where(in_lane[u], turned[0][(u - g) % group], mine)
         parts.append(total)
-        repeated.append(jnp.take_along_axis(packed[0][...], (lane & (width - 1)) + g * width, axis=1))
+        repeated.append(mine)
     sketch = jnp.concatenate(parts, axis=0)
     mine = jnp.concatenate(repeated, axis=0)
     top, low = halves(sketch)
@@ -177,27 +195,32 @@
 
 
 def transform(panel, signs):
-    width, row_count = panel.shape
+    width, _ = panel.shape
+    rolled = LANES // width if 8 * width > LANES else 0
     return pl.pallas_call(
-        functools.partial(transform_kernel, width),
-        out_shape=jax.ShapeDtypeStruct((row_count * width // LANES, LANES), f32),
+        functools.partial(transform_kernel, width, rolled),
+        out_shape=[
+            jax.ShapeDtypeStruct((16 * (8 - rolled) * width, 2 * LANES), bf16),
+            jax.ShapeDtypeStruct((16 * LANES, LANES), f32),
+        ],
         in_specs=[VMEM] * 2,
-        out_specs=VMEM,
+        out_specs=[VMEM] * 2,
         scratch_shapes=[pltpu.VMEM((LANES, width, LANES), f32)],
         compiler_params=PARAMS,
         name="transform",
     )(panel, signs.reshape(LANES, LANES))
 
 
-def spread_lanes(mixed, width):
+def spread_lanes(parts, width):
+    rolled = LANES // width if 8 * width > LANES else 0
     return pl.pallas_call(
-        functools.partial(table_kernel, width),
+        functools.partial(table_kernel, width, rolled),
         out_shape=jax.ShapeDtypeStruct((LANES * LANES, LANES), f32),
-        in_specs=[VMEM],
+        in_specs=[VMEM] * 2,
         out_specs=VMEM,
         compiler_params=PARAMS,
         name="table",
-    )(mixed)
+    )(*parts)
 
 
 def reverse(i, bits):
@@ -215,7 +238,7 @@
     listed = [offsets]
     for t in range(1, 1 << near):
         listed.append(swapped(offsets, "row", t))
-    mixed = transform(panel, signs)
+    parts = transform(panel, signs)
     arrays, entries = list(listed), [(t, 0) for t in range(1 << near)]
     if bits > near:
         far = jnp.concatenate(listed)
@@ -226,7 +249,7 @@
             held = jnp.concatenate([arrays[k][at : at + count] for k, at in entries])
             arrays.append(swapped(held, "row", 1 << level))
             entries += [(len(arrays) - 1, t * count) for t in range(1 << level)]
-    table = spread_lanes(mixed, width)
+    table = spread_lanes(parts, width)
 
     def pick(*pieces):
         used = sorted({entries[t][0] for slots, _, _ in pieces for t in slots})

time: 61.1 us -> 60.1 us (0.984)
  Pallas kernels: 13.3 us -> 12.3 us
    pallas_call x2, Pallas kernels: 4.83 us -> 3.89 us  [the longest x1 2.06 us: spread_lanes(): pl.pallas_call(functools.partial(table_kernel, width, rolled), out_shape=...]
  transfers between devices with their start and end apart: 19 -> 19, of which waited for: 13 -> 13; matrix products, arithmetic and copies ran while one was open for 1% -> 1% of each run, Pallas kernels for 16% -> 15%
where the time goes in v5:
time: 60.1 us; the launch traced here: 59.9 us
  starting transfers between devices  21.6 us (36%)
  waiting for transfers between devices  21.6 us (36%)
  Pallas kernels  12.3 us (20%)
  local copies, waits for them, and re-layouts  2.73 us (5%)
  other arithmetic  1.47 us (2%)
    ppermute x19, starting transfers between devices, swapped(): lax.ppermute(x, axis, [(i, i ^ distance) for i in range(lax.axis_size(axi...  21.6 us
    ppermute x19, waiting for transfers between devices, swapped(): lax.ppermute(x, axis, [(i, i ^ distance) for i in range(lax.axis_size(axi...  21.6 us
    pallas_call x3, Pallas kernels, pick(): pl.pallas_call(functools.partial(pick_kernel, width, full, count, straigh...  7 us
    unnamed x10, local copies, waits for them, and re-layouts  2.67 us
    pallas_call x1, Pallas kernels, spread_lanes(): pl.pallas_call(functools.partial(table_kernel, width, rolled), out_shape=...  2.06 us
    pallas_call x1, Pallas kernels, transform(): pl.pallas_call(functools.partial(transform_kernel, width, rolled), out_sh...  1.83 us
    pallas_call x1, Pallas kernels, body(): pl.pallas_call(functools.partial(gram_kernel, width, count, devices, scal...  1.36 us
  transfers between devices with their start and end apart: 19, of which 13 were waited for; matrix products, arithmetic and copies ran while one was open for 1% of the time, Pallas kernels for 15%

profile of v5, /device:TPU:0, one launch (start us, length us, event | category | flops | bytes accessed | tf_op | source)
XLA Modules:
  0.0 59.9 jit_solution(874782352650099243)
XLA Ops:
  0.0 3.1 %collective-permute-start = (s32[1024]{0:T(1024)}, s32[1024]{0:T(1024)S(1)}, u32[]{:S(2)}, u32[]{:S(2)}) collective-permute-start(s32[1024]{0:T(1024)} %refs_0_.1), channel_id=1, source_target_pairs={{0,8},{4,12},{8,0},{12,4},{16,24},{20,28},{24,16},{28,20},{1,9},{5... | collective-permute-start | bytes 12296 | tf_op jit(solution)/shard_map/ppermute | solution.py:16
  3.1 1.5 %collective-permute-start.1 = (s32[1024]{0:T(1024)}, s32[1024]{0:T(1024)S(1)}, u32[]{:S(2)}, u32[]{:S(2)}) collective-permute-start(s32[1024]{0:T(1024)} %refs_0_.1), channel_id=1, source_target_pairs={{0,4},{4,0},{8,12},{12,8},{16,20},{20,16},{24,28},{28,24},{1,5},{5... | collective-permute-start | bytes 12296 | tf_op jit(solution)/shard_map/ppermute | solution.py:16
  4.8 2.0 %collective-permute-done.1.refs_0_ = s32[1024]{0:T(1024)S(1)} collective-permute-done((s32[1024]{0:T(1024)}, s32[1024]{0:T(1024)S(1)}, u32[]{:S(2)}, u32[]{:S(2)}) %collective-permute-start.1) | collective-permute-done | bytes 4128 | tf_op jit(solution)/shard_map/ppermute | solution.py:16
  6.9 2.4 %collective-permute-done.2.refs_1_ = s32[1024]{0:T(1024)S(1)} collective-permute-done((s32[1024]{0:T(1024)}, s32[1024]{0:T(1024)S(1)}, u32[]{:S(2)}, u32[]{:S(2)}) %collective-permute-start.2) | collective-permute-done | bytes 4128 | tf_op jit(solution)/shard_map/ppermute | solution.py:16
  10.0 2.6 %collective-permute-start.3 = (s32[4096]{0:T(1024)S(1)}, s32[4096]{0:T(1024)S(1)}, u32[]{:S(2)}, u32[]{:S(2)}) collective-permute-start(s32[4096]{0:T(1024)S(1)} %pad_add_fusion), channel_id=1, source_target_pairs={{0,16},{4,20},{8,24},{12,28},{16,0},{20,4},{24,8},{28,12},{1,17},{... | collective-permute-start | bytes 49160 | tf_op jit(solution)/shard_map/ppermute | solution.py:16
  12.5 1.6 %copy-done = f32[32,16384]{1,0:T(8,128)S(1)} copy-done((f32[32,16384]{1,0:T(8,128)S(1)}, f32[32,16384]{1,0:T(8,128)}, u32[]{:S(2)}) %copy-start) | copy-done | bytes 2097176
  15.0 1.8 %transform.1 = (bf16[2048,256]{1,0:T(8,128)(2,1)S(1)}, f32[2048,128]{1,0:T(8,128)S(1)}) custom-call(f32[32,16384]{1,0:T(8,128)S(1)} %copy-done, s32[128,128]{1,0:T(8,128)S(1)} %bitcast.13), custom_call_target="tpu_custom_call" | custom-call | tf_op jit(solution)/shard_map/transform/pallas_call | solution.py:200
  16.8 2.1 %table.1.refs_2_.refs_3_.refs_1_ = f32[16384,128]{1,0:T(8,128)S(1)} custom-call(bf16[2048,256]{1,0:T(8,128)(2,1)S(1)} %get-tuple-element.14.both_ref, f32[2048,128]{1,0:T(8,128)S(1)} %get-tuple-element.15.mixed_ref), custom_call_target="tpu_custom_call" | custom-call | tf_op jit(solution)/shard_map/table/pallas_call | solution.py:216
  18.9 1.9 %pick.5 = (f32[256,128]{1,0:T(8,128)S(1)}, f32[256,128]{1,0:T(8,128)S(1)}) custom-call(s32[4096]{0:T(1024)S(1)} %collective-permute-done.3.refs_2_.refs_0_, f32[16384,128]{1,0:T(8,128)S(1)} %table.1.refs_2_.refs_3_.refs_1_), custom_call_target="tpu_custom_call" | custom-call | tf_op jit(solution)/shard_map/pick/pallas_call | solution.py:261
  21.4 1.5 %collective-permute-start.9 = (f32[256,128]{1,0:T(8,128)S(1)}, f32[256,128]{1,0:T(8,128)S(1)}, u32[]{:S(2)}, u32[]{:S(2)}) collective-permute-start(f32[256,128]{1,0:T(8,128)S(1)} %get-tuple-element.22), channel_id=1, source_target_pairs={{0,4},{4,0},{8,12},{12,8},{16,20},{20,16},{24,28},{28,24},{1,5},{5... | collective-permute-start | bytes 393224 | tf_op jit(solution)/shard_map/ppermute | solution.py:16
  22.9 3.3 %pick.4 = (f32[512,128]{1,0:T(8,128)S(1)}, f32[256,128]{1,0:T(8,128)S(1)}, f32[256,128]{1,0:T(8,128)S(1)}) custom-call(s32[1024]{0:T(1024)S(1)} %collective-permute-done.1.refs_0_, s32[1024]{0:T(1024)S(1)} %collective-permute-done.2.refs_1_, s32[4096]{0:T(1024)S(1)} %collective-permute-done.3.refs_2_.refs_0_, f32[16384,128]{1,0:T(8,128)S(1)} %table.1.refs_2_.refs_3_.refs_1_), custom_call_target="tpu_custom_call" | custom-call | tf_op jit(solution)/shard_map/pick/pallas_call | solution.py:261
  27.3 1.8 %pick.3 = f32[512,128]{1,0:T(8,128)S(1)} custom-call(s32[1024]{0:T(1024)S(1)} %copy-done.2, s32[1024]{0:T(1024)S(1)} %collective-permute-done.refs_1_, f32[16384,128]{1,0:T(8,128)S(1)} %table.1.refs_2_.refs_3_.refs_1_), custom_call_target="tpu_custom_call" | custom-call | tf_op jit(solution)/shard_map/pick/pallas_call | solution.py:261
  29.2 1.6 %collective-permute-start.10 = (f32[128,128]{1,0:T(8,128)S(1)}, f32[128,128]{1,0:T(8,128)S(1)}, u32[]{:S(2)}, u32[]{:S(2)}) collective-permute-start(f32[128,128]{1,0:T(8,128)S(1)} %slice.75), channel_id=1, source_target_pairs={{0,8},{4,12},{8,0},{12,4},{16,24},{20,28},{24,16},{28,20},{1,9},{5... | collective-permute-start | bytes 196616 | tf_op jit(solution)/shard_map/ppermute | solution.py:16
  31.2 1.9 %collective-permute-done.4 = f32[512,128]{1,0:T(8,128)S(1)} collective-permute-done((f32[512,128]{1,0:T(8,128)S(1)}, f32[512,128]{1,0:T(8,128)S(1)}, u32[]{:S(2)}, u32[]{:S(2)}) %collective-permute-start.4) | collective-permute-done | bytes 262176 | tf_op jit(solution)/shard_map/ppermute | solution.py:16
  33.2 1.6 %collective-permute-start.5 = (f32[256,128]{1,0:T(8,128)S(1)}, f32[256,128]{1,0:T(8,128)S(1)}, u32[]{:S(2)}, u32[]{:S(2)}) collective-permute-start(f32[256,128]{1,0:T(8,128)S(1)} %slice.69), channel_id=1, source_target_pairs={{0,8},{4,12},{8,0},{12,4},{16,24},{20,28},{24,16},{28,20},{1,9},{5... | collective-permute-start | bytes 393224 | tf_op jit(solution)/shard_map/ppermute | solution.py:16
  35.2 3.3 %collective-permute-done.5 = f32[256,128]{1,0:T(8,128)S(1)} collective-permute-done((f32[256,128]{1,0:T(8,128)S(1)}, f32[256,128]{1,0:T(8,128)S(1)}, u32[]{:S(2)}, u32[]{:S(2)}) %collective-permute-start.5) | collective-permute-done | bytes 131104 | tf_op jit(solution)/shard_map/ppermute | solution.py:16
  38.6 1.6 %collective-permute-start.12 = (f32[128,128]{1,0:T(8,128)S(1)}, f32[128,128]{1,0:T(8,128)S(1)}, u32[]{:S(2)}, u32[]{:S(2)}) collective-permute-start(f32[128,128]{1,0:T(8,128)S(1)} %get-tuple-element.19), channel_id=1, source_target_pairs={{0,2},{1,3},{2,0},{3,1},{4,6},{5,7},{6,4},{7,5},{8,10},{9,11},{10,... | collective-permute-start | bytes 196616 | tf_op jit(solution)/shard_map/ppermute | solution.py:16
  40.8 1.6 %collective-permute-start.13 = (f32[128,128]{1,0:T(8,128)S(1)}, f32[128,128]{1,0:T(8,128)S(1)}, u32[]{:S(2)}, u32[]{:S(2)}) collective-permute-start(f32[128,128]{1,0:T(8,128)S(1)} %add.43), channel_id=1, source_target_pairs={{0,2},{1,3},{2,0},{3,1},{4,6},{5,7},{6,4},{7,5},{8,10},{9,11},{10,... | collective-permute-start | bytes 196616 | tf_op jit(solution)/shard_map/ppermute | solution.py:16
  43.0 2.2 %collective-permute-done.13 = f32[128,128]{1,0:T(8,128)S(1)} collective-permute-done((f32[128,128]{1,0:T(8,128)S(1)}, f32[128,128]{1,0:T(8,128)S(1)}, u32[]{:S(2)}, u32[]{:S(2)}) %collective-permute-start.13) | collective-permute-done | bytes 65568 | tf_op jit(solution)/shard_map/ppermute | solution.py:16
  46.8 1.4 %gram.1 = f32[256,128]{1,0:T(8,128)S(1)} custom-call(s32[1024,1]{1,0:T(8,128)S(1)} %copy.5.owner_ref, f32[256,128]{1,0:T(8,128)S(1)} %get-tuple-element.30.refs_0_, f32[256,128]{1,0:T(8,128)S(1)} %get-tuple-element.24.refs_1_, f32[256,128]{1,0:T(8,128)S(1)} %constant_dynamic-update-slice_fusion.refs_2_, f32[256,128]{1,0:T(8,128)S(1)} %get-tuple-element.23.refs_3_), custom_call_target="tpu_custom_call" | custom-call | tf_op jit(solution)/shard_map/gram/pallas_call | solution.py:306
  48.1 1.6 %collective-permute-start.15 = (f32[2,32,128]{2,1,0:T(8,128)S(1)}, f32[2,32,128]{2,1,0:T(8,128)S(1)}, u32[]{:S(2)}, u32[]{:S(2)}) collective-permute-start(f32[2,32,128]{2,1,0:T(8,128)S(1)} %bitcast.17), channel_id=1, source_target_pairs={{0,4},{4,0},{8,12},{12,8},{16,20},{20,16},{24,28},{28,24},{1,5},{5... | collective-permute-start | bytes 98312 | tf_op jit(solution)/shard_map/ppermute | solution.py:16
  49.7 2.0 %collective-permute-start.17 = (f32[2,32,128]{2,1,0:T(8,128)S(1)}, f32[2,32,128]{2,1,0:T(8,128)S(1)}, u32[]{:S(2)}, u32[]{:S(2)}) collective-permute-start(f32[2,32,128]{2,1,0:T(8,128)S(1)} %bitcast.15), channel_id=1, source_target_pairs={{0,12},{4,8},{8,4},{12,0},{16,28},{20,24},{24,20},{28,16},{1,13},{... | collective-permute-start | bytes 98312 | tf_op jit(solution)/shard_map/ppermute | solution.py:16
  52.1 1.5 %collective-permute-done.16 = f32[2,32,128]{2,1,0:T(8,128)S(1)} collective-permute-done((f32[2,32,128]{2,1,0:T(8,128)S(1)}, f32[2,32,128]{2,1,0:T(8,128)S(1)}, u32[]{:S(2)}, u32[]{:S(2)}) %collective-permute-start.16) | collective-permute-done | bytes 32800 | tf_op jit(solution)/shard_map/ppermute | solution.py:16
  55.1 4.2 %collective-permute-done.18 = f32[1,32,128]{2,1,0:T(8,128)S(1)} collective-permute-done((f32[1,32,128]{2,1,0:T(8,128)S(1)}, f32[1,32,128]{2,1,0:T(8,128)S(1)}, u32[]{:S(2)}, u32[]{:S(2)}) %collective-permute-start.18) | collective-permute-done | bytes 16416 | tf_op jit(solution)/shard_map/ppermute | solution.py:16
  (50 shorter events, 9.7 us)
Async XLA Ops:
  0.0 4.8 %collective-permute-start = (s32[1024]{0:T(1024)}, s32[1024]{0:T(1024)S(1)}, u32[]{:S(2)}, u32[]{:S(2)}) collective-permute-start(s32[1024]{0:T(1024)} %refs_0_.1), channel_id=1, source_target_pairs={{0,8},{4,12},{8,0},{12,4},{16,24},{20,28},{24,16},{28,20},{1,9},{5... | collective-permute-start | bytes 12296 | tf_op jit(solution)/shard_map/ppermute | solution.py:16
  3.1 3.8 %collective-permute-start.1 = (s32[1024]{0:T(1024)}, s32[1024]{0:T(1024)S(1)}, u32[]{:S(2)}, u32[]{:S(2)}) collective-permute-start(s32[1024]{0:T(1024)} %refs_0_.1), channel_id=1, source_target_pairs={{0,4},{4,0},{8,12},{12,8},{16,20},{20,16},{24,28},{28,24},{1,5},{5... | collective-permute-start | bytes 12296 | tf_op jit(solution)/shard_map/ppermute | solution.py:16
  4.5 4.7 %collective-permute-start.2 = (s32[1024]{0:T(1024)}, s32[1024]{0:T(1024)S(1)}, u32[]{:S(2)}, u32[]{:S(2)}) collective-permute-start(s32[1024]{0:T(1024)} %refs_0_.1), channel_id=1, source_target_pairs={{0,12},{4,8},{8,4},{12,0},{16,28},{20,24},{24,20},{28,16},{1,13},{... | collective-permute-start | bytes 12296 | tf_op jit(solution)/shard_map/ppermute | solution.py:16
  10.0 8.9 %collective-permute-start.3 = (s32[4096]{0:T(1024)S(1)}, s32[4096]{0:T(1024)S(1)}, u32[]{:S(2)}, u32[]{:S(2)}) collective-permute-start(s32[4096]{0:T(1024)S(1)} %pad_add_fusion), channel_id=1, source_target_pairs={{0,16},{4,20},{8,24},{12,28},{16,0},{20,4},{24,8},{28,12},{1,17},{... | collective-permute-start | bytes 49160 | tf_op jit(solution)/shard_map/ppermute | solution.py:16
  12.5 1.6 %copy-start = (f32[32,16384]{1,0:T(8,128)S(1)}, f32[32,16384]{1,0:T(8,128)}, u32[]{:S(2)}) copy-start(f32[32,16384]{1,0:T(8,128)} %x_ref.1) | copy-start | bytes 6291460
  14.1 0.8 %copy-start.1 = (s32[16384]{0:T(1024)S(1)}, s32[16384]{0:T(1024)}, u32[]{:S(2)}) copy-start(s32[16384]{0:T(1024)} %param.5) | copy-start | bytes 196612
  18.9 8.4 %copy-start.2 = (s32[1024]{0:T(1024)S(1)}, s32[1024]{0:T(1024)}, u32[]{:S(2)}) copy-start(s32[1024]{0:T(1024)} %refs_0_.1) | copy-start | bytes 12292
  20.8 5.4 %collective-permute-start.6 = (f32[256,128]{1,0:T(8,128)S(1)}, f32[256,128]{1,0:T(8,128)S(1)}, u32[]{:S(2)}, u32[]{:S(2)}) collective-permute-start(f32[256,128]{1,0:T(8,128)S(1)} %get-tuple-element.18), channel_id=1, source_target_pairs={{0,4},{4,0},{8,12},{12,8},{16,20},{20,16},{24,28},{28,24},{1,5},{5... | collective-permute-start | bytes 393224 | tf_op jit(solution)/shard_map/ppermute | solution.py:16
  21.4 7.7 %collective-permute-start.9 = (f32[256,128]{1,0:T(8,128)S(1)}, f32[256,128]{1,0:T(8,128)S(1)}, u32[]{:S(2)}, u32[]{:S(2)}) collective-permute-start(f32[256,128]{1,0:T(8,128)S(1)} %get-tuple-element.22), channel_id=1, source_target_pairs={{0,4},{4,0},{8,12},{12,8},{16,20},{20,16},{24,28},{28,24},{1,5},{5... | collective-permute-start | bytes 393224 | tf_op jit(solution)/shard_map/ppermute | solution.py:16
  26.2 19.0 %copy-start.3 = (s32[1024,1]{0,1:T(1,128)S(1)}, s32[1024,1]{0,1:T(1,128)}, u32[]{:S(2)}) copy-start(s32[1024,1]{0,1:T(1,128)} %param.7) | copy-start | bytes 12292
  26.2 4.6 %collective-permute-start.7 = (f32[128,128]{1,0:T(8,128)S(1)}, f32[128,128]{1,0:T(8,128)S(1)}, u32[]{:S(2)}, u32[]{:S(2)}) collective-permute-start(f32[128,128]{1,0:T(8,128)S(1)} %slice.73), channel_id=1, source_target_pairs={{0,8},{4,12},{8,0},{12,4},{16,24},{20,28},{24,16},{28,20},{1,9},{5... | collective-permute-start | bytes 196616 | tf_op jit(solution)/shard_map/ppermute | solution.py:16
  26.8 6.4 %collective-permute-start.4 = (f32[512,128]{1,0:T(8,128)S(1)}, f32[512,128]{1,0:T(8,128)S(1)}, u32[]{:S(2)}, u32[]{:S(2)}) collective-permute-start(f32[512,128]{1,0:T(8,128)S(1)} %get-tuple-element.16), channel_id=1, source_target_pairs={{0,4},{4,0},{8,12},{12,8},{16,20},{20,16},{24,28},{28,24},{1,5},{5... | collective-permute-start | bytes 786440 | tf_op jit(solution)/shard_map/ppermute | solution.py:16
  29.2 5.7 %collective-permute-start.10 = (f32[128,128]{1,0:T(8,128)S(1)}, f32[128,128]{1,0:T(8,128)S(1)}, u32[]{:S(2)}, u32[]{:S(2)}) collective-permute-start(f32[128,128]{1,0:T(8,128)S(1)} %slice.75), channel_id=1, source_target_pairs={{0,8},{4,12},{8,0},{12,4},{16,24},{20,28},{24,16},{28,20},{1,9},{5... | collective-permute-start | bytes 196616 | tf_op jit(solution)/shard_map/ppermute | solution.py:16
  30.8 7.8 %collective-permute-start.8 = (f32[128,128]{1,0:T(8,128)S(1)}, f32[128,128]{1,0:T(8,128)S(1)}, u32[]{:S(2)}, u32[]{:S(2)}) collective-permute-start(f32[128,128]{1,0:T(8,128)S(1)} %slice_add_fusion.2), channel_id=1, source_target_pairs={{0,16},{4,20},{8,24},{12,28},{16,0},{20,4},{24,8},{28,12},{1,17},{... | collective-permute-start | bytes 196616 | tf_op jit(solution)/shard_map/ppermute | solution.py:16
  33.2 5.4 %collective-permute-start.5 = (f32[256,128]{1,0:T(8,128)S(1)}, f32[256,128]{1,0:T(8,128)S(1)}, u32[]{:S(2)}, u32[]{:S(2)}) collective-permute-start(f32[256,128]{1,0:T(8,128)S(1)} %slice.69), channel_id=1, source_target_pairs={{0,8},{4,12},{8,0},{12,4},{16,24},{20,28},{24,16},{28,20},{1,9},{5... | collective-permute-start | bytes 393224 | tf_op jit(solution)/shard_map/ppermute | solution.py:16
  34.8 5.9 %collective-permute-start.11 = (f32[128,128]{1,0:T(8,128)S(1)}, f32[128,128]{1,0:T(8,128)S(1)}, u32[]{:S(2)}, u32[]{:S(2)}) collective-permute-start(f32[128,128]{1,0:T(8,128)S(1)} %slice_add_fusion.1), channel_id=1, source_target_pairs={{0,16},{4,20},{8,24},{12,28},{16,0},{20,4},{24,8},{28,12},{1,17},{... | collective-permute-start | bytes 196616 | tf_op jit(solution)/shard_map/ppermute | solution.py:16
  38.6 4.3 %collective-permute-start.12 = (f32[128,128]{1,0:T(8,128)S(1)}, f32[128,128]{1,0:T(8,128)S(1)}, u32[]{:S(2)}, u32[]{:S(2)}) collective-permute-start(f32[128,128]{1,0:T(8,128)S(1)} %get-tuple-element.19), channel_id=1, source_target_pairs={{0,2},{1,3},{2,0},{3,1},{4,6},{5,7},{6,4},{7,5},{8,10},{9,11},{10,... | collective-permute-start | bytes 196616 | tf_op jit(solution)/shard_map/ppermute | solution.py:16
  40.8 4.3 %collective-permute-start.13 = (f32[128,128]{1,0:T(8,128)S(1)}, f32[128,128]{1,0:T(8,128)S(1)}, u32[]{:S(2)}, u32[]{:S(2)}) collective-permute-start(f32[128,128]{1,0:T(8,128)S(1)} %add.43), channel_id=1, source_target_pairs={{0,2},{1,3},{2,0},{3,1},{4,6},{5,7},{6,4},{7,5},{8,10},{9,11},{10,... | collective-permute-start | bytes 196616 | tf_op jit(solution)/shard_map/ppermute | solution.py:16
  45.1 1.6 %collective-permute-start.14 = (f32[2,256,128]{2,1,0:T(8,128)S(1)}, f32[2,256,128]{2,1,0:T(8,128)S(1)}, u32[]{:S(2)}, u32[]{:S(2)}) collective-permute-start(f32[2,256,128]{2,1,0:T(8,128)S(1)} %pad_maximum_fusion), channel_id=1, source_target_pairs={{0,1},{1,0},{2,3},{3,2},{4,5},{5,4},{6,7},{7,6},{8,9},{9,8},{10,11... | collective-permute-start | bytes 786440 | tf_op jit(solution)/shard_map/ppermute | solution.py:16
  48.1 4.0 %collective-permute-start.15 = (f32[2,32,128]{2,1,0:T(8,128)S(1)}, f32[2,32,128]{2,1,0:T(8,128)S(1)}, u32[]{:S(2)}, u32[]{:S(2)}) collective-permute-start(f32[2,32,128]{2,1,0:T(8,128)S(1)} %bitcast.17), channel_id=1, source_target_pairs={{0,4},{4,0},{8,12},{12,8},{16,20},{20,16},{24,28},{28,24},{1,5},{5... | collective-permute-start | bytes 98312 | tf_op jit(solution)/shard_map/ppermute | solution.py:16
  49.7 3.9 %collective-permute-start.16 = (f32[2,32,128]{2,1,0:T(8,128)S(1)}, f32[2,32,128]{2,1,0:T(8,128)S(1)}, u32[]{:S(2)}, u32[]{:S(2)}) collective-permute-start(f32[2,32,128]{2,1,0:T(8,128)S(1)} %bitcast.16), channel_id=1, source_target_pairs={{0,8},{4,12},{8,0},{12,4},{16,24},{20,28},{24,16},{28,20},{1,9},{5... | collective-permute-start | bytes 98312 | tf_op jit(solution)/shard_map/ppermute | solution.py:16
  49.7 4.8 %collective-permute-start.17 = (f32[2,32,128]{2,1,0:T(8,128)S(1)}, f32[2,32,128]{2,1,0:T(8,128)S(1)}, u32[]{:S(2)}, u32[]{:S(2)}) collective-permute-start(f32[2,32,128]{2,1,0:T(8,128)S(1)} %bitcast.15), channel_id=1, source_target_pairs={{0,12},{4,8},{8,4},{12,0},{16,28},{20,24},{24,20},{28,16},{1,13},{... | collective-permute-start | bytes 98312 | tf_op jit(solution)/shard_map/ppermute | solution.py:16
  54.6 4.7 %collective-permute-start.18 = (f32[1,32,128]{2,1,0:T(8,128)S(1)}, f32[1,32,128]{2,1,0:T(8,128)S(1)}, u32[]{:S(2)}, u32[]{:S(2)}) collective-permute-start(f32[1,32,128]{2,1,0:T(8,128)S(1)} %slice.83), channel_id=1, source_target_pairs={{0,16},{4,20},{8,24},{12,28},{16,0},{20,4},{24,8},{28,12},{1,17},{... | collective-permute-start | bytes 49160 | tf_op jit(solution)/shard_map/ppermute | solution.py:16

commit v6 on v5

--- a/solution.py
+++ b/solution.py
@@ -52,7 +52,7 @@
     return lax.dot_general(hadamard, both, (((1,), (1,)), ((), ())), preferred_element_type=f32)
 
 
-def transform_kernel(width, rolled, x_ref, sign_ref, both_ref, mixed_ref, work_ref):
+def transform_kernel(width, x_ref, sign_ref, both_ref, work_ref):
     bands = width // 8
 
     def first(lo, _):
@@ -68,8 +68,6 @@
         return 0
 
     lax.fori_loop(0, 8, first, 0)
-    hadamard = signs_of(LANES, 2 * LANES)
-    straight = (8 - rolled) * width
 
     def second(hi, _):
         rows = [
@@ -77,29 +75,27 @@
         ]
         y = jnp.concatenate([rows[band][lo] for lo in range(8) for band in range(bands)], axis=0)
         both = jnp.concatenate(halves(y), axis=1)
-        both_ref[pl.ds(pl.multiple_of(hi * straight, 8), straight), :] = both[:straight]
-        if rolled:
-            mixed_ref[pl.ds(pl.multiple_of(hi * LANES, LANES), LANES), :] = times(hadamard, both[straight:])
+        both_ref[pl.ds(pl.multiple_of(hi * 8 * width, LANES), 8 * width), :] = both
         return 0
 
     lax.fori_loop(0, 16, second, 0, unroll=4)
 
 
-def table_kernel(width, rolled, both_ref, mixed_ref, table_ref):
+def table_kernel(width, rolled, both_ref, table_ref):
     group = LANES // width
     lane = lax.broadcasted_iota(jnp.int32, (LANES, LANES), 1) // width
     in_lane = [lane == g for g in range(group)]
     hadamard = signs_of(LANES, 2 * LANES)
-    straight = (8 - rolled) * width
 
     def some(hi, _):
+        top = pl.multiple_of(hi * 8 * width, LANES)
         results = []
         for e in range(0, 8 - rolled, 2):
-            rows = [both_ref[pl.ds(hi * straight + (e + i) * width, width), :] for i in range(2)]
+            rows = [both_ref[pl.ds(top + (e + i) * width, width), :] for i in range(2)]
             mixed = times(hadamard, jnp.concatenate([row for row in rows for _ in range(group)], axis=0))
             results += [mixed[:, :LANES], mixed[:, LANES:]]
         if rolled:
-            mixed = mixed_ref[pl.ds(pl.multiple_of(hi * LANES, LANES), LANES), :]
+            mixed = times(hadamard, both_ref[pl.ds(top + (8 - rolled) * width, LANES), :])
             turned = [mixed] + [pltpu.roll(mixed, k * width, 1) for k in range(1, group)]
             for e in range(group):
                 total = turned[-e % group]
@@ -196,15 +192,11 @@
 
 def transform(panel, signs):
     width, _ = panel.shape
-    rolled = LANES // width if 8 * width > LANES else 0
     return pl.pallas_call(
-        functools.partial(transform_kernel, width, rolled),
-        out_shape=[
-            jax.ShapeDtypeStruct((16 * (8 - rolled) * width, 2 * LANES), bf16),
-            jax.ShapeDtypeStruct((16 * LANES, LANES), f32),
-        ],
+        functools.partial(transform_kernel, width),
+        out_shape=jax.ShapeDtypeStruct((LANES * width, 2 * LANES), bf16),
         in_specs=[VMEM] * 2,
-        out_specs=[VMEM] * 2,
+        out_specs=VMEM,
         scratch_shapes=[pltpu.VMEM((LANES, width, LANES), f32)],
         compiler_params=PARAMS,
         name="transform",
@@ -216,11 +208,11 @@
     return pl.pallas_call(
         functools.partial(table_kernel, width, rolled),
         out_shape=jax.ShapeDtypeStruct((LANES * LANES, LANES), f32),
-        in_specs=[VMEM] * 2,
+        in_specs=[VMEM],
         out_specs=VMEM,
         compiler_params=PARAMS,
         name="table",
-    )(*parts)
+    )(parts)
 
 
 def reverse(i, bits):

time: 60.1 us -> 59.8 us (level)
    pallas_call x1, Pallas kernels: 1.83 us -> 1.04 us  [transform(): pl.pallas_call(functools.partial(transform_kernel, width), out_shape=jax....]
where the time goes in v6:
time: 59.8 us; the launch traced here: 59.6 us
  starting transfers between devices  21.7 us (36%)
  waiting for transfers between devices  21.6 us (36%)
  Pallas kernels  11.9 us (20%)
  local copies, waits for them, and re-layouts  2.73 us (5%)
  other arithmetic  1.47 us (2%)
    ppermute x19, starting transfers between devices, swapped(): lax.ppermute(x, axis, [(i, i ^ distance) for i in range(lax.axis_size(axi...  21.7 us
    ppermute x19, waiting for transfers between devices, swapped(): lax.ppermute(x, axis, [(i, i ^ distance) for i in range(lax.axis_size(axi...  21.6 us
    pallas_call x3, Pallas kernels, pick(): pl.pallas_call(functools.partial(pick_kernel, width, full, count, straigh...  7 us
    unnamed x10, local copies, waits for them, and re-layouts  2.67 us
    pallas_call x1, Pallas kernels, spread_lanes(): pl.pallas_call(functools.partial(table_kernel, width, rolled), out_shape=...  2.54 us
    pallas_call x1, Pallas kernels, body(): pl.pallas_call(functools.partial(gram_kernel, width, count, devices, scal...  1.36 us
  transfers between devices with their start and end apart: 19, of which 13 were waited for; matrix products, arithmetic and copies ran while one was open for 1% of the time, Pallas kernels for 15%

profile of v6, /device:TPU:0, one launch (start us, length us, event | category | flops | bytes accessed | tf_op | source)
XLA Modules:
  0.0 59.6 jit_solution(2285671846314928785)
XLA Ops:
  0.0 3.1 %collective-permute-start = (s32[1024]{0:T(1024)}, s32[1024]{0:T(1024)S(1)}, u32[]{:S(2)}, u32[]{:S(2)}) collective-permute-start(s32[1024]{0:T(1024)} %refs_0_.1), channel_id=1, source_target_pairs={{0,8},{4,12},{8,0},{12,4},{16,24},{20,28},{24,16},{28,20},{1,9},{5... | collective-permute-start | bytes 12296 | tf_op jit(solution)/shard_map/ppermute | solution.py:16
  3.1 1.5 %collective-permute-start.1 = (s32[1024]{0:T(1024)}, s32[1024]{0:T(1024)S(1)}, u32[]{:S(2)}, u32[]{:S(2)}) collective-permute-start(s32[1024]{0:T(1024)} %refs_0_.1), channel_id=1, source_target_pairs={{0,4},{4,0},{8,12},{12,8},{16,20},{20,16},{24,28},{28,24},{1,5},{5... | collective-permute-start | bytes 12296 | tf_op jit(solution)/shard_map/ppermute | solution.py:16
  4.8 2.0 %collective-permute-done.1.refs_0_ = s32[1024]{0:T(1024)S(1)} collective-permute-done((s32[1024]{0:T(1024)}, s32[1024]{0:T(1024)S(1)}, u32[]{:S(2)}, u32[]{:S(2)}) %collective-permute-start.1) | collective-permute-done | bytes 4128 | tf_op jit(solution)/shard_map/ppermute | solution.py:16
  6.9 2.4 %collective-permute-done.2.refs_1_ = s32[1024]{0:T(1024)S(1)} collective-permute-done((s32[1024]{0:T(1024)}, s32[1024]{0:T(1024)S(1)}, u32[]{:S(2)}, u32[]{:S(2)}) %collective-permute-start.2) | collective-permute-done | bytes 4128 | tf_op jit(solution)/shard_map/ppermute | solution.py:16
  10.0 2.6 %collective-permute-start.3 = (s32[4096]{0:T(1024)S(1)}, s32[4096]{0:T(1024)S(1)}, u32[]{:S(2)}, u32[]{:S(2)}) collective-permute-start(s32[4096]{0:T(1024)S(1)} %pad_add_fusion), channel_id=1, source_target_pairs={{0,16},{4,20},{8,24},{12,28},{16,0},{20,4},{24,8},{28,12},{1,17},{... | collective-permute-start | bytes 49160 | tf_op jit(solution)/shard_map/ppermute | solution.py:16
  12.5 1.6 %copy-done = f32[32,16384]{1,0:T(8,128)S(1)} copy-done((f32[32,16384]{1,0:T(8,128)S(1)}, f32[32,16384]{1,0:T(8,128)}, u32[]{:S(2)}) %copy-start) | copy-done | bytes 2097176
  16.0 2.5 %table.1.refs_2_.refs_3_.refs_1_ = f32[16384,128]{1,0:T(8,128)S(1)} custom-call(bf16[4096,256]{1,0:T(8,128)(2,1)S(1)} %transform.1.both_ref), custom_call_target="tpu_custom_call" | custom-call | tf_op jit(solution)/shard_map/table/pallas_call | solution.py:208
  18.6 1.9 %pick.5 = (f32[256,128]{1,0:T(8,128)S(1)}, f32[256,128]{1,0:T(8,128)S(1)}) custom-call(s32[4096]{0:T(1024)S(1)} %collective-permute-done.3.refs_2_.refs_0_, f32[16384,128]{1,0:T(8,128)S(1)} %table.1.refs_2_.refs_3_.refs_1_), custom_call_target="tpu_custom_call" | custom-call | tf_op jit(solution)/shard_map/pick/pallas_call | solution.py:253
  21.1 1.5 %collective-permute-start.9 = (f32[256,128]{1,0:T(8,128)S(1)}, f32[256,128]{1,0:T(8,128)S(1)}, u32[]{:S(2)}, u32[]{:S(2)}) collective-permute-start(f32[256,128]{1,0:T(8,128)S(1)} %get-tuple-element.18), channel_id=1, source_target_pairs={{0,4},{4,0},{8,12},{12,8},{16,20},{20,16},{24,28},{28,24},{1,5},{5... | collective-permute-start | bytes 393224 | tf_op jit(solution)/shard_map/ppermute | solution.py:16
  22.6 3.3 %pick.4 = (f32[512,128]{1,0:T(8,128)S(1)}, f32[256,128]{1,0:T(8,128)S(1)}, f32[256,128]{1,0:T(8,128)S(1)}) custom-call(s32[1024]{0:T(1024)S(1)} %collective-permute-done.1.refs_0_, s32[1024]{0:T(1024)S(1)} %collective-permute-done.2.refs_1_, s32[4096]{0:T(1024)S(1)} %collective-permute-done.3.refs_2_.refs_0_, f32[16384,128]{1,0:T(8,128)S(1)} %table.1.refs_2_.refs_3_.refs_1_), custom_call_target="tpu_custom_call" | custom-call | tf_op jit(solution)/shard_map/pick/pallas_call | solution.py:253
  27.0 1.8 %pick.3 = f32[512,128]{1,0:T(8,128)S(1)} custom-call(s32[1024]{0:T(1024)S(1)} %copy-done.2, s32[1024]{0:T(1024)S(1)} %collective-permute-done.refs_1_, f32[16384,128]{1,0:T(8,128)S(1)} %table.1.refs_2_.refs_3_.refs_1_), custom_call_target="tpu_custom_call" | custom-call | tf_op jit(solution)/shard_map/pick/pallas_call | solution.py:253
  28.9 1.6 %collective-permute-start.10 = (f32[128,128]{1,0:T(8,128)S(1)}, f32[128,128]{1,0:T(8,128)S(1)}, u32[]{:S(2)}, u32[]{:S(2)}) collective-permute-start(f32[128,128]{1,0:T(8,128)S(1)} %slice.75), channel_id=1, source_target_pairs={{0,8},{4,12},{8,0},{12,4},{16,24},{20,28},{24,16},{28,20},{1,9},{5... | collective-permute-start | bytes 196616 | tf_op jit(solution)/shard_map/ppermute | solution.py:16
  30.9 1.9 %collective-permute-done.4 = f32[512,128]{1,0:T(8,128)S(1)} collective-permute-done((f32[512,128]{1,0:T(8,128)S(1)}, f32[512,128]{1,0:T(8,128)S(1)}, u32[]{:S(2)}, u32[]{:S(2)}) %collective-permute-start.4) | collective-permute-done | bytes 262176 | tf_op jit(solution)/shard_map/ppermute | solution.py:16
  32.8 1.6 %collective-permute-start.5 = (f32[256,128]{1,0:T(8,128)S(1)}, f32[256,128]{1,0:T(8,128)S(1)}, u32[]{:S(2)}, u32[]{:S(2)}) collective-permute-start(f32[256,128]{1,0:T(8,128)S(1)} %slice.69), channel_id=1, source_target_pairs={{0,8},{4,12},{8,0},{12,4},{16,24},{20,28},{24,16},{28,20},{1,9},{5... | collective-permute-start | bytes 393224 | tf_op jit(solution)/shard_map/ppermute | solution.py:16
  34.9 3.3 %collective-permute-done.5 = f32[256,128]{1,0:T(8,128)S(1)} collective-permute-done((f32[256,128]{1,0:T(8,128)S(1)}, f32[256,128]{1,0:T(8,128)S(1)}, u32[]{:S(2)}, u32[]{:S(2)}) %collective-permute-start.5) | collective-permute-done | bytes 131104 | tf_op jit(solution)/shard_map/ppermute | solution.py:16
  38.3 1.6 %collective-permute-start.12 = (f32[128,128]{1,0:T(8,128)S(1)}, f32[128,128]{1,0:T(8,128)S(1)}, u32[]{:S(2)}, u32[]{:S(2)}) collective-permute-start(f32[128,128]{1,0:T(8,128)S(1)} %get-tuple-element.15), channel_id=1, source_target_pairs={{0,2},{1,3},{2,0},{3,1},{4,6},{5,7},{6,4},{7,5},{8,10},{9,11},{10,... | collective-permute-start | bytes 196616 | tf_op jit(solution)/shard_map/ppermute | solution.py:16
  40.4 1.6 %collective-permute-start.13 = (f32[128,128]{1,0:T(8,128)S(1)}, f32[128,128]{1,0:T(8,128)S(1)}, u32[]{:S(2)}, u32[]{:S(2)}) collective-permute-start(f32[128,128]{1,0:T(8,128)S(1)} %add.43), channel_id=1, source_target_pairs={{0,2},{1,3},{2,0},{3,1},{4,6},{5,7},{6,4},{7,5},{8,10},{9,11},{10,... | collective-permute-start | bytes 196616 | tf_op jit(solution)/shard_map/ppermute | solution.py:16
  42.6 2.1 %collective-permute-done.13 = f32[128,128]{1,0:T(8,128)S(1)} collective-permute-done((f32[128,128]{1,0:T(8,128)S(1)}, f32[128,128]{1,0:T(8,128)S(1)}, u32[]{:S(2)}, u32[]{:S(2)}) %collective-permute-start.13) | collective-permute-done | bytes 65568 | tf_op jit(solution)/shard_map/ppermute | solution.py:16
  45.1 1.3 %collective-permute-done.14 = f32[2,256,128]{2,1,0:T(8,128)S(1)} collective-permute-done((f32[2,256,128]{2,1,0:T(8,128)S(1)}, f32[2,256,128]{2,1,0:T(8,128)S(1)}, u32[]{:S(2)}, u32[]{:S(2)}) %collective-permute-start.14) | collective-permute-done | bytes 262176 | tf_op jit(solution)/shard_map/ppermute | solution.py:16
  46.4 1.4 %gram.1 = f32[256,128]{1,0:T(8,128)S(1)} custom-call(s32[1024,1]{1,0:T(8,128)S(1)} %copy.5.owner_ref, f32[256,128]{1,0:T(8,128)S(1)} %get-tuple-element.26.refs_0_, f32[256,128]{1,0:T(8,128)S(1)} %get-tuple-element.20.refs_1_, f32[256,128]{1,0:T(8,128)S(1)} %constant_dynamic-update-slice_fusion.refs_2_, f32[256,128]{1,0:T(8,128)S(1)} %get-tuple-element.19.refs_3_), custom_call_target="tpu_custom_call" | custom-call | tf_op jit(solution)/shard_map/gram/pallas_call | solution.py:298
  47.8 1.6 %collective-permute-start.15 = (f32[2,32,128]{2,1,0:T(8,128)S(1)}, f32[2,32,128]{2,1,0:T(8,128)S(1)}, u32[]{:S(2)}, u32[]{:S(2)}) collective-permute-start(f32[2,32,128]{2,1,0:T(8,128)S(1)} %bitcast.17), channel_id=1, source_target_pairs={{0,4},{4,0},{8,12},{12,8},{16,20},{20,16},{24,28},{28,24},{1,5},{5... | collective-permute-start | bytes 98312 | tf_op jit(solution)/shard_map/ppermute | solution.py:16
  49.4 2.0 %collective-permute-start.17 = (f32[2,32,128]{2,1,0:T(8,128)S(1)}, f32[2,32,128]{2,1,0:T(8,128)S(1)}, u32[]{:S(2)}, u32[]{:S(2)}) collective-permute-start(f32[2,32,128]{2,1,0:T(8,128)S(1)} %bitcast.15), channel_id=1, source_target_pairs={{0,12},{4,8},{8,4},{12,0},{16,28},{20,24},{24,20},{28,16},{1,13},{... | collective-permute-start | bytes 98312 | tf_op jit(solution)/shard_map/ppermute | solution.py:16
  51.8 1.5 %collective-permute-done.16 = f32[2,32,128]{2,1,0:T(8,128)S(1)} collective-permute-done((f32[2,32,128]{2,1,0:T(8,128)S(1)}, f32[2,32,128]{2,1,0:T(8,128)S(1)}, u32[]{:S(2)}, u32[]{:S(2)}) %collective-permute-start.16) | collective-permute-done | bytes 32800 | tf_op jit(solution)/shard_map/ppermute | solution.py:16
  54.8 4.2 %collective-permute-done.18 = f32[1,32,128]{2,1,0:T(8,128)S(1)} collective-permute-done((f32[1,32,128]{2,1,0:T(8,128)S(1)}, f32[1,32,128]{2,1,0:T(8,128)S(1)}, u32[]{:S(2)}, u32[]{:S(2)}) %collective-permute-start.18) | collective-permute-done | bytes 16416 | tf_op jit(solution)/shard_map/ppermute | solution.py:16
  (50 shorter events, 9.4 us)
Async XLA Ops:
  0.0 4.8 %collective-permute-start = (s32[1024]{0:T(1024)}, s32[1024]{0:T(1024)S(1)}, u32[]{:S(2)}, u32[]{:S(2)}) collective-permute-start(s32[1024]{0:T(1024)} %refs_0_.1), channel_id=1, source_target_pairs={{0,8},{4,12},{8,0},{12,4},{16,24},{20,28},{24,16},{28,20},{1,9},{5... | collective-permute-start | bytes 12296 | tf_op jit(solution)/shard_map/ppermute | solution.py:16
  3.1 3.8 %collective-permute-start.1 = (s32[1024]{0:T(1024)}, s32[1024]{0:T(1024)S(1)}, u32[]{:S(2)}, u32[]{:S(2)}) collective-permute-start(s32[1024]{0:T(1024)} %refs_0_.1), channel_id=1, source_target_pairs={{0,4},{4,0},{8,12},{12,8},{16,20},{20,16},{24,28},{28,24},{1,5},{5... | collective-permute-start | bytes 12296 | tf_op jit(solution)/shard_map/ppermute | solution.py:16
  4.5 4.7 %collective-permute-start.2 = (s32[1024]{0:T(1024)}, s32[1024]{0:T(1024)S(1)}, u32[]{:S(2)}, u32[]{:S(2)}) collective-permute-start(s32[1024]{0:T(1024)} %refs_0_.1), channel_id=1, source_target_pairs={{0,12},{4,8},{8,4},{12,0},{16,28},{20,24},{24,20},{28,16},{1,13},{... | collective-permute-start | bytes 12296 | tf_op jit(solution)/shard_map/ppermute | solution.py:16
  10.0 8.6 %collective-permute-start.3 = (s32[4096]{0:T(1024)S(1)}, s32[4096]{0:T(1024)S(1)}, u32[]{:S(2)}, u32[]{:S(2)}) collective-permute-start(s32[4096]{0:T(1024)S(1)} %pad_add_fusion), channel_id=1, source_target_pairs={{0,16},{4,20},{8,24},{12,28},{16,0},{20,4},{24,8},{28,12},{1,17},{... | collective-permute-start | bytes 49160 | tf_op jit(solution)/shard_map/ppermute | solution.py:16
  12.5 1.6 %copy-start = (f32[32,16384]{1,0:T(8,128)S(1)}, f32[32,16384]{1,0:T(8,128)}, u32[]{:S(2)}) copy-start(f32[32,16384]{1,0:T(8,128)} %x_ref.1) | copy-start | bytes 6291460
  14.1 0.8 %copy-start.1 = (s32[16384]{0:T(1024)S(1)}, s32[16384]{0:T(1024)}, u32[]{:S(2)}) copy-start(s32[16384]{0:T(1024)} %param.5) | copy-start | bytes 196612
  20.5 5.4 %collective-permute-start.6 = (f32[256,128]{1,0:T(8,128)S(1)}, f32[256,128]{1,0:T(8,128)S(1)}, u32[]{:S(2)}, u32[]{:S(2)}) collective-permute-start(f32[256,128]{1,0:T(8,128)S(1)} %get-tuple-element.14), channel_id=1, source_target_pairs={{0,4},{4,0},{8,12},{12,8},{16,20},{20,16},{24,28},{28,24},{1,5},{5... | collective-permute-start | bytes 393224 | tf_op jit(solution)/shard_map/ppermute | solution.py:16
  21.1 5.9 %copy-start.2 = (s32[1024]{0:T(1024)S(1)}, s32[1024]{0:T(1024)}, u32[]{:S(2)}) copy-start(s32[1024]{0:T(1024)} %refs_0_.1) | copy-start | bytes 12292
  21.1 7.7 %collective-permute-start.9 = (f32[256,128]{1,0:T(8,128)S(1)}, f32[256,128]{1,0:T(8,128)S(1)}, u32[]{:S(2)}, u32[]{:S(2)}) collective-permute-start(f32[256,128]{1,0:T(8,128)S(1)} %get-tuple-element.18), channel_id=1, source_target_pairs={{0,4},{4,0},{8,12},{12,8},{16,20},{20,16},{24,28},{28,24},{1,5},{5... | collective-permute-start | bytes 393224 | tf_op jit(solution)/shard_map/ppermute | solution.py:16
  25.9 4.6 %collective-permute-start.7 = (f32[128,128]{1,0:T(8,128)S(1)}, f32[128,128]{1,0:T(8,128)S(1)}, u32[]{:S(2)}, u32[]{:S(2)}) collective-permute-start(f32[128,128]{1,0:T(8,128)S(1)} %slice.73), channel_id=1, source_target_pairs={{0,8},{4,12},{8,0},{12,4},{16,24},{20,28},{24,16},{28,20},{1,9},{5... | collective-permute-start | bytes 196616 | tf_op jit(solution)/shard_map/ppermute | solution.py:16
  26.4 6.4 %collective-permute-start.4 = (f32[512,128]{1,0:T(8,128)S(1)}, f32[512,128]{1,0:T(8,128)S(1)}, u32[]{:S(2)}, u32[]{:S(2)}) collective-permute-start(f32[512,128]{1,0:T(8,128)S(1)} %get-tuple-element.12), channel_id=1, source_target_pairs={{0,4},{4,0},{8,12},{12,8},{16,20},{20,16},{24,28},{28,24},{1,5},{5... | collective-permute-start | bytes 786440 | tf_op jit(solution)/shard_map/ppermute | solution.py:16
  28.8 16.1 %copy-start.3 = (s32[1024,1]{0,1:T(1,128)S(1)}, s32[1024,1]{0,1:T(1,128)}, u32[]{:S(2)}) copy-start(s32[1024,1]{0,1:T(1,128)} %param.7) | copy-start | bytes 12292
  28.9 5.6 %collective-permute-start.10 = (f32[128,128]{1,0:T(8,128)S(1)}, f32[128,128]{1,0:T(8,128)S(1)}, u32[]{:S(2)}, u32[]{:S(2)}) collective-permute-start(f32[128,128]{1,0:T(8,128)S(1)} %slice.75), channel_id=1, source_target_pairs={{0,8},{4,12},{8,0},{12,4},{16,24},{20,28},{24,16},{28,20},{1,9},{5... | collective-permute-start | bytes 196616 | tf_op jit(solution)/shard_map/ppermute | solution.py:16
  30.5 7.8 %collective-permute-start.8 = (f32[128,128]{1,0:T(8,128)S(1)}, f32[128,128]{1,0:T(8,128)S(1)}, u32[]{:S(2)}, u32[]{:S(2)}) collective-permute-start(f32[128,128]{1,0:T(8,128)S(1)} %slice_add_fusion.2), channel_id=1, source_target_pairs={{0,16},{4,20},{8,24},{12,28},{16,0},{20,4},{24,8},{28,12},{1,17},{... | collective-permute-start | bytes 196616 | tf_op jit(solution)/shard_map/ppermute | solution.py:16
  32.8 5.4 %collective-permute-start.5 = (f32[256,128]{1,0:T(8,128)S(1)}, f32[256,128]{1,0:T(8,128)S(1)}, u32[]{:S(2)}, u32[]{:S(2)}) collective-permute-start(f32[256,128]{1,0:T(8,128)S(1)} %slice.69), channel_id=1, source_target_pairs={{0,8},{4,12},{8,0},{12,4},{16,24},{20,28},{24,16},{28,20},{1,9},{5... | collective-permute-start | bytes 393224 | tf_op jit(solution)/shard_map/ppermute | solution.py:16
  34.5 5.9 %collective-permute-start.11 = (f32[128,128]{1,0:T(8,128)S(1)}, f32[128,128]{1,0:T(8,128)S(1)}, u32[]{:S(2)}, u32[]{:S(2)}) collective-permute-start(f32[128,128]{1,0:T(8,128)S(1)} %slice_add_fusion.1), channel_id=1, source_target_pairs={{0,16},{4,20},{8,24},{12,28},{16,0},{20,4},{24,8},{28,12},{1,17},{... | collective-permute-start | bytes 196616 | tf_op jit(solution)/shard_map/ppermute | solution.py:16
  38.3 4.3 %collective-permute-start.12 = (f32[128,128]{1,0:T(8,128)S(1)}, f32[128,128]{1,0:T(8,128)S(1)}, u32[]{:S(2)}, u32[]{:S(2)}) collective-permute-start(f32[128,128]{1,0:T(8,128)S(1)} %get-tuple-element.15), channel_id=1, source_target_pairs={{0,2},{1,3},{2,0},{3,1},{4,6},{5,7},{6,4},{7,5},{8,10},{9,11},{10,... | collective-permute-start | bytes 196616 | tf_op jit(solution)/shard_map/ppermute | solution.py:16
  40.4 4.3 %collective-permute-start.13 = (f32[128,128]{1,0:T(8,128)S(1)}, f32[128,128]{1,0:T(8,128)S(1)}, u32[]{:S(2)}, u32[]{:S(2)}) collective-permute-start(f32[128,128]{1,0:T(8,128)S(1)} %add.43), channel_id=1, source_target_pairs={{0,2},{1,3},{2,0},{3,1},{4,6},{5,7},{6,4},{7,5},{8,10},{9,11},{10,... | collective-permute-start | bytes 196616 | tf_op jit(solution)/shard_map/ppermute | solution.py:16
  44.8 1.6 %collective-permute-start.14 = (f32[2,256,128]{2,1,0:T(8,128)S(1)}, f32[2,256,128]{2,1,0:T(8,128)S(1)}, u32[]{:S(2)}, u32[]{:S(2)}) collective-permute-start(f32[2,256,128]{2,1,0:T(8,128)S(1)} %pad_maximum_fusion), channel_id=1, source_target_pairs={{0,1},{1,0},{2,3},{3,2},{4,5},{5,4},{6,7},{7,6},{8,9},{9,8},{10,11... | collective-permute-start | bytes 786440 | tf_op jit(solution)/shard_map/ppermute | solution.py:16
  47.8 4.0 %collective-permute-start.15 = (f32[2,32,128]{2,1,0:T(8,128)S(1)}, f32[2,32,128]{2,1,0:T(8,128)S(1)}, u32[]{:S(2)}, u32[]{:S(2)}) collective-permute-start(f32[2,32,128]{2,1,0:T(8,128)S(1)} %bitcast.17), channel_id=1, source_target_pairs={{0,4},{4,0},{8,12},{12,8},{16,20},{20,16},{24,28},{28,24},{1,5},{5... | collective-permute-start | bytes 98312 | tf_op jit(solution)/shard_map/ppermute | solution.py:16
  49.4 3.9 %collective-permute-start.16 = (f32[2,32,128]{2,1,0:T(8,128)S(1)}, f32[2,32,128]{2,1,0:T(8,128)S(1)}, u32[]{:S(2)}, u32[]{:S(2)}) collective-permute-start(f32[2,32,128]{2,1,0:T(8,128)S(1)} %bitcast.16), channel_id=1, source_target_pairs={{0,8},{4,12},{8,0},{12,4},{16,24},{20,28},{24,16},{28,20},{1,9},{5... | collective-permute-start | bytes 98312 | tf_op jit(solution)/shard_map/ppermute | solution.py:16
  49.4 4.8 %collective-permute-start.17 = (f32[2,32,128]{2,1,0:T(8,128)S(1)}, f32[2,32,128]{2,1,0:T(8,128)S(1)}, u32[]{:S(2)}, u32[]{:S(2)}) collective-permute-start(f32[2,32,128]{2,1,0:T(8,128)S(1)} %bitcast.15), channel_id=1, source_target_pairs={{0,12},{4,8},{8,4},{12,0},{16,28},{20,24},{24,20},{28,16},{1,13},{... | collective-permute-start | bytes 98312 | tf_op jit(solution)/shard_map/ppermute | solution.py:16
  54.2 4.7 %collective-permute-start.18 = (f32[1,32,128]{2,1,0:T(8,128)S(1)}, f32[1,32,128]{2,1,0:T(8,128)S(1)}, u32[]{:S(2)}, u32[]{:S(2)}) collective-permute-start(f32[1,32,128]{2,1,0:T(8,128)S(1)} %slice.83), channel_id=1, source_target_pairs={{0,16},{4,20},{8,24},{12,28},{16,0},{20,4},{24,8},{28,12},{1,17},{... | collective-permute-start | bytes 49160 | tf_op jit(solution)/shard_map/ppermute | solution.py:16

commit v7 on v6

--- a/solution.py
+++ b/solution.py
@@ -52,7 +52,7 @@
     return lax.dot_general(hadamard, both, (((1,), (1,)), ((), ())), preferred_element_type=f32)
 
 
-def transform_kernel(width, x_ref, sign_ref, both_ref, work_ref):
+def transform_kernel(width, rolled, x_ref, sign_ref, part_ref, work_ref):
     bands = width // 8
 
     def first(lo, _):
@@ -68,20 +68,25 @@
         return 0
 
     lax.fori_loop(0, 8, first, 0)
+    hadamard = signs_of(LANES, 2 * LANES)
+    straight = (8 - rolled) * width
 
     def second(hi, _):
         rows = [
             butterflies([work_ref[hi * 8 + lo, pl.ds(band * 8, 8), :] for lo in range(8)]) for band in range(bands)
         ]
         y = jnp.concatenate([rows[band][lo] for lo in range(8) for band in range(bands)], axis=0)
-        both = jnp.concatenate(halves(y), axis=1)
-        both_ref[pl.ds(pl.multiple_of(hi * 8 * width, LANES), 8 * width), :] = both
+        top = pl.multiple_of(hi * 8 * width, LANES)
+        part_ref[pl.ds(top, straight), :] = y[:straight]
+        if rolled:
+            both = jnp.concatenate(halves(y[straight:]), axis=1)
+            part_ref[pl.ds(top + straight, LANES), :] = times(hadamard, both)
         return 0
 
     lax.fori_loop(0, 16, second, 0, unroll=4)
 
 
-def table_kernel(width, rolled, both_ref, table_ref):
+def table_kernel(width, rolled, part_ref, table_ref):
     group = LANES // width
     lane = lax.broadcasted_iota(jnp.int32, (LANES, LANES), 1) // width
     in_lane = [lane == g for g in range(group)]
@@ -91,11 +96,13 @@
         top = pl.multiple_of(hi * 8 * width, LANES)
         results = []
         for e in range(0, 8 - rolled, 2):
-            rows = [both_ref[pl.ds(top + (e + i) * width, width), :] for i in range(2)]
+            rows = [
+                jnp.concatenate(halves(part_ref[pl.ds(top + (e + i) * width, width), :]), axis=1) for i in range(2)
+            ]
             mixed = times(hadamard, jnp.concatenate([row for row in rows for _ in range(group)], axis=0))
             results += [mixed[:, :LANES], mixed[:, LANES:]]
         if rolled:
-            mixed = times(hadamard, both_ref[pl.ds(top + (8 - rolled) * width, LANES), :])
+            mixed = part_ref[pl.ds(top + (8 - rolled) * width, LANES), :]
             turned = [mixed] + [pltpu.roll(mixed, k * width, 1) for k in range(1, group)]
             for e in range(group):
                 total = turned[-e % group]
@@ -174,10 +181,10 @@
     for block in range(named * width // LANES):
         match = whose == tall + block * group
         left = jnp.where(match, mine_top, zero)
-        gram = lax.dot_general(left, top, over, preferred_element_type=f32)
-        gram = gram + lax.dot_general(left, low, over, preferred_element_type=f32)
+        gram = lax.dot_general(top, left, over, preferred_element_type=f32)
+        gram = gram + lax.dot_general(low, left, over, preferred_element_type=f32)
         left = jnp.where(match, mine_low, zero)
-        gram = gram + lax.dot_general(left, top, over, preferred_element_type=f32)
+        gram = (gram + lax.dot_general(top, left, over, preferred_element_type=f32)).T
         gram = jnp.take_along_axis(gram, turned, axis=1) * scale
         for k in range(group):
             slot = (block * group + k) ^ me
@@ -192,9 +199,10 @@
 
 def transform(panel, signs):
     width, _ = panel.shape
+    rolled = LANES // width if 8 * width > LANES else 0
     return pl.pallas_call(
-        functools.partial(transform_kernel, width),
-        out_shape=jax.ShapeDtypeStruct((LANES * width, 2 * LANES), bf16),
+        functools.partial(transform_kernel, width, rolled),
+        out_shape=jax.ShapeDtypeStruct((LANES * width, LANES), f32),
         in_specs=[VMEM] * 2,
         out_specs=VMEM,
         scratch_shapes=[pltpu.VMEM((LANES, width, LANES), f32)],

time: 59.8 us -> 60.1 us (level)
    pallas_call x1, Pallas kernels: 1.04 us -> 1.71 us  [transform(): pl.pallas_call(functools.partial(transform_kernel, width, rolled), out_sh...]
where the time goes in v7:
time: 60.1 us; the launch traced here: 59.9 us
  starting transfers between devices  21.7 us (36%)
  waiting for transfers between devices  21.6 us (36%)
  Pallas kernels  12.3 us (20%)
  local copies, waits for them, and re-layouts  2.73 us (5%)
  other arithmetic  1.47 us (2%)
    ppermute x19, starting transfers between devices, swapped(): lax.ppermute(x, axis, [(i, i ^ distance) for i in range(lax.axis_size(axi...  21.7 us
    ppermute x19, waiting for transfers between devices, swapped(): lax.ppermute(x, axis, [(i, i ^ distance) for i in range(lax.axis_size(axi...  21.6 us
    pallas_call x3, Pallas kernels, pick(): pl.pallas_call(functools.partial(pick_kernel, width, full, count, straigh...  7 us
    unnamed x10, local copies, waits for them, and re-layouts  2.67 us
    pallas_call x1, Pallas kernels, spread_lanes(): pl.pallas_call(functools.partial(table_kernel, width, rolled), out_shape=...  2.08 us
    pallas_call x1, Pallas kernels, transform(): pl.pallas_call(functools.partial(transform_kernel, width, rolled), out_sh...  1.71 us
    pallas_call x1, Pallas kernels, body(): pl.pallas_call(functools.partial(gram_kernel, width, count, devices, scal...  1.48 us
  transfers between devices with their start and end apart: 19, of which 13 were waited for; matrix products, arithmetic and copies ran while one was open for 1% of the time, Pallas kernels for 15%

profile of v7, /device:TPU:0, one launch (start us, length us, event | category | flops | bytes accessed | tf_op | source)
XLA Modules:
  0.0 59.9 jit_solution(7659594197373795397)
XLA Ops:
  0.0 3.1 %collective-permute-start = (s32[1024]{0:T(1024)}, s32[1024]{0:T(1024)S(1)}, u32[]{:S(2)}, u32[]{:S(2)}) collective-permute-start(s32[1024]{0:T(1024)} %refs_0_.1), channel_id=1, source_target_pairs={{0,8},{4,12},{8,0},{12,4},{16,24},{20,28},{24,16},{28,20},{1,9},{5... | collective-permute-start | bytes 12296 | tf_op jit(solution)/shard_map/ppermute | solution.py:16
  3.1 1.5 %collective-permute-start.1 = (s32[1024]{0:T(1024)}, s32[1024]{0:T(1024)S(1)}, u32[]{:S(2)}, u32[]{:S(2)}) collective-permute-start(s32[1024]{0:T(1024)} %refs_0_.1), channel_id=1, source_target_pairs={{0,4},{4,0},{8,12},{12,8},{16,20},{20,16},{24,28},{28,24},{1,5},{5... | collective-permute-start | bytes 12296 | tf_op jit(solution)/shard_map/ppermute | solution.py:16
  4.8 2.0 %collective-permute-done.1.refs_0_ = s32[1024]{0:T(1024)S(1)} collective-permute-done((s32[1024]{0:T(1024)}, s32[1024]{0:T(1024)S(1)}, u32[]{:S(2)}, u32[]{:S(2)}) %collective-permute-start.1) | collective-permute-done | bytes 4128 | tf_op jit(solution)/shard_map/ppermute | solution.py:16
  6.9 2.4 %collective-permute-done.2.refs_1_ = s32[1024]{0:T(1024)S(1)} collective-permute-done((s32[1024]{0:T(1024)}, s32[1024]{0:T(1024)S(1)}, u32[]{:S(2)}, u32[]{:S(2)}) %collective-permute-start.2) | collective-permute-done | bytes 4128 | tf_op jit(solution)/shard_map/ppermute | solution.py:16
  10.0 2.6 %collective-permute-start.3 = (s32[4096]{0:T(1024)S(1)}, s32[4096]{0:T(1024)S(1)}, u32[]{:S(2)}, u32[]{:S(2)}) collective-permute-start(s32[4096]{0:T(1024)S(1)} %pad_add_fusion), channel_id=1, source_target_pairs={{0,16},{4,20},{8,24},{12,28},{16,0},{20,4},{24,8},{28,12},{1,17},{... | collective-permute-start | bytes 49160 | tf_op jit(solution)/shard_map/ppermute | solution.py:16
  12.5 1.6 %copy-done = f32[32,16384]{1,0:T(8,128)S(1)} copy-done((f32[32,16384]{1,0:T(8,128)S(1)}, f32[32,16384]{1,0:T(8,128)}, u32[]{:S(2)}) %copy-start) | copy-done | bytes 2097176
  15.0 1.7 %transform.1.part_ref = f32[4096,128]{1,0:T(8,128)S(1)} custom-call(f32[32,16384]{1,0:T(8,128)S(1)} %copy-done, s32[128,128]{1,0:T(8,128)S(1)} %bitcast.13), custom_call_target="tpu_custom_call" | custom-call | tf_op jit(solution)/shard_map/transform/pallas_call | solution.py:203
  16.7 2.1 %table.1.refs_2_.refs_3_.refs_1_ = f32[16384,128]{1,0:T(8,128)S(1)} custom-call(f32[4096,128]{1,0:T(8,128)S(1)} %transform.1.part_ref), custom_call_target="tpu_custom_call" | custom-call | tf_op jit(solution)/shard_map/table/pallas_call | solution.py:216
  18.8 1.9 %pick.5 = (f32[256,128]{1,0:T(8,128)S(1)}, f32[256,128]{1,0:T(8,128)S(1)}) custom-call(s32[4096]{0:T(1024)S(1)} %collective-permute-done.3.refs_2_.refs_0_, f32[16384,128]{1,0:T(8,128)S(1)} %table.1.refs_2_.refs_3_.refs_1_), custom_call_target="tpu_custom_call" | custom-call | tf_op jit(solution)/shard_map/pick/pallas_call | solution.py:261
  21.3 1.5 %collective-permute-start.9 = (f32[256,128]{1,0:T(8,128)S(1)}, f32[256,128]{1,0:T(8,128)S(1)}, u32[]{:S(2)}, u32[]{:S(2)}) collective-permute-start(f32[256,128]{1,0:T(8,128)S(1)} %get-tuple-element.18), channel_id=1, source_target_pairs={{0,4},{4,0},{8,12},{12,8},{16,20},{20,16},{24,28},{28,24},{1,5},{5... | collective-permute-start | bytes 393224 | tf_op jit(solution)/shard_map/ppermute | solution.py:16
  22.8 3.3 %pick.4 = (f32[512,128]{1,0:T(8,128)S(1)}, f32[256,128]{1,0:T(8,128)S(1)}, f32[256,128]{1,0:T(8,128)S(1)}) custom-call(s32[1024]{0:T(1024)S(1)} %collective-permute-done.1.refs_0_, s32[1024]{0:T(1024)S(1)} %collective-permute-done.2.refs_1_, s32[4096]{0:T(1024)S(1)} %collective-permute-done.3.refs_2_.refs_0_, f32[16384,128]{1,0:T(8,128)S(1)} %table.1.refs_2_.refs_3_.refs_1_), custom_call_target="tpu_custom_call" | custom-call | tf_op jit(solution)/shard_map/pick/pallas_call | solution.py:261
  27.2 1.8 %pick.3 = f32[512,128]{1,0:T(8,128)S(1)} custom-call(s32[1024]{0:T(1024)S(1)} %copy-done.2, s32[1024]{0:T(1024)S(1)} %collective-permute-done.refs_1_, f32[16384,128]{1,0:T(8,128)S(1)} %table.1.refs_2_.refs_3_.refs_1_), custom_call_target="tpu_custom_call" | custom-call | tf_op jit(solution)/shard_map/pick/pallas_call | solution.py:261
  29.1 1.6 %collective-permute-start.10 = (f32[128,128]{1,0:T(8,128)S(1)}, f32[128,128]{1,0:T(8,128)S(1)}, u32[]{:S(2)}, u32[]{:S(2)}) collective-permute-start(f32[128,128]{1,0:T(8,128)S(1)} %slice.75), channel_id=1, source_target_pairs={{0,8},{4,12},{8,0},{12,4},{16,24},{20,28},{24,16},{28,20},{1,9},{5... | collective-permute-start | bytes 196616 | tf_op jit(solution)/shard_map/ppermute | solution.py:16
  31.1 1.9 %collective-permute-done.4 = f32[512,128]{1,0:T(8,128)S(1)} collective-permute-done((f32[512,128]{1,0:T(8,128)S(1)}, f32[512,128]{1,0:T(8,128)S(1)}, u32[]{:S(2)}, u32[]{:S(2)}) %collective-permute-start.4) | collective-permute-done | bytes 262176 | tf_op jit(solution)/shard_map/ppermute | solution.py:16
  33.1 1.6 %collective-permute-start.5 = (f32[256,128]{1,0:T(8,128)S(1)}, f32[256,128]{1,0:T(8,128)S(1)}, u32[]{:S(2)}, u32[]{:S(2)}) collective-permute-start(f32[256,128]{1,0:T(8,128)S(1)} %slice.69), channel_id=1, source_target_pairs={{0,8},{4,12},{8,0},{12,4},{16,24},{20,28},{24,16},{28,20},{1,9},{5... | collective-permute-start | bytes 393224 | tf_op jit(solution)/shard_map/ppermute | solution.py:16
  35.1 3.3 %collective-permute-done.5 = f32[256,128]{1,0:T(8,128)S(1)} collective-permute-done((f32[256,128]{1,0:T(8,128)S(1)}, f32[256,128]{1,0:T(8,128)S(1)}, u32[]{:S(2)}, u32[]{:S(2)}) %collective-permute-start.5) | collective-permute-done | bytes 131104 | tf_op jit(solution)/shard_map/ppermute | solution.py:16
  38.5 1.6 %collective-permute-start.12 = (f32[128,128]{1,0:T(8,128)S(1)}, f32[128,128]{1,0:T(8,128)S(1)}, u32[]{:S(2)}, u32[]{:S(2)}) collective-permute-start(f32[128,128]{1,0:T(8,128)S(1)} %get-tuple-element.15), channel_id=1, source_target_pairs={{0,2},{1,3},{2,0},{3,1},{4,6},{5,7},{6,4},{7,5},{8,10},{9,11},{10,... | collective-permute-start | bytes 196616 | tf_op jit(solution)/shard_map/ppermute | solution.py:16
  40.7 1.6 %collective-permute-start.13 = (f32[128,128]{1,0:T(8,128)S(1)}, f32[128,128]{1,0:T(8,128)S(1)}, u32[]{:S(2)}, u32[]{:S(2)}) collective-permute-start(f32[128,128]{1,0:T(8,128)S(1)} %add.43), channel_id=1, source_target_pairs={{0,2},{1,3},{2,0},{3,1},{4,6},{5,7},{6,4},{7,5},{8,10},{9,11},{10,... | collective-permute-start | bytes 196616 | tf_op jit(solution)/shard_map/ppermute | solution.py:16
  42.9 2.1 %collective-permute-done.13 = f32[128,128]{1,0:T(8,128)S(1)} collective-permute-done((f32[128,128]{1,0:T(8,128)S(1)}, f32[128,128]{1,0:T(8,128)S(1)}, u32[]{:S(2)}, u32[]{:S(2)}) %collective-permute-start.13) | collective-permute-done | bytes 65568 | tf_op jit(solution)/shard_map/ppermute | solution.py:16
  46.6 1.5 %gram.1 = f32[256,128]{1,0:T(8,128)S(1)} custom-call(s32[1024,1]{1,0:T(8,128)S(1)} %copy.5.owner_ref, f32[256,128]{1,0:T(8,128)S(1)} %get-tuple-element.26.refs_0_, f32[256,128]{1,0:T(8,128)S(1)} %get-tuple-element.20.refs_1_, f32[256,128]{1,0:T(8,128)S(1)} %constant_dynamic-update-slice_fusion.refs_2_, f32[256,128]{1,0:T(8,128)S(1)} %get-tuple-element.19.refs_3_), custom_call_target="tpu_custom_call" | custom-call | tf_op jit(solution)/shard_map/gram/pallas_call | solution.py:306
  48.2 1.6 %collective-permute-start.15 = (f32[2,32,128]{2,1,0:T(8,128)S(1)}, f32[2,32,128]{2,1,0:T(8,128)S(1)}, u32[]{:S(2)}, u32[]{:S(2)}) collective-permute-start(f32[2,32,128]{2,1,0:T(8,128)S(1)} %bitcast.17), channel_id=1, source_target_pairs={{0,4},{4,0},{8,12},{12,8},{16,20},{20,16},{24,28},{28,24},{1,5},{5... | collective-permute-start | bytes 98312 | tf_op jit(solution)/shard_map/ppermute | solution.py:16
  49.7 2.0 %collective-permute-start.17 = (f32[2,32,128]{2,1,0:T(8,128)S(1)}, f32[2,32,128]{2,1,0:T(8,128)S(1)}, u32[]{:S(2)}, u32[]{:S(2)}) collective-permute-start(f32[2,32,128]{2,1,0:T(8,128)S(1)} %bitcast.15), channel_id=1, source_target_pairs={{0,12},{4,8},{8,4},{12,0},{16,28},{20,24},{24,20},{28,16},{1,13},{... | collective-permute-start | bytes 98312 | tf_op jit(solution)/shard_map/ppermute | solution.py:16
  52.1 1.5 %collective-permute-done.16 = f32[2,32,128]{2,1,0:T(8,128)S(1)} collective-permute-done((f32[2,32,128]{2,1,0:T(8,128)S(1)}, f32[2,32,128]{2,1,0:T(8,128)S(1)}, u32[]{:S(2)}, u32[]{:S(2)}) %collective-permute-start.16) | collective-permute-done | bytes 32800 | tf_op jit(solution)/shard_map/ppermute | solution.py:16
  55.1 4.2 %collective-permute-done.18 = f32[1,32,128]{2,1,0:T(8,128)S(1)} collective-permute-done((f32[1,32,128]{2,1,0:T(8,128)S(1)}, f32[1,32,128]{2,1,0:T(8,128)S(1)}, u32[]{:S(2)}, u32[]{:S(2)}) %collective-permute-start.18) | collective-permute-done | bytes 16416 | tf_op jit(solution)/shard_map/ppermute | solution.py:16
  (50 shorter events, 9.7 us)
Async XLA Ops:
  0.0 4.8 %collective-permute-start = (s32[1024]{0:T(1024)}, s32[1024]{0:T(1024)S(1)}, u32[]{:S(2)}, u32[]{:S(2)}) collective-permute-start(s32[1024]{0:T(1024)} %refs_0_.1), channel_id=1, source_target_pairs={{0,8},{4,12},{8,0},{12,4},{16,24},{20,28},{24,16},{28,20},{1,9},{5... | collective-permute-start | bytes 12296 | tf_op jit(solution)/shard_map/ppermute | solution.py:16
  3.1 3.8 %collective-permute-start.1 = (s32[1024]{0:T(1024)}, s32[1024]{0:T(1024)S(1)}, u32[]{:S(2)}, u32[]{:S(2)}) collective-permute-start(s32[1024]{0:T(1024)} %refs_0_.1), channel_id=1, source_target_pairs={{0,4},{4,0},{8,12},{12,8},{16,20},{20,16},{24,28},{28,24},{1,5},{5... | collective-permute-start | bytes 12296 | tf_op jit(solution)/shard_map/ppermute | solution.py:16
  4.5 4.7 %collective-permute-start.2 = (s32[1024]{0:T(1024)}, s32[1024]{0:T(1024)S(1)}, u32[]{:S(2)}, u32[]{:S(2)}) collective-permute-start(s32[1024]{0:T(1024)} %refs_0_.1), channel_id=1, source_target_pairs={{0,12},{4,8},{8,4},{12,0},{16,28},{20,24},{24,20},{28,16},{1,13},{... | collective-permute-start | bytes 12296 | tf_op jit(solution)/shard_map/ppermute | solution.py:16
  10.0 8.8 %collective-permute-start.3 = (s32[4096]{0:T(1024)S(1)}, s32[4096]{0:T(1024)S(1)}, u32[]{:S(2)}, u32[]{:S(2)}) collective-permute-start(s32[4096]{0:T(1024)S(1)} %pad_add_fusion), channel_id=1, source_target_pairs={{0,16},{4,20},{8,24},{12,28},{16,0},{20,4},{24,8},{28,12},{1,17},{... | collective-permute-start | bytes 49160 | tf_op jit(solution)/shard_map/ppermute | solution.py:16
  12.5 1.6 %copy-start = (f32[32,16384]{1,0:T(8,128)S(1)}, f32[32,16384]{1,0:T(8,128)}, u32[]{:S(2)}) copy-start(f32[32,16384]{1,0:T(8,128)} %x_ref.1) | copy-start | bytes 6291460
  14.1 0.8 %copy-start.1 = (s32[16384]{0:T(1024)S(1)}, s32[16384]{0:T(1024)}, u32[]{:S(2)}) copy-start(s32[16384]{0:T(1024)} %param.5) | copy-start | bytes 196612
  20.7 5.4 %collective-permute-start.6 = (f32[256,128]{1,0:T(8,128)S(1)}, f32[256,128]{1,0:T(8,128)S(1)}, u32[]{:S(2)}, u32[]{:S(2)}) collective-permute-start(f32[256,128]{1,0:T(8,128)S(1)} %get-tuple-element.14), channel_id=1, source_target_pairs={{0,4},{4,0},{8,12},{12,8},{16,20},{20,16},{24,28},{28,24},{1,5},{5... | collective-permute-start | bytes 393224 | tf_op jit(solution)/shard_map/ppermute | solution.py:16
  21.3 5.9 %copy-start.2 = (s32[1024]{0:T(1024)S(1)}, s32[1024]{0:T(1024)}, u32[]{:S(2)}) copy-start(s32[1024]{0:T(1024)} %refs_0_.1) | copy-start | bytes 12292
  21.3 7.7 %collective-permute-start.9 = (f32[256,128]{1,0:T(8,128)S(1)}, f32[256,128]{1,0:T(8,128)S(1)}, u32[]{:S(2)}, u32[]{:S(2)}) collective-permute-start(f32[256,128]{1,0:T(8,128)S(1)} %get-tuple-element.18), channel_id=1, source_target_pairs={{0,4},{4,0},{8,12},{12,8},{16,20},{20,16},{24,28},{28,24},{1,5},{5... | collective-permute-start | bytes 393224 | tf_op jit(solution)/shard_map/ppermute | solution.py:16
  26.1 4.6 %collective-permute-start.7 = (f32[128,128]{1,0:T(8,128)S(1)}, f32[128,128]{1,0:T(8,128)S(1)}, u32[]{:S(2)}, u32[]{:S(2)}) collective-permute-start(f32[128,128]{1,0:T(8,128)S(1)} %slice.73), channel_id=1, source_target_pairs={{0,8},{4,12},{8,0},{12,4},{16,24},{20,28},{24,16},{28,20},{1,9},{5... | collective-permute-start | bytes 196616 | tf_op jit(solution)/shard_map/ppermute | solution.py:16
  26.6 6.4 %collective-permute-start.4 = (f32[512,128]{1,0:T(8,128)S(1)}, f32[512,128]{1,0:T(8,128)S(1)}, u32[]{:S(2)}, u32[]{:S(2)}) collective-permute-start(f32[512,128]{1,0:T(8,128)S(1)} %get-tuple-element.12), channel_id=1, source_target_pairs={{0,4},{4,0},{8,12},{12,8},{16,20},{20,16},{24,28},{28,24},{1,5},{5... | collective-permute-start | bytes 786440 | tf_op jit(solution)/shard_map/ppermute | solution.py:16
  29.0 16.1 %copy-start.3 = (s32[1024,1]{0,1:T(1,128)S(1)}, s32[1024,1]{0,1:T(1,128)}, u32[]{:S(2)}) copy-start(s32[1024,1]{0,1:T(1,128)} %param.7) | copy-start | bytes 12292
  29.1 5.6 %collective-permute-start.10 = (f32[128,128]{1,0:T(8,128)S(1)}, f32[128,128]{1,0:T(8,128)S(1)}, u32[]{:S(2)}, u32[]{:S(2)}) collective-permute-start(f32[128,128]{1,0:T(8,128)S(1)} %slice.75), channel_id=1, source_target_pairs={{0,8},{4,12},{8,0},{12,4},{16,24},{20,28},{24,16},{28,20},{1,9},{5... | collective-permute-start | bytes 196616 | tf_op jit(solution)/shard_map/ppermute | solution.py:16
  30.7 7.8 %collective-permute-start.8 = (f32[128,128]{1,0:T(8,128)S(1)}, f32[128,128]{1,0:T(8,128)S(1)}, u32[]{:S(2)}, u32[]{:S(2)}) collective-permute-start(f32[128,128]{1,0:T(8,128)S(1)} %slice_add_fusion.2), channel_id=1, source_target_pairs={{0,16},{4,20},{8,24},{12,28},{16,0},{20,4},{24,8},{28,12},{1,17},{... | collective-permute-start | bytes 196616 | tf_op jit(solution)/shard_map/ppermute | solution.py:16
  33.1 5.4 %collective-permute-start.5 = (f32[256,128]{1,0:T(8,128)S(1)}, f32[256,128]{1,0:T(8,128)S(1)}, u32[]{:S(2)}, u32[]{:S(2)}) collective-permute-start(f32[256,128]{1,0:T(8,128)S(1)} %slice.69), channel_id=1, source_target_pairs={{0,8},{4,12},{8,0},{12,4},{16,24},{20,28},{24,16},{28,20},{1,9},{5... | collective-permute-start | bytes 393224 | tf_op jit(solution)/shard_map/ppermute | solution.py:16
  34.7 5.9 %collective-permute-start.11 = (f32[128,128]{1,0:T(8,128)S(1)}, f32[128,128]{1,0:T(8,128)S(1)}, u32[]{:S(2)}, u32[]{:S(2)}) collective-permute-start(f32[128,128]{1,0:T(8,128)S(1)} %slice_add_fusion.1), channel_id=1, source_target_pairs={{0,16},{4,20},{8,24},{12,28},{16,0},{20,4},{24,8},{28,12},{1,17},{... | collective-permute-start | bytes 196616 | tf_op jit(solution)/shard_map/ppermute | solution.py:16
  38.5 4.3 %collective-permute-start.12 = (f32[128,128]{1,0:T(8,128)S(1)}, f32[128,128]{1,0:T(8,128)S(1)}, u32[]{:S(2)}, u32[]{:S(2)}) collective-permute-start(f32[128,128]{1,0:T(8,128)S(1)} %get-tuple-element.15), channel_id=1, source_target_pairs={{0,2},{1,3},{2,0},{3,1},{4,6},{5,7},{6,4},{7,5},{8,10},{9,11},{10,... | collective-permute-start | bytes 196616 | tf_op jit(solution)/shard_map/ppermute | solution.py:16
  40.7 4.3 %collective-permute-start.13 = (f32[128,128]{1,0:T(8,128)S(1)}, f32[128,128]{1,0:T(8,128)S(1)}, u32[]{:S(2)}, u32[]{:S(2)}) collective-permute-start(f32[128,128]{1,0:T(8,128)S(1)} %add.43), channel_id=1, source_target_pairs={{0,2},{1,3},{2,0},{3,1},{4,6},{5,7},{6,4},{7,5},{8,10},{9,11},{10,... | collective-permute-start | bytes 196616 | tf_op jit(solution)/shard_map/ppermute | solution.py:16
  45.0 1.6 %collective-permute-start.14 = (f32[2,256,128]{2,1,0:T(8,128)S(1)}, f32[2,256,128]{2,1,0:T(8,128)S(1)}, u32[]{:S(2)}, u32[]{:S(2)}) collective-permute-start(f32[2,256,128]{2,1,0:T(8,128)S(1)} %pad_maximum_fusion), channel_id=1, source_target_pairs={{0,1},{1,0},{2,3},{3,2},{4,5},{5,4},{6,7},{7,6},{8,9},{9,8},{10,11... | collective-permute-start | bytes 786440 | tf_op jit(solution)/shard_map/ppermute | solution.py:16
  48.2 4.0 %collective-permute-start.15 = (f32[2,32,128]{2,1,0:T(8,128)S(1)}, f32[2,32,128]{2,1,0:T(8,128)S(1)}, u32[]{:S(2)}, u32[]{:S(2)}) collective-permute-start(f32[2,32,128]{2,1,0:T(8,128)S(1)} %bitcast.17), channel_id=1, source_target_pairs={{0,4},{4,0},{8,12},{12,8},{16,20},{20,16},{24,28},{28,24},{1,5},{5... | collective-permute-start | bytes 98312 | tf_op jit(solution)/shard_map/ppermute | solution.py:16
  49.7 3.9 %collective-permute-start.16 = (f32[2,32,128]{2,1,0:T(8,128)S(1)}, f32[2,32,128]{2,1,0:T(8,128)S(1)}, u32[]{:S(2)}, u32[]{:S(2)}) collective-permute-start(f32[2,32,128]{2,1,0:T(8,128)S(1)} %bitcast.16), channel_id=1, source_target_pairs={{0,8},{4,12},{8,0},{12,4},{16,24},{20,28},{24,16},{28,20},{1,9},{5... | collective-permute-start | bytes 98312 | tf_op jit(solution)/shard_map/ppermute | solution.py:16
  49.7 4.8 %collective-permute-start.17 = (f32[2,32,128]{2,1,0:T(8,128)S(1)}, f32[2,32,128]{2,1,0:T(8,128)S(1)}, u32[]{:S(2)}, u32[]{:S(2)}) collective-permute-start(f32[2,32,128]{2,1,0:T(8,128)S(1)} %bitcast.15), channel_id=1, source_target_pairs={{0,12},{4,8},{8,4},{12,0},{16,28},{20,24},{24,20},{28,16},{1,13},{... | collective-permute-start | bytes 98312 | tf_op jit(solution)/shard_map/ppermute | solution.py:16
  54.6 4.7 %collective-permute-start.18 = (f32[1,32,128]{2,1,0:T(8,128)S(1)}, f32[1,32,128]{2,1,0:T(8,128)S(1)}, u32[]{:S(2)}, u32[]{:S(2)}) collective-permute-start(f32[1,32,128]{2,1,0:T(8,128)S(1)} %slice.83), channel_id=1, source_target_pairs={{0,16},{4,20},{8,24},{12,28},{16,0},{20,4},{24,8},{28,12},{1,17},{... | collective-permute-start | bytes 49160 | tf_op jit(solution)/shard_map/ppermute | solution.py:16

commit v8 on v7

--- a/solution.py
+++ b/solution.py
@@ -113,7 +113,7 @@
             table_ref[pl.ds(pl.multiple_of((hi * 8 + e) * LANES, LANES), LANES), :] = result
         return 0
 
-    lax.fori_loop(0, 16, some, 0, unroll=4)
+    lax.fori_loop(0, 16, some, 0, unroll=8)
 
 
 def pick_kernel(width, pieces, count, straight, *refs):
@@ -181,10 +181,10 @@
     for block in range(named * width // LANES):
         match = whose == tall + block * group
         left = jnp.where(match, mine_top, zero)
-        gram = lax.dot_general(top, left, over, preferred_element_type=f32)
-        gram = gram + lax.dot_general(low, left, over, preferred_element_type=f32)
+        gram = lax.dot_general(left, top, over, preferred_element_type=f32)
+        gram = gram + lax.dot_general(left, low, over, preferred_element_type=f32)
         left = jnp.where(match, mine_low, zero)
-        gram = (gram + lax.dot_general(top, left, over, preferred_element_type=f32)).T
+        gram = gram + lax.dot_general(left, top, over, preferred_element_type=f32)
         gram = jnp.take_along_axis(gram, turned, axis=1) * scale
         for k in range(group):
             slot = (block * group + k) ^ me

time: 60.1 us -> 59.7 us (level)
  transfers between devices with their start and end apart: 19 -> 19, of which waited for: 13 -> 13; matrix products, arithmetic and copies ran while one was open for 1% -> 1% of each run, Pallas kernels for 15% -> 14%
where the time goes in v8:
time: 59.7 us; the launch traced here: 59.5 us
  starting transfers between devices  21.7 us (36%)
  waiting for transfers between devices  21.5 us (36%)
  Pallas kernels  11.9 us (20%)
  local copies, waits for them, and re-layouts  2.73 us (5%)
  other arithmetic  1.47 us (2%)
    ppermute x19, starting transfers between devices, swapped(): lax.ppermute(x, axis, [(i, i ^ distance) for i in range(lax.axis_size(axi...  21.7 us
    ppermute x19, waiting for transfers between devices, swapped(): lax.ppermute(x, axis, [(i, i ^ distance) for i in range(lax.axis_size(axi...  21.5 us
    pallas_call x3, Pallas kernels, pick(): pl.pallas_call(functools.partial(pick_kernel, width, full, count, straigh...  7 us
    unnamed x10, local copies, waits for them, and re-layouts  2.67 us
    pallas_call x1, Pallas kernels, spread_lanes(): pl.pallas_call(functools.partial(table_kernel, width, rolled), out_shape=...  1.79 us
    pallas_call x1, Pallas kernels, transform(): pl.pallas_call(functools.partial(transform_kernel, width, rolled), out_sh...  1.71 us
    pallas_call x1, Pallas kernels, body(): pl.pallas_call(functools.partial(gram_kernel, width, count, devices, scal...  1.36 us
  transfers between devices with their start and end apart: 19, of which 13 were waited for; matrix products, arithmetic and copies ran while one was open for 1% of the time, Pallas kernels for 14%

profile of v8, /device:TPU:0, one launch (start us, length us, event | category | flops | bytes accessed | tf_op | source)
XLA Modules:
  0.0 59.5 jit_solution(4901149555206290867)
XLA Ops:
  0.0 3.1 %collective-permute-start = (s32[1024]{0:T(1024)}, s32[1024]{0:T(1024)S(1)}, u32[]{:S(2)}, u32[]{:S(2)}) collective-permute-start(s32[1024]{0:T(1024)} %refs_0_.1), channel_id=1, source_target_pairs={{0,8},{4,12},{8,0},{12,4},{16,24},{20,28},{24,16},{28,20},{1,9},{5... | collective-permute-start | bytes 12296 | tf_op jit(solution)/shard_map/ppermute | solution.py:16
  3.1 1.5 %collective-permute-start.1 = (s32[1024]{0:T(1024)}, s32[1024]{0:T(1024)S(1)}, u32[]{:S(2)}, u32[]{:S(2)}) collective-permute-start(s32[1024]{0:T(1024)} %refs_0_.1), channel_id=1, source_target_pairs={{0,4},{4,0},{8,12},{12,8},{16,20},{20,16},{24,28},{28,24},{1,5},{5... | collective-permute-start | bytes 12296 | tf_op jit(solution)/shard_map/ppermute | solution.py:16
  4.8 2.0 %collective-permute-done.1.refs_0_ = s32[1024]{0:T(1024)S(1)} collective-permute-done((s32[1024]{0:T(1024)}, s32[1024]{0:T(1024)S(1)}, u32[]{:S(2)}, u32[]{:S(2)}) %collective-permute-start.1) | collective-permute-done | bytes 4128 | tf_op jit(solution)/shard_map/ppermute | solution.py:16
  6.9 2.4 %collective-permute-done.2.refs_1_ = s32[1024]{0:T(1024)S(1)} collective-permute-done((s32[1024]{0:T(1024)}, s32[1024]{0:T(1024)S(1)}, u32[]{:S(2)}, u32[]{:S(2)}) %collective-permute-start.2) | collective-permute-done | bytes 4128 | tf_op jit(solution)/shard_map/ppermute | solution.py:16
  10.0 2.6 %collective-permute-start.3 = (s32[4096]{0:T(1024)S(1)}, s32[4096]{0:T(1024)S(1)}, u32[]{:S(2)}, u32[]{:S(2)}) collective-permute-start(s32[4096]{0:T(1024)S(1)} %pad_add_fusion), channel_id=1, source_target_pairs={{0,16},{4,20},{8,24},{12,28},{16,0},{20,4},{24,8},{28,12},{1,17},{... | collective-permute-start | bytes 49160 | tf_op jit(solution)/shard_map/ppermute | solution.py:16
  12.5 1.6 %copy-done = f32[32,16384]{1,0:T(8,128)S(1)} copy-done((f32[32,16384]{1,0:T(8,128)S(1)}, f32[32,16384]{1,0:T(8,128)}, u32[]{:S(2)}) %copy-start) | copy-done | bytes 2097176
  15.0 1.7 %transform.1.part_ref = f32[4096,128]{1,0:T(8,128)S(1)} custom-call(f32[32,16384]{1,0:T(8,128)S(1)} %copy-done, s32[128,128]{1,0:T(8,128)S(1)} %bitcast.13), custom_call_target="tpu_custom_call" | custom-call | tf_op jit(solution)/shard_map/transform/pallas_call | solution.py:203
  16.7 1.8 %table.1.refs_2_.refs_3_.refs_1_ = f32[16384,128]{1,0:T(8,128)S(1)} custom-call(f32[4096,128]{1,0:T(8,128)S(1)} %transform.1.part_ref), custom_call_target="tpu_custom_call" | custom-call | tf_op jit(solution)/shard_map/table/pallas_call | solution.py:216
  18.5 1.9 %pick.5 = (f32[256,128]{1,0:T(8,128)S(1)}, f32[256,128]{1,0:T(8,128)S(1)}) custom-call(s32[4096]{0:T(1024)S(1)} %collective-permute-done.3.refs_2_.refs_0_, f32[16384,128]{1,0:T(8,128)S(1)} %table.1.refs_2_.refs_3_.refs_1_), custom_call_target="tpu_custom_call" | custom-call | tf_op jit(solution)/shard_map/pick/pallas_call | solution.py:261
  21.0 1.5 %collective-permute-start.9 = (f32[256,128]{1,0:T(8,128)S(1)}, f32[256,128]{1,0:T(8,128)S(1)}, u32[]{:S(2)}, u32[]{:S(2)}) collective-permute-start(f32[256,128]{1,0:T(8,128)S(1)} %get-tuple-element.18), channel_id=1, source_target_pairs={{0,4},{4,0},{8,12},{12,8},{16,20},{20,16},{24,28},{28,24},{1,5},{5... | collective-permute-start | bytes 393224 | tf_op jit(solution)/shard_map/ppermute | solution.py:16
  22.5 3.3 %pick.4 = (f32[512,128]{1,0:T(8,128)S(1)}, f32[256,128]{1,0:T(8,128)S(1)}, f32[256,128]{1,0:T(8,128)S(1)}) custom-call(s32[1024]{0:T(1024)S(1)} %collective-permute-done.1.refs_0_, s32[1024]{0:T(1024)S(1)} %collective-permute-done.2.refs_1_, s32[4096]{0:T(1024)S(1)} %collective-permute-done.3.refs_2_.refs_0_, f32[16384,128]{1,0:T(8,128)S(1)} %table.1.refs_2_.refs_3_.refs_1_), custom_call_target="tpu_custom_call" | custom-call | tf_op jit(solution)/shard_map/pick/pallas_call | solution.py:261
  26.9 1.8 %pick.3 = f32[512,128]{1,0:T(8,128)S(1)} custom-call(s32[1024]{0:T(1024)S(1)} %copy-done.2, s32[1024]{0:T(1024)S(1)} %collective-permute-done.refs_1_, f32[16384,128]{1,0:T(8,128)S(1)} %table.1.refs_2_.refs_3_.refs_1_), custom_call_target="tpu_custom_call" | custom-call | tf_op jit(solution)/shard_map/pick/pallas_call | solution.py:261
  28.8 1.6 %collective-permute-start.10 = (f32[128,128]{1,0:T(8,128)S(1)}, f32[128,128]{1,0:T(8,128)S(1)}, u32[]{:S(2)}, u32[]{:S(2)}) collective-permute-start(f32[128,128]{1,0:T(8,128)S(1)} %slice.75), channel_id=1, source_target_pairs={{0,8},{4,12},{8,0},{12,4},{16,24},{20,28},{24,16},{28,20},{1,9},{5... | collective-permute-start | bytes 196616 | tf_op jit(solution)/shard_map/ppermute | solution.py:16
  30.8 1.9 %collective-permute-done.4 = f32[512,128]{1,0:T(8,128)S(1)} collective-permute-done((f32[512,128]{1,0:T(8,128)S(1)}, f32[512,128]{1,0:T(8,128)S(1)}, u32[]{:S(2)}, u32[]{:S(2)}) %collective-permute-start.4) | collective-permute-done | bytes 262176 | tf_op jit(solution)/shard_map/ppermute | solution.py:16
  32.8 1.6 %collective-permute-start.5 = (f32[256,128]{1,0:T(8,128)S(1)}, f32[256,128]{1,0:T(8,128)S(1)}, u32[]{:S(2)}, u32[]{:S(2)}) collective-permute-start(f32[256,128]{1,0:T(8,128)S(1)} %slice.69), channel_id=1, source_target_pairs={{0,8},{4,12},{8,0},{12,4},{16,24},{20,28},{24,16},{28,20},{1,9},{5... | collective-permute-start | bytes 393224 | tf_op jit(solution)/shard_map/ppermute | solution.py:16
  34.8 3.3 %collective-permute-done.5 = f32[256,128]{1,0:T(8,128)S(1)} collective-permute-done((f32[256,128]{1,0:T(8,128)S(1)}, f32[256,128]{1,0:T(8,128)S(1)}, u32[]{:S(2)}, u32[]{:S(2)}) %collective-permute-start.5) | collective-permute-done | bytes 131104 | tf_op jit(solution)/shard_map/ppermute | solution.py:16
  38.2 1.6 %collective-permute-start.12 = (f32[128,128]{1,0:T(8,128)S(1)}, f32[128,128]{1,0:T(8,128)S(1)}, u32[]{:S(2)}, u32[]{:S(2)}) collective-permute-start(f32[128,128]{1,0:T(8,128)S(1)} %get-tuple-element.15), channel_id=1, source_target_pairs={{0,2},{1,3},{2,0},{3,1},{4,6},{5,7},{6,4},{7,5},{8,10},{9,11},{10,... | collective-permute-start | bytes 196616 | tf_op jit(solution)/shard_map/ppermute | solution.py:16
  40.4 1.6 %collective-permute-start.13 = (f32[128,128]{1,0:T(8,128)S(1)}, f32[128,128]{1,0:T(8,128)S(1)}, u32[]{:S(2)}, u32[]{:S(2)}) collective-permute-start(f32[128,128]{1,0:T(8,128)S(1)} %add.43), channel_id=1, source_target_pairs={{0,2},{1,3},{2,0},{3,1},{4,6},{5,7},{6,4},{7,5},{8,10},{9,11},{10,... | collective-permute-start | bytes 196616 | tf_op jit(solution)/shard_map/ppermute | solution.py:16
  42.6 2.1 %collective-permute-done.13 = f32[128,128]{1,0:T(8,128)S(1)} collective-permute-done((f32[128,128]{1,0:T(8,128)S(1)}, f32[128,128]{1,0:T(8,128)S(1)}, u32[]{:S(2)}, u32[]{:S(2)}) %collective-permute-start.13) | collective-permute-done | bytes 65568 | tf_op jit(solution)/shard_map/ppermute | solution.py:16
  46.3 1.4 %gram.1 = f32[256,128]{1,0:T(8,128)S(1)} custom-call(s32[1024,1]{1,0:T(8,128)S(1)} %copy.5.owner_ref, f32[256,128]{1,0:T(8,128)S(1)} %get-tuple-element.26.refs_0_, f32[256,128]{1,0:T(8,128)S(1)} %get-tuple-element.20.refs_1_, f32[256,128]{1,0:T(8,128)S(1)} %constant_dynamic-update-slice_fusion.refs_2_, f32[256,128]{1,0:T(8,128)S(1)} %get-tuple-element.19.refs_3_), custom_call_target="tpu_custom_call" | custom-call | tf_op jit(solution)/shard_map/gram/pallas_call | solution.py:306
  47.7 1.6 %collective-permute-start.15 = (f32[2,32,128]{2,1,0:T(8,128)S(1)}, f32[2,32,128]{2,1,0:T(8,128)S(1)}, u32[]{:S(2)}, u32[]{:S(2)}) collective-permute-start(f32[2,32,128]{2,1,0:T(8,128)S(1)} %bitcast.17), channel_id=1, source_target_pairs={{0,4},{4,0},{8,12},{12,8},{16,20},{20,16},{24,28},{28,24},{1,5},{5... | collective-permute-start | bytes 98312 | tf_op jit(solution)/shard_map/ppermute | solution.py:16
  49.3 2.0 %collective-permute-start.17 = (f32[2,32,128]{2,1,0:T(8,128)S(1)}, f32[2,32,128]{2,1,0:T(8,128)S(1)}, u32[]{:S(2)}, u32[]{:S(2)}) collective-permute-start(f32[2,32,128]{2,1,0:T(8,128)S(1)} %bitcast.15), channel_id=1, source_target_pairs={{0,12},{4,8},{8,4},{12,0},{16,28},{20,24},{24,20},{28,16},{1,13},{... | collective-permute-start | bytes 98312 | tf_op jit(solution)/shard_map/ppermute | solution.py:16
  51.7 1.5 %collective-permute-done.16 = f32[2,32,128]{2,1,0:T(8,128)S(1)} collective-permute-done((f32[2,32,128]{2,1,0:T(8,128)S(1)}, f32[2,32,128]{2,1,0:T(8,128)S(1)}, u32[]{:S(2)}, u32[]{:S(2)}) %collective-permute-start.16) | collective-permute-done | bytes 32800 | tf_op jit(solution)/shard_map/ppermute | solution.py:16
  54.7 4.2 %collective-permute-done.18 = f32[1,32,128]{2,1,0:T(8,128)S(1)} collective-permute-done((f32[1,32,128]{2,1,0:T(8,128)S(1)}, f32[1,32,128]{2,1,0:T(8,128)S(1)}, u32[]{:S(2)}, u32[]{:S(2)}) %collective-permute-start.18) | collective-permute-done | bytes 16416 | tf_op jit(solution)/shard_map/ppermute | solution.py:16
  (50 shorter events, 9.7 us)
Async XLA Ops:
  0.0 4.8 %collective-permute-start = (s32[1024]{0:T(1024)}, s32[1024]{0:T(1024)S(1)}, u32[]{:S(2)}, u32[]{:S(2)}) collective-permute-start(s32[1024]{0:T(1024)} %refs_0_.1), channel_id=1, source_target_pairs={{0,8},{4,12},{8,0},{12,4},{16,24},{20,28},{24,16},{28,20},{1,9},{5... | collective-permute-start | bytes 12296 | tf_op jit(solution)/shard_map/ppermute | solution.py:16
  3.1 3.8 %collective-permute-start.1 = (s32[1024]{0:T(1024)}, s32[1024]{0:T(1024)S(1)}, u32[]{:S(2)}, u32[]{:S(2)}) collective-permute-start(s32[1024]{0:T(1024)} %refs_0_.1), channel_id=1, source_target_pairs={{0,4},{4,0},{8,12},{12,8},{16,20},{20,16},{24,28},{28,24},{1,5},{5... | collective-permute-start | bytes 12296 | tf_op jit(solution)/shard_map/ppermute | solution.py:16
  4.5 4.7 %collective-permute-start.2 = (s32[1024]{0:T(1024)}, s32[1024]{0:T(1024)S(1)}, u32[]{:S(2)}, u32[]{:S(2)}) collective-permute-start(s32[1024]{0:T(1024)} %refs_0_.1), channel_id=1, source_target_pairs={{0,12},{4,8},{8,4},{12,0},{16,28},{20,24},{24,20},{28,16},{1,13},{... | collective-permute-start | bytes 12296 | tf_op jit(solution)/shard_map/ppermute | solution.py:16
  10.0 8.5 %collective-permute-start.3 = (s32[4096]{0:T(1024)S(1)}, s32[4096]{0:T(1024)S(1)}, u32[]{:S(2)}, u32[]{:S(2)}) collective-permute-start(s32[4096]{0:T(1024)S(1)} %pad_add_fusion), channel_id=1, source_target_pairs={{0,16},{4,20},{8,24},{12,28},{16,0},{20,4},{24,8},{28,12},{1,17},{... | collective-permute-start | bytes 49160 | tf_op jit(solution)/shard_map/ppermute | solution.py:16
  12.5 1.6 %copy-start = (f32[32,16384]{1,0:T(8,128)S(1)}, f32[32,16384]{1,0:T(8,128)}, u32[]{:S(2)}) copy-start(f32[32,16384]{1,0:T(8,128)} %x_ref.1) | copy-start | bytes 6291460
  14.1 0.8 %copy-start.1 = (s32[16384]{0:T(1024)S(1)}, s32[16384]{0:T(1024)}, u32[]{:S(2)}) copy-start(s32[16384]{0:T(1024)} %param.5) | copy-start | bytes 196612
  20.4 5.4 %collective-permute-start.6 = (f32[256,128]{1,0:T(8,128)S(1)}, f32[256,128]{1,0:T(8,128)S(1)}, u32[]{:S(2)}, u32[]{:S(2)}) collective-permute-start(f32[256,128]{1,0:T(8,128)S(1)} %get-tuple-element.14), channel_id=1, source_target_pairs={{0,4},{4,0},{8,12},{12,8},{16,20},{20,16},{24,28},{28,24},{1,5},{5... | collective-permute-start | bytes 393224 | tf_op jit(solution)/shard_map/ppermute | solution.py:16
  21.0 5.9 %copy-start.2 = (s32[1024]{0:T(1024)S(1)}, s32[1024]{0:T(1024)}, u32[]{:S(2)}) copy-start(s32[1024]{0:T(1024)} %refs_0_.1) | copy-start | bytes 12292
  21.0 7.7 %collective-permute-start.9 = (f32[256,128]{1,0:T(8,128)S(1)}, f32[256,128]{1,0:T(8,128)S(1)}, u32[]{:S(2)}, u32[]{:S(2)}) collective-permute-start(f32[256,128]{1,0:T(8,128)S(1)} %get-tuple-element.18), channel_id=1, source_target_pairs={{0,4},{4,0},{8,12},{12,8},{16,20},{20,16},{24,28},{28,24},{1,5},{5... | collective-permute-start | bytes 393224 | tf_op jit(solution)/shard_map/ppermute | solution.py:16
  25.8 4.6 %collective-permute-start.7 = (f32[128,128]{1,0:T(8,128)S(1)}, f32[128,128]{1,0:T(8,128)S(1)}, u32[]{:S(2)}, u32[]{:S(2)}) collective-permute-start(f32[128,128]{1,0:T(8,128)S(1)} %slice.73), channel_id=1, source_target_pairs={{0,8},{4,12},{8,0},{12,4},{16,24},{20,28},{24,16},{28,20},{1,9},{5... | collective-permute-start | bytes 196616 | tf_op jit(solution)/shard_map/ppermute | solution.py:16
  26.3 6.4 %collective-permute-start.4 = (f32[512,128]{1,0:T(8,128)S(1)}, f32[512,128]{1,0:T(8,128)S(1)}, u32[]{:S(2)}, u32[]{:S(2)}) collective-permute-start(f32[512,128]{1,0:T(8,128)S(1)} %get-tuple-element.12), channel_id=1, source_target_pairs={{0,4},{4,0},{8,12},{12,8},{16,20},{20,16},{24,28},{28,24},{1,5},{5... | collective-permute-start | bytes 786440 | tf_op jit(solution)/shard_map/ppermute | solution.py:16
  28.7 16.1 %copy-start.3 = (s32[1024,1]{0,1:T(1,128)S(1)}, s32[1024,1]{0,1:T(1,128)}, u32[]{:S(2)}) copy-start(s32[1024,1]{0,1:T(1,128)} %param.7) | copy-start | bytes 12292
  28.8 5.6 %collective-permute-start.10 = (f32[128,128]{1,0:T(8,128)S(1)}, f32[128,128]{1,0:T(8,128)S(1)}, u32[]{:S(2)}, u32[]{:S(2)}) collective-permute-start(f32[128,128]{1,0:T(8,128)S(1)} %slice.75), channel_id=1, source_target_pairs={{0,8},{4,12},{8,0},{12,4},{16,24},{20,28},{24,16},{28,20},{1,9},{5... | collective-permute-start | bytes 196616 | tf_op jit(solution)/shard_map/ppermute | solution.py:16
  30.4 7.8 %collective-permute-start.8 = (f32[128,128]{1,0:T(8,128)S(1)}, f32[128,128]{1,0:T(8,128)S(1)}, u32[]{:S(2)}, u32[]{:S(2)}) collective-permute-start(f32[128,128]{1,0:T(8,128)S(1)} %slice_add_fusion.2), channel_id=1, source_target_pairs={{0,16},{4,20},{8,24},{12,28},{16,0},{20,4},{24,8},{28,12},{1,17},{... | collective-permute-start | bytes 196616 | tf_op jit(solution)/shard_map/ppermute | solution.py:16
  32.8 5.4 %collective-permute-start.5 = (f32[256,128]{1,0:T(8,128)S(1)}, f32[256,128]{1,0:T(8,128)S(1)}, u32[]{:S(2)}, u32[]{:S(2)}) collective-permute-start(f32[256,128]{1,0:T(8,128)S(1)} %slice.69), channel_id=1, source_target_pairs={{0,8},{4,12},{8,0},{12,4},{16,24},{20,28},{24,16},{28,20},{1,9},{5... | collective-permute-start | bytes 393224 | tf_op jit(solution)/shard_map/ppermute | solution.py:16
  34.4 5.9 %collective-permute-start.11 = (f32[128,128]{1,0:T(8,128)S(1)}, f32[128,128]{1,0:T(8,128)S(1)}, u32[]{:S(2)}, u32[]{:S(2)}) collective-permute-start(f32[128,128]{1,0:T(8,128)S(1)} %slice_add_fusion.1), channel_id=1, source_target_pairs={{0,16},{4,20},{8,24},{12,28},{16,0},{20,4},{24,8},{28,12},{1,17},{... | collective-permute-start | bytes 196616 | tf_op jit(solution)/shard_map/ppermute | solution.py:16
  38.2 4.3 %collective-permute-start.12 = (f32[128,128]{1,0:T(8,128)S(1)}, f32[128,128]{1,0:T(8,128)S(1)}, u32[]{:S(2)}, u32[]{:S(2)}) collective-permute-start(f32[128,128]{1,0:T(8,128)S(1)} %get-tuple-element.15), channel_id=1, source_target_pairs={{0,2},{1,3},{2,0},{3,1},{4,6},{5,7},{6,4},{7,5},{8,10},{9,11},{10,... | collective-permute-start | bytes 196616 | tf_op jit(solution)/shard_map/ppermute | solution.py:16
  40.4 4.3 %collective-permute-start.13 = (f32[128,128]{1,0:T(8,128)S(1)}, f32[128,128]{1,0:T(8,128)S(1)}, u32[]{:S(2)}, u32[]{:S(2)}) collective-permute-start(f32[128,128]{1,0:T(8,128)S(1)} %add.43), channel_id=1, source_target_pairs={{0,2},{1,3},{2,0},{3,1},{4,6},{5,7},{6,4},{7,5},{8,10},{9,11},{10,... | collective-permute-start | bytes 196616 | tf_op jit(solution)/shard_map/ppermute | solution.py:16
  44.7 1.6 %collective-permute-start.14 = (f32[2,256,128]{2,1,0:T(8,128)S(1)}, f32[2,256,128]{2,1,0:T(8,128)S(1)}, u32[]{:S(2)}, u32[]{:S(2)}) collective-permute-start(f32[2,256,128]{2,1,0:T(8,128)S(1)} %pad_maximum_fusion), channel_id=1, source_target_pairs={{0,1},{1,0},{2,3},{3,2},{4,5},{5,4},{6,7},{7,6},{8,9},{9,8},{10,11... | collective-permute-start | bytes 786440 | tf_op jit(solution)/shard_map/ppermute | solution.py:16
  47.7 4.0 %collective-permute-start.15 = (f32[2,32,128]{2,1,0:T(8,128)S(1)}, f32[2,32,128]{2,1,0:T(8,128)S(1)}, u32[]{:S(2)}, u32[]{:S(2)}) collective-permute-start(f32[2,32,128]{2,1,0:T(8,128)S(1)} %bitcast.17), channel_id=1, source_target_pairs={{0,4},{4,0},{8,12},{12,8},{16,20},{20,16},{24,28},{28,24},{1,5},{5... | collective-permute-start | bytes 98312 | tf_op jit(solution)/shard_map/ppermute | solution.py:16
  49.3 3.9 %collective-permute-start.16 = (f32[2,32,128]{2,1,0:T(8,128)S(1)}, f32[2,32,128]{2,1,0:T(8,128)S(1)}, u32[]{:S(2)}, u32[]{:S(2)}) collective-permute-start(f32[2,32,128]{2,1,0:T(8,128)S(1)} %bitcast.16), channel_id=1, source_target_pairs={{0,8},{4,12},{8,0},{12,4},{16,24},{20,28},{24,16},{28,20},{1,9},{5... | collective-permute-start | bytes 98312 | tf_op jit(solution)/shard_map/ppermute | solution.py:16
  49.3 4.8 %collective-permute-start.17 = (f32[2,32,128]{2,1,0:T(8,128)S(1)}, f32[2,32,128]{2,1,0:T(8,128)S(1)}, u32[]{:S(2)}, u32[]{:S(2)}) collective-permute-start(f32[2,32,128]{2,1,0:T(8,128)S(1)} %bitcast.15), channel_id=1, source_target_pairs={{0,12},{4,8},{8,4},{12,0},{16,28},{20,24},{24,20},{28,16},{1,13},{... | collective-permute-start | bytes 98312 | tf_op jit(solution)/shard_map/ppermute | solution.py:16
  54.2 4.7 %collective-permute-start.18 = (f32[1,32,128]{2,1,0:T(8,128)S(1)}, f32[1,32,128]{2,1,0:T(8,128)S(1)}, u32[]{:S(2)}, u32[]{:S(2)}) collective-permute-start(f32[1,32,128]{2,1,0:T(8,128)S(1)} %slice.83), channel_id=1, source_target_pairs={{0,16},{4,20},{8,24},{12,28},{16,0},{20,4},{24,8},{28,12},{1,17},{... | collective-permute-start | bytes 49160 | tf_op jit(solution)/shard_map/ppermute | solution.py:16
